TPU v7x, 32 devices: a whole 2x2x4 slice. The times are simulated.
32 devices in a mesh: gx: 8 (over z, y), gy: 4 (over x, core).
Axes of the slice: x: 2, y: 2, z: 4, core: 2. Of those that a mesh axis runs over, the one named last changes fastest.
Arguments:
- bus_start: float32 [4, 524288], P(None, ('gx', 'gy')), may hold values from -6 to 6
- bus_target: float32 [4, 524288], P(None, ('gx', 'gy')), may hold values from -6 to 6
- bus_weight: float32 [4, 524288], P(None, ('gx', 'gy')), may hold values from 0.25 to 4
- inner_ends: int32 [2, 655360], P(None, ('gx', 'gy')), may hold values from 0 to 16383, as said below
- cross_from: int32 [131072], P(('gx', 'gy')), may hold values from 0 to 16383, as said below
- boundary_lists: int32 [32, 4096], P(('gx', 'gy')), may hold values from 0 to 16383, as said below
- kkt_map: float32 [8, 8, 786432], P(None, None, ('gx', 'gy'))
- active_set: int32 [8, 786432], P(None, ('gx', 'gy')), may hold values 0 or 1
- limits: float32 [8, 786432], P(None, ('gx', 'gy')), may hold values from -3 to 3
- penalty_level: int32 [786432], P(('gx', 'gy')), may hold values from 1 to 8
- hv_bus: int32 [1024], P(('gx', 'gy')), may hold values from 0 to 16383
- hv_partner: int32 [1024], P(('gx', 'gy')), may hold values from 0 to 1023, as said below
- hv_level: int32 [1024], P(('gx', 'gy')), may hold values from 1 to 8
Outputs:
- bus_state: float32 [4, 524288], P(None, ('gx', 'gy'))
- branch_dual: float32 [8, 786432], P(None, ('gx', 'gy'))
- hv_dual: float32 [1024], P(('gx', 'gy'))
Inputs may be any that keep to these rules, and one draw needn't show every extreme that they name: `inner_ends`: local bus indices; both ends of a device's interior branch j lie in its cluster j // 320, that is among local buses 256 * (j // 320) to 256 * (j // 320) + 255. `cross_from`: local bus index; a device's crossing branch j has its own end in its cluster j // 64, that is among local buses 256 * (j // 64) to 256 * (j // 64) + 255. `hv_bus`: local bus index on the terminal's own device. `hv_partner`: links pair terminals: the partner of a terminal's partner is the terminal itself, and it lies on another device; two devices share either no link or exactly 2 links. `boundary_lists`: within a row all entries are distinct local bus indices; position i of each list lies in cluster i // 16, that is among local buses 256 * (i // 16) to 256 * (i // 16) + 255.
All inputs are finite; a program needn't handle non-finite values. No bound on the sum of `active_set` on one device may be relied on, other than what follows from the above.
Results may differ from a plain program's by a relative error of at most 0.000052.
Values sent between devices are 32-bit elements; how exact they have to be, the bound alone decides.
No kernel may reach another device: no remote copies, remote signals or barrier semaphores. Data moves between devices by JAX's collectives and lax.ppermute only.
A program may use at most 128 MiB of HBM per device.

v0:
```python
import functools

import jax
import jax.numpy as jnp
from jax import lax
from jax.experimental import pallas as pl
from jax.experimental.pallas import tpu as pltpu
from jax.sharding import PartitionSpec as P

F32 = jnp.float32
BF16 = jnp.bfloat16
BLK = 256
LANES = 128
GROUP = 8
PAIR = 2 * BLK
STATIC_ROWS = 25


def swapped(value, axis, first):
    count = lax.axis_size(axis)
    moves = []
    for low in range(first, count - 1, 2):
        moves += [(low, low + 1), (low + 1, low)]
    return lax.ppermute(value, axis, moves)


def to_all(rows):
    return lax.all_to_all(rows, ("gx", "gy"), split_axis=0, concat_axis=0, tiled=True)


def take_lanes(table, lane):
    return jnp.take_along_axis(table, lane, axis=1, mode="promise_in_bounds")


def pick(tables, index, tiles):
    lane, tile = (index & (LANES - 1), index >> 7)
    found = None
    for h in tiles:
        got = take_lanes(tables[h], lane)
        found = got if found is None else jnp.where(tile == h, got, found)
    return found


def spread8(row, rows=8):
    return jnp.broadcast_to(row, (rows, row.shape[-1]))


def one_hot(index, sublane):
    low = spread8(index & (LANES - 1), 16).astype(F32).astype(BF16)
    column = jnp.concatenate([low] * (LANES // 16), axis=0)
    return jnp.where(column == sublane, jnp.ones((), BF16), jnp.zeros((), BF16))


def contract(left, right):
    return lax.dot_general(
        left.astype(BF16), right, (((1,), (1,)), ((), ())), preferred_element_type=F32
    )


def halves(values):
    high = values.astype(BF16).astype(F32)
    return high, values - high


def sublanes():
    return lax.broadcasted_iota(jnp.int32, (LANES, LANES), 0).astype(F32).astype(BF16)


def folded(first, second, distance, mask):
    return jnp.where(
        mask,
        first + pltpu.roll(first, 8 - distance, 0),
        second + pltpu.roll(second, distance, 0),
    )


def product(kkt_ref, cols, target):
    row = lax.broadcasted_iota(jnp.int32, (8, LANES), 0)
    terms = [kkt_ref[8 * i : 8 * i + 8, cols] * target for i in range(8)]
    upper = row < 4
    quads = [
        jnp.where(upper, terms[i], terms[i + 4]) + pltpu.roll(jnp.where(upper, terms[i + 4], terms[i]), 4, 0)
        for i in range(4)
    ]
    even_two = (row & 2) == 0
    twos = [folded(quads[i], quads[i + 2], 2, even_two) for i in range(2)]
    return folded(twos[0], twos[1], 1, (row & 1) == 0)


def doubled(block):
    return block if block.shape[0] == 8 else jnp.concatenate([block, block], axis=0)


def tiles_of(states):
    return [states[:, h * LANES : (h + 1) * LANES] for h in range(states.shape[1] // LANES)]


def inner_ends_of(tables, index_ref, base, cols, t, upper):
    near = index_ref[0:1, cols] - base
    far = index_ref[1:2, cols] - base
    tiles = (0, 1) if t < 2 else (2, 3) if t > 2 else (0, 1, 2, 3)
    both = jnp.where(upper, spread8(near), spread8(far))
    return pick(tables, both, tiles), near, far, tiles


def inner_kernel(first, *refs):
    if first:
        s_ref, index_ref, kkt_ref, act_ref, lim_ref, lev_ref, y_ref, acc_ref, w_ref = refs
    else:
        s_ref, index_ref, kkt_ref, act_ref, lim_ref, lev_ref, old_ref, y_ref, acc_ref = refs
    step = pl.program_id(0)
    states = doubled(s_ref[...])
    upper = lax.broadcasted_iota(jnp.int32, (8, LANES), 0) < 4
    row16 = lax.broadcasted_iota(jnp.int32, (16, LANES), 0)
    sublane = sublanes()
    width = states.shape[1]
    per_pair = kkt_ref.shape[1] // (width // PAIR)
    for p in range(width // PAIR):
        tables = tiles_of(states[:, p * PAIR : (p + 1) * PAIR])
        base = step * width + p * PAIR
        sums = [jnp.zeros((8, LANES), F32)] * 4
        weights = jnp.zeros((16, LANES), F32)
        for t in range(per_pair // LANES):
            cols = slice(p * per_pair + t * LANES, p * per_pair + (t + 1) * LANES)
            ends, near, far, tiles = inner_ends_of(tables, index_ref, base, cols, t, upper)
            penalty = 0.25 * lev_ref[0:1, cols].astype(F32)
            if first:
                scaled, target = (None, ends)
            else:
                scaled = old_ref[:, cols] - ends
                target = ends - scaled
            flows = product(kkt_ref, cols, target)
            flows = jnp.where(act_ref[:, cols] == 1, lim_ref[:, cols], flows)
            y = flows if first else flows + scaled
            y_ref[:, cols] = y
            high, low = halves(spread8(penalty) * y)
            from_part = jnp.where(upper, high, pltpu.roll(low, 4, 0))
            to_part = jnp.where(upper, pltpu.roll(high, 4, 0), low)
            near_tile, far_tile = (spread8(near >> 7), spread8(far >> 7))
            left = [
                jnp.concatenate(
                    [
                        jnp.where(near_tile == h, from_part, 0.0),
                        jnp.where(far_tile == h, to_part, 0.0),
                    ],
                    axis=1,
                )
                for h in tiles
            ]
            if first:
                level = spread8(penalty, 16)
                left.append(
                    jnp.concatenate(
                        [
                            jnp.where(spread8(near >> 7, 16) == row16, level, 0.0),
                            jnp.where(spread8(far >> 7, 16) == row16, level, 0.0),
                        ],
                        axis=1,
                    )
                )
            right = jnp.concatenate([one_hot(near, sublane), one_hot(far, sublane)], axis=1)
            out = contract(jnp.concatenate(left, axis=0), right)
            for place, h in enumerate(tiles):
                sums[h] = sums[h] + out[8 * place : 8 * place + 8]
            if first:
                weights = weights + out[8 * len(tiles) :]
        for h in range(4):
            spot = slice(p * PAIR + h * LANES, p * PAIR + (h + 1) * LANES)
            acc_ref[:, spot] = sums[h]
            if first:
                w_ref[0:1, spot] = weights[h : h + 1]


def list_picks(tables, list_ref, step, base, upper):
    count = list_ref.shape[1] // 4
    places = [
        list_ref[0:1, pl.ds(pl.multiple_of(k * count + step * LANES, LANES), LANES)] - base
        for k in range(4)
    ]
    picks = []
    for k in (0, 2):
        both = jnp.where(upper, spread8(places[k]), spread8(places[k + 1]))
        picks.append(pick(tables, both, range(len(tables))))
    return places, picks


def even_sides():
    return lax.axis_index("gx") % 2 == 0, lax.axis_index("gy") % 2 == 0


def slots(outs, step, per_list_steps):
    even_x, even_y = even_sides()
    block = step // per_list_steps
    wanted = (
        jnp.where(even_x, 1, 0),
        jnp.where(even_x, 0, 1),
        jnp.where(even_y, 3, 2),
        jnp.where(even_y, 2, 3),
    )
    return [(ref, block == want) for ref, want in zip(outs, wanted)]


def write_ghosts(outs, picks, step):
    even_x, even_y = even_sides()
    spot = pl.ds(pl.multiple_of(step * LANES, LANES), LANES)
    for out_even, out_odd, even, both in (
        (outs[0], outs[1], even_x, picks[0]),
        (outs[2], outs[3], even_y, picks[1]),
    ):
        out_even[0:4, spot] = jnp.where(even, both[:4], both[4:])
        out_odd[0:4, spot] = jnp.where(even, both[4:], both[:4])


def cross_spot(step, per_list_steps, t, width):
    start = (step % per_list_steps) * width + t * LANES
    return pl.ds(pl.multiple_of(start, LANES), LANES)


def hv_states(s_ref, hv_bus_ref, work_ref):
    lane = lax.broadcasted_iota(jnp.int32, (1, LANES), 1)

    def body(t, carry):
        bus = hv_bus_ref[t]
        start = pl.multiple_of((bus >> 7) * LANES, LANES)
        row = s_ref[2:3, pl.ds(start, LANES)]
        work_ref[pl.ds(t, 1), :] = jnp.where(lane == (bus & (LANES - 1)), row, 0.0)
        return carry

    lax.fori_loop(0, work_ref.shape[0], body, 0, unroll=8)
    return jnp.broadcast_to(jnp.sum(work_ref[...], axis=1, keepdims=True), work_ref.shape)


def hv_penalties(level_ref, work_ref):
    def body(t, carry):
        work_ref[pl.ds(t, 1), :] = jnp.full((1, LANES), level_ref[t], jnp.int32).astype(F32) * 0.25
        return carry

    lax.fori_loop(0, work_ref.shape[0], body, 0, unroll=8)
    return work_ref[...]


def as_row(values, width, offset):
    count = values.shape[0]
    wide = jnp.broadcast_to(values[:, :1], (count, width))
    lane = lax.broadcasted_iota(jnp.int32, (count, width), 1)
    own = lax.broadcasted_iota(jnp.int32, (count, width), 0)
    return jnp.sum(jnp.where(lane == own + offset, wide, 0.0), axis=0, keepdims=True)


def write_hv(out_ref, values, penalties):
    width = out_ref.shape[-1]
    row = as_row(values, width, 0) + as_row(penalties, width, values.shape[0])
    out_ref[...] = jnp.broadcast_to(row, out_ref.shape)


def start_kernel(
    bus_ref, level_ref, s_ref, list_ref, from_ref, kkt_ref, act_ref, lim_ref, lev_ref,
    xe_ref, xo_ref, ye_ref, yo_ref, z_ref, hv_ref, hv_own_ref, work_ref, turn_ref,
):
    step = pl.program_id(0)
    width = s_ref.shape[1] // pl.num_programs(0)
    outs = (xe_ref, xo_ref, ye_ref, yo_ref)
    upper = lax.broadcasted_iota(jnp.int32, (8, LANES), 0) < 4

    @pl.when(step == 0)
    def _():
        values = hv_states(s_ref, bus_ref, work_ref)
        hv_own_ref[...] = values
        penalties = hv_penalties(level_ref, work_ref)
        write_hv(hv_ref, values, penalties)

    base = step * width
    states = doubled(s_ref[:, pl.ds(pl.multiple_of(base, width), width)])
    tables = tiles_of(states)
    _, picks = list_picks(tables, list_ref, step, base, upper)
    z_ref[0:8, :] = picks[0]
    z_ref[8:16, :] = picks[1]
    write_ghosts(outs, picks, step)
    cross = from_ref.shape[1]
    per_list_steps = xe_ref.shape[1] // cross
    found = []
    for t in range(cross // LANES):
        cols = slice(t * LANES, (t + 1) * LANES)
        index = spread8(from_ref[0:1, cols] - (base + t * PAIR))
        ends = pick(tables[4 * t : 4 * t + 4], index, range(4))
        fixed = act_ref[:, cols] == 1
        part = jnp.where(fixed, lim_ref[:, cols], product(kkt_ref, cols, jnp.where(upper, ends, 0.0)))
        for i in range(8):
            turn_ref[64 * t + 8 * i : 64 * t + 8 * i + 8, :] = kkt_ref[8 * i : 8 * i + 8, cols]
        block = [
            jnp.where(fixed, 0.0, turn_ref[pl.ds(64 * t + 4 + j, 8, stride=8), :])[4:] for j in range(4)
        ]
        found.append((part[4:], block, 0.25 * lev_ref[0:1, cols].astype(F32)))
    for ref, here in slots(outs, step, per_list_steps):

        @pl.when(here)
        def _():
            for t, (part, block, penalty) in enumerate(found):
                spot = cross_spot(step, per_list_steps, t, cross)
                ref[4:8, spot] = part
                for j in range(4):
                    ref[8 + 4 * j : 12 + 4 * j, spot] = block[j]
                ref[24:25, spot] = penalty


def far_hv(first, bus_ref, partner_ref, level_ref, all_ref, own, scaled, sum_ref, weight_ref, work_ref, pen_ref):
    count = work_ref.shape[0]
    width = all_ref.shape[-1]
    lane = lax.broadcasted_iota(jnp.int32, (1, LANES), 1)
    wide = lax.broadcasted_iota(jnp.int32, (1, width), 1)

    def fetch(t, carry):
        partner = partner_ref[t]
        device, place = (partner // count, partner % count)
        row = all_ref[pl.ds(device, 1), :]
        value = jnp.sum(jnp.where(wide == place, row, 0.0), axis=1, keepdims=True)
        weight = jnp.sum(jnp.where(wide == place + count, row, 0.0), axis=1, keepdims=True)
        work_ref[pl.ds(t, 1), :] = jnp.broadcast_to(value, (1, LANES))
        pen_ref[pl.ds(t, 1), :] = jnp.broadcast_to(weight, (1, LANES))
        return carry

    lax.fori_loop(0, count, fetch, 0, unroll=8)
    far_value = work_ref[...]
    far_penalty = pen_ref[...]
    penalty = hv_penalties(level_ref, pen_ref)
    flow = (penalty * own - far_penalty * far_value) / (penalty + far_penalty)
    y = flow if first else flow + scaled
    work_ref[...] = penalty * y
    sum_ref[...] = jnp.zeros_like(sum_ref)
    if first:
        weight_ref[...] = jnp.zeros_like(weight_ref)

    def place_terms(t, carry):
        bus = bus_ref[t]
        spot = pl.ds(pl.multiple_of((bus >> 7) * LANES, LANES), LANES)
        here = lane == (bus & (LANES - 1))
        sum_ref[0:1, spot] += jnp.where(here, work_ref[pl.ds(t, 1), :], 0.0)
        if first:
            weight_ref[0:1, spot] += jnp.where(here, pen_ref[pl.ds(t, 1), :], 0.0)
        return carry

    lax.fori_loop(0, count, place_terms, 0, unroll=8)
    return penalty, y


def outer_kernel(first, *refs):
    if first:
        (
            bus_ref, partner_ref, level_ref, all_ref, own_ref, xe, xo, ye, yo, acc_ref, weight_in_ref,
            s_ref, list_ref, from_ref, kkt_ref, act_ref, lim_ref, lev_ref, z_ref, target_ref, prior_ref,
            new_ref, inv_ref, oxe, oxo, oye, oyo, yc_ref, ym_ref, zn_ref, hv_ref, hv_scaled_ref, hv_own_ref,
            sum_ref, hv_weight_ref, work_ref, pen_ref, hold_ref,
        ) = refs
        now = (xe, xo, ye, yo)
        scaled_ref = None
    else:
        (
            bus_ref, partner_ref, level_ref, all_ref, own_ref, scaled_ref, xe, xo, ye, yo, nxe, nxo, nye, nyo,
            acc_ref, inv_ref, s_ref, list_ref, from_ref, kkt_ref, act_ref, lim_ref, lev_ref, z_ref, yc_old_ref,
            ym_old_ref, target_ref, prior_ref,
            new_ref, state_ref, oxe, oxo, oye, oyo, yc_ref, hv_dual_ref,
            sum_ref, work_ref, pen_ref, hold_ref,
        ) = refs
        now = (nxe, nxo, nye, nyo)
        hv_weight_ref = None
    fixed_parts = (xe, xo, ye, yo)
    outs = (oxe, oxo, oye, oyo)
    step = pl.program_id(0)
    width = s_ref.shape[1]
    upper = lax.broadcasted_iota(jnp.int32, (8, LANES), 0) < 4
    row8 = lax.broadcasted_iota(jnp.int32, (8, LANES), 0)
    row16 = lax.broadcasted_iota(jnp.int32, (16, LANES), 0)
    power = (row8 == 2) | (row8 == 6)
    sublane = sublanes()
    even_x, even_y = even_sides()

    @pl.when(step == 0)
    def _():
        scaled = None if first else scaled_ref[...]
        _, y = far_hv(
            first, bus_ref, partner_ref, level_ref, all_ref, own_ref[...], scaled, sum_ref, hv_weight_ref,
            work_ref, pen_ref,
        )
        hold_ref[...] = y

    base = step * width
    tables = tiles_of(doubled(s_ref[...]))
    cross = from_ref.shape[1]
    per_list_steps = xe.shape[1] // cross
    block = step // per_list_steps
    places, _ = (
        [
            list_ref[0:1, pl.ds(pl.multiple_of(k * (list_ref.shape[1] // 4) + step * LANES, LANES), LANES)] - base
            for k in range(4)
        ],
        None,
    )
    sums = [None] * len(tables)
    weights = [None] * len(tables)

    use_even = jnp.where(even_x, block == 1, block == 0) | (jnp.where(even_y, block == 3, block == 2))
    along_x = block < 2
    outputs = []
    for t in range(cross // LANES):
        cols = slice(t * LANES, (t + 1) * LANES)
        spot = cross_spot(step, per_list_steps, t, cross)
        ghost = jnp.where(
            along_x,
            jnp.where(use_even, now[0][0:4, spot], now[1][0:4, spot]),
            jnp.where(use_even, now[2][0:4, spot], now[3][0:4, spot]),
        )
        near = from_ref[0:1, cols] - (base + t * PAIR)
        ends = pick(tables[4 * t : 4 * t + 4], spread8(near), range(4))
        ends = jnp.where(upper, ends, doubled(ghost))
        penalty = 0.25 * lev_ref[0:1, cols].astype(F32)
        if first:
            scaled, target = (None, ends)
        else:
            scaled = yc_old_ref[:, cols] - ends
            target = ends - scaled
        flows = product(kkt_ref, cols, target)
        flows = jnp.where(act_ref[:, cols] == 1, lim_ref[:, cols], flows)
        y = flows if first else flows + scaled
        yc_ref[:, cols] = y
        outputs.append(y)
        high, low = halves(spread8(penalty) * y)
        part = jnp.where(upper, high, pltpu.roll(low, 4, 0))
        tile = spread8(near >> 7)
        left = [jnp.where(tile == h, part, 0.0) for h in range(4)]
        if first:
            left.append(jnp.where(spread8(near >> 7, 16) == row16, spread8(penalty, 16), 0.0))
        out = contract(jnp.concatenate(left, axis=0), one_hot(near, sublane))
        for h in range(4):
            sums[4 * t + h] = out[8 * h : 8 * h + 8]
            if first:
                weights[4 * t + h] = out[32 + h : 33 + h]

    spot = pl.ds(pl.multiple_of(step * LANES, LANES), LANES)
    lefts, rights = ([], [])
    for k, (even, pair) in enumerate(((even_x, 0), (even_x, 1), (even_y, 0), (even_y, 1))):
        start = 0 if k < 2 else 2
        from_even = even if pair == 0 else jnp.logical_not(even)

        def received(parts, rows):
            return jnp.where(from_even, parts[start][rows, spot], parts[start + 1][rows, spot])

        rows = slice(4 * k, 4 * k + 4)
        held = z_ref[rows, :]
        if first:
            scaled, target = (None, held)
        else:
            scaled = ym_old_ref[rows, :] - held
            target = held - scaled
        flows = received(now, slice(4, 8))
        for j in range(4):
            flows = flows + received(fixed_parts, slice(8 + 4 * j, 12 + 4 * j)) * spread8(target[j : j + 1], 4)
        penalty = received(fixed_parts, slice(24, 25))
        y = flows if first else flows + scaled
        if first:
            ym_ref[rows, :] = y
        high, low = halves(spread8(penalty, 4) * y)
        part = jnp.concatenate([high, low], axis=0)
        tile = spread8(places[k] >> 7)
        left = [jnp.where(tile == h, part, 0.0) for h in range(len(tables))]
        if first:
            left.append(jnp.where(spread8(places[k] >> 7, 16) == row16, spread8(penalty, 16), 0.0))
        lefts.append(jnp.concatenate(left, axis=0))
        rights.append(one_hot(places[k], sublane))
    out = contract(jnp.concatenate(lefts[:2], axis=1), jnp.concatenate(rights[:2], axis=1))
    out = out + contract(jnp.concatenate(lefts[2:], axis=1), jnp.concatenate(rights[2:], axis=1))

    fresh = []
    for h in range(len(tables)):
        cols = slice(h * LANES, (h + 1) * LANES)
        whole = pl.ds(pl.multiple_of(base + h * LANES, LANES), LANES)
        total = acc_ref[:, cols] + sums[h] + out[8 * h : 8 * h + 8]
        total = total + pltpu.roll(total, 4, 0)
        total = total + jnp.where(power, spread8(sum_ref[0:1, whole]), 0.0)
        prior = doubled(prior_ref[:, cols])
        total = total + prior * doubled(target_ref[:, cols])
        if first:
            count = 8 * len(tables)
            weight = weight_in_ref[0:1, cols] + weights[h] + out[count + h : count + h + 1]
            weight = spread8(weight) + jnp.where(power, spread8(hv_weight_ref[0:1, whole]), 0.0) + prior
            inverse = 1.0 / weight
            inv_ref[:, cols] = inverse
        else:
            inverse = inv_ref[:, cols]
        state = total * inverse
        new_ref[:, whole] = state
        if not first:
            state_ref[:, cols] = state[:4]
        fresh.append(state)

    _, picks = list_picks(fresh, list_ref, step, base, upper)
    write_ghosts(outs, picks, step)
    if first:
        zn_ref[0:8, :] = picks[0]
        zn_ref[8:16, :] = picks[1]
        parts = []
        for t in range(cross // LANES):
            cols = slice(t * LANES, (t + 1) * LANES)
            near = from_ref[0:1, cols] - (base + t * PAIR)
            ends = pick(fresh[4 * t : 4 * t + 4], spread8(near), range(4))
            target = 2.0 * ends - outputs[t]
            part = product(kkt_ref, cols, jnp.where(upper, target, 0.0))
            parts.append(jnp.where(act_ref[:, cols] == 1, lim_ref[:, cols], part)[4:])
        for ref, here in slots(outs, step, per_list_steps):

            @pl.when(here)
            def _():
                for t, part in enumerate(parts):
                    ref[4:8, cross_spot(step, per_list_steps, t, cross)] = part

    @pl.when(step == pl.num_programs(0) - 1)
    def _():
        reached = hv_states(new_ref, bus_ref, work_ref)
        left_over = hold_ref[...] - reached
        penalty = hv_penalties(level_ref, pen_ref)
        if first:
            hv_scaled_ref[...] = left_over
            hv_own_ref[...] = reached - left_over
            write_hv(hv_ref, reached - left_over, penalty)
        else:
            row = as_row(penalty * left_over, LANES, 0)
            hv_dual_ref[...] = row[:, : hv_dual_ref.shape[1]]


def inner_dual_kernel(s_ref, index_ref, y_ref, lev_ref, dual_ref):
    step = pl.program_id(0)
    upper = lax.broadcasted_iota(jnp.int32, (8, LANES), 0) < 4
    width = s_ref.shape[1]
    per_pair = index_ref.shape[1] // (width // PAIR)
    for p in range(width // PAIR):
        tables = tiles_of(s_ref[:, p * PAIR : (p + 1) * PAIR])
        base = step * width + p * PAIR
        for t in range(per_pair // LANES):
            cols = slice(p * per_pair + t * LANES, p * per_pair + (t + 1) * LANES)
            ends, _, _, _ = inner_ends_of(tables, index_ref, base, cols, t, upper)
            penalty = 0.25 * lev_ref[0:1, cols].astype(F32)
            dual_ref[:, cols] = spread8(penalty) * (y_ref[:, cols] - ends)


def outer_dual_kernel(dual_in_ref, xe, xo, ye, yo, s_ref, from_ref, y_ref, lev_ref, dual_ref):
    step = pl.program_id(0)
    width = s_ref.shape[1]
    upper = lax.broadcasted_iota(jnp.int32, (8, LANES), 0) < 4
    even_x, even_y = even_sides()
    tables = tiles_of(s_ref[...])
    cross = from_ref.shape[1]
    per_list_steps = xe.shape[1] // cross
    block = step // per_list_steps
    use_even = jnp.where(even_x, block == 1, block == 0) | (jnp.where(even_y, block == 3, block == 2))
    along_x = block < 2
    for t in range(cross // LANES):
        cols = slice(t * LANES, (t + 1) * LANES)
        spot = cross_spot(step, per_list_steps, t, cross)
        ghost = jnp.where(
            along_x,
            jnp.where(use_even, xe[0:4, spot], xo[0:4, spot]),
            jnp.where(use_even, ye[0:4, spot], yo[0:4, spot]),
        )
        near = from_ref[0:1, cols] - (step * width + t * PAIR)
        ends = pick(tables[4 * t : 4 * t + 4], spread8(near), range(4))
        ends = jnp.where(upper, ends, doubled(ghost))
        penalty = 0.25 * lev_ref[0:1, cols].astype(F32)
        dual_ref[:, cols] = spread8(penalty) * (y_ref[:, cols] - ends)


def split(rows, width, first=0):
    return pl.BlockSpec((rows, width), lambda g: (0, first + g))


def whole(shape):
    return pl.BlockSpec(shape, lambda g: (0,) * len(shape))


def scalars():
    return pl.BlockSpec(memory_space=pltpu.SMEM)


def shape_of(*dims):
    return jax.ShapeDtypeStruct(dims, F32)


def params():
    return pltpu.CompilerParams(
        dimension_semantics=("arbitrary",), vmem_limit_bytes=32 * 1024 * 1024
    )


def cost(flops, moved):
    return pl.CostEstimate(flops=flops, bytes_accessed=moved, transcendentals=0)


def on_device(
    bus_start, bus_target, bus_weight, inner_ends, cross_from, boundary_lists, kkt_map, active_set, limits,
    penalty_level, hv_bus, hv_partner, hv_level,
):
    _, bus_count = bus_start.shape
    list_len = boundary_lists.shape[1] // 4
    inner_count = inner_ends.shape[1]
    cross_count = cross_from.shape[0]
    branch_count = kkt_map.shape[2]
    terms = hv_bus.shape[0]
    devices = lax.axis_size("gx") * lax.axis_size("gy")
    steps = bus_count // (GROUP * BLK)
    buses, inner, cross = (bus_count // steps, inner_count // steps, cross_count // steps)
    start = inner_count // cross
    hv_width = max(LANES, 2 * terms)
    kkt = kkt_map.reshape(64, branch_count)
    from_row = cross_from.reshape(1, cross_count)
    level_row = penalty_level.reshape(1, branch_count)
    inner_args = (inner_ends, kkt, active_set, limits, level_row)
    inner_specs = [split(2, inner), split(64, inner), split(8, inner), split(8, inner), split(1, inner)]
    cross_args = (from_row, kkt, active_set, limits, level_row)
    cross_specs = [
        split(1, cross), split(64, cross, start), split(8, cross, start), split(8, cross, start), split(1, cross, start),
    ]
    hv_block = (terms, LANES)
    common = dict(grid=(steps,), compiler_params=params())

    *sent, held, hv_rows, hv_own = pl.pallas_call(
        start_kernel,
        name="first_messages",
        in_specs=[scalars(), scalars(), whole(bus_start.shape), whole(boundary_lists.shape)] + cross_specs,
        out_shape=[shape_of(STATIC_ROWS, list_len)] * 4
        + [shape_of(16, list_len), shape_of(devices, hv_width), shape_of(*hv_block)],
        out_specs=[whole((STATIC_ROWS, list_len))] * 4
        + [split(16, LANES), whole((devices, hv_width)), whole(hv_block)],
        scratch_shapes=[pltpu.VMEM(hv_block, F32), pltpu.VMEM((64 * (cross // LANES), LANES), F32)],
        cost_estimate=cost(10**6, 4 * 10**6),
        **common,
    )(hv_bus, hv_level, bus_start, boundary_lists, *cross_args)

    def exchange(messages):
        xe, xo, ye, yo = messages
        xo = swapped(xo, "gx", 1)
        yo = swapped(yo, "gy", 1)
        xe = swapped(xe, "gx", 0)
        ye = swapped(ye, "gy", 0)
        return (xe, xo, ye, yo)

    first_got = exchange(sent)
    hv_all = to_all(hv_rows)
    y_inner, sums, weights = pl.pallas_call(
        functools.partial(inner_kernel, True),
        name="inner_first",
        in_specs=[split(4, buses)] + inner_specs,
        out_shape=[shape_of(8, inner_count), shape_of(8, bus_count), shape_of(1, bus_count)],
        out_specs=[split(8, inner), split(8, buses), split(1, buses)],
        cost_estimate=cost(10**8, 10**7),
        **common,
    )(bus_start, *inner_args)
    message_shape = (8, list_len)
    state, inverse, *rest = pl.pallas_call(
        functools.partial(outer_kernel, True),
        name="outer_first",
        in_specs=[scalars()] * 3
        + [whole((devices, hv_width)), whole(hv_block)]
        + [whole((STATIC_ROWS, list_len))] * 4
        + [split(8, buses), split(1, buses), split(4, buses), whole(boundary_lists.shape)]
        + cross_specs
        + [split(16, LANES), split(4, buses), split(4, buses)],
        out_shape=[shape_of(8, bus_count), shape_of(8, bus_count)]
        + [shape_of(*message_shape)] * 4
        + [shape_of(8, cross_count), shape_of(16, list_len), shape_of(16, list_len)]
        + [shape_of(devices, hv_width), shape_of(*hv_block), shape_of(*hv_block)],
        out_specs=[whole((8, bus_count)), split(8, buses)]
        + [whole(message_shape)] * 4
        + [split(8, cross), split(16, LANES), split(16, LANES)]
        + [whole((devices, hv_width)), whole(hv_block), whole(hv_block)],
        scratch_shapes=[pltpu.VMEM((1, bus_count), F32)] * 2 + [pltpu.VMEM(hv_block, F32)] * 3,
        cost_estimate=cost(10**7, 5 * 10**6),
        **common,
    )(
        hv_bus, hv_partner, hv_level, hv_all, hv_own, *first_got, sums, weights, bus_start, boundary_lists,
        *cross_args, held, bus_target, bus_weight,
    )
    sent, (y_cross, y_mirror, held, hv_rows, hv_scaled, hv_own) = (rest[:4], rest[4:])

    second_got = exchange(sent)
    hv_all = to_all(hv_rows)
    y_inner, sums = pl.pallas_call(
        functools.partial(inner_kernel, False),
        name="inner_second",
        in_specs=[split(8, buses)] + inner_specs + [split(8, inner)],
        out_shape=[shape_of(8, inner_count), shape_of(8, bus_count)],
        out_specs=[split(8, inner), split(8, buses)],
        cost_estimate=cost(10**8, 10**7),
        **common,
    )(state, *inner_args, y_inner)
    last_shape = (4, list_len)
    state, bus_state, *rest = pl.pallas_call(
        functools.partial(outer_kernel, False),
        name="outer_second",
        in_specs=[scalars()] * 3
        + [whole((devices, hv_width)), whole(hv_block), whole(hv_block)]
        + [whole((STATIC_ROWS, list_len))] * 4
        + [whole(message_shape)] * 4
        + [split(8, buses), split(8, buses), split(8, buses), whole(boundary_lists.shape)]
        + cross_specs
        + [split(16, LANES), split(8, cross), split(16, LANES), split(4, buses), split(4, buses)],
        out_shape=[shape_of(8, bus_count), shape_of(4, bus_count)]
        + [shape_of(*last_shape)] * 4
        + [shape_of(8, cross_count), shape_of(1, terms)],
        out_specs=[whole((8, bus_count)), split(4, buses)]
        + [whole(last_shape)] * 4
        + [split(8, cross), whole((1, terms))],
        scratch_shapes=[pltpu.VMEM((1, bus_count), F32)] + [pltpu.VMEM(hv_block, F32)] * 3,
        cost_estimate=cost(10**7, 5 * 10**6),
        **common,
    )(
        hv_bus, hv_partner, hv_level, hv_all, hv_own, hv_scaled, *first_got, *second_got, sums, inverse, state,
        boundary_lists, *cross_args, held, y_cross, y_mirror, bus_target, bus_weight,
    )
    sent, (y_cross, hv_dual) = (rest[:4], rest[4:])

    last_got = exchange(sent)
    duals = pl.pallas_call(
        inner_dual_kernel,
        name="inner_duals",
        in_specs=[split(8, buses), split(2, inner), split(8, inner), split(1, inner)],
        out_shape=shape_of(8, branch_count),
        out_specs=split(8, inner),
        cost_estimate=cost(10**7, 3 * 10**6),
        **common,
    )(state, inner_ends, y_inner, level_row)
    duals = pl.pallas_call(
        outer_dual_kernel,
        name="outer_duals",
        in_specs=[pl.BlockSpec(memory_space=pl.ANY)]
        + [whole(last_shape)] * 4
        + [split(8, buses), split(1, cross), split(8, cross), split(1, cross, start)],
        out_shape=shape_of(8, branch_count),
        out_specs=split(8, cross, start),
        input_output_aliases={0: 0},
        cost_estimate=cost(10**6, 10**6),
        **common,
    )(duals, *last_got, state, from_row, y_cross, level_row)
    return (bus_state, duals, hv_dual.reshape(terms))


def solution(mesh):
    return jax.shard_map(
        on_device,
        mesh=mesh,
        in_specs=(
            P(None, ("gx", "gy")),
            P(None, ("gx", "gy")),
            P(None, ("gx", "gy")),
            P(None, ("gx", "gy")),
            P(("gx", "gy")),
            P(("gx", "gy"), None),
            P(None, None, ("gx", "gy")),
            P(None, ("gx", "gy")),
            P(None, ("gx", "gy")),
            P(("gx", "gy")),
            P(("gx", "gy")),
            P(("gx", "gy")),
            P(("gx", "gy")),
        ),
        out_specs=(P(None, ("gx", "gy")), P(None, ("gx", "gy")), P(("gx", "gy"))),
        check_vma=False,
    )
```

profile of v0, /device:TPU:5, one launch (start us, length us, event | category | flops | bytes accessed | tf_op | source)
XLA Modules:
  0.0 120.0 jit_solution(15815964176753359403)
XLA Ops:
  0.6 2.8 %copy-done = f32[8,8,24576]{2,1,0:T(8,128)S(1)} copy-done((f32[8,8,24576]{2,1,0:T(8,128)S(1)}, f32[8,8,24576]{2,1,0:T(8,128)}, u32[]{:S(2)}) %copy-start) | copy-done | bytes 6291480
  3.4 1.1 copy-done.5
  4.6 1.1 copy-done.7
  5.7 0.9 copy-done.9
  6.6 0.9 copy-done.11
  7.5 0.7 copy-done.29
  8.3 0.7 copy-done.31
  9.0 0.7 copy-done.59
  9.6 0.7 copy-done.62
  10.3 3.6 %first_messages.1 = (f32[25,1024]{1,0:T(8,128)}, f32[25,1024]{1,0:T(8,128)}, f32[25,1024]{1,0:T(8,128)S(1)}, f32[25,1024]{1,0:T(8,128)S(1)}, f32[16,1024]{1,0:T(...) custom-call(s32[32]{0:T(128)S(1)} %copy-done.59, s32[32]{0:T(128)S(1)} %copy-done.62, f32[4,16384]{1,0:T(4,128)S(1)} %copy-done.11, ...), custom_call_target="tpu_custom_call" | custom-call | flops 1000000 | bytes 4000000 | tf_op jit(solution)/shard_map/first_messages/pallas_call | solution.py:623
  13.9 0.6 copy-done.40
  15.1 4.4 %collective-permute-start.1 = (f32[25,1024]{1,0:T(8,128)}, f32[25,1024]{1,0:T(8,128)S(1)}, u32[]{:S(2)}, u32[]{:S(2)}) collective-permute-start(f32[25,1024]{1,0:T(8,128)} %get-tuple-element.38), channel_id=1, source_target_pairs={{4,8},{8,4},{12,16},{16,12},{20,24},{24,20},{5,9},{9,5},{13,17},{1... | collective-permute-start | bytes 307208 | tf_op jit(solution)/shard_map/ppermute | solution.py:24
  19.5 1.3 %collective-permute-start.2 = (f32[25,1024]{1,0:T(8,128)S(1)}, f32[25,1024]{1,0:T(8,128)S(1)}, u32[]{:S(2)}, u32[]{:S(2)}) collective-permute-start(f32[25,1024]{1,0:T(8,128)S(1)} %get-tuple-element.39), channel_id=1, source_target_pairs={{0,1},{1,0},{2,3},{3,2},{4,5},{5,4},{6,7},{7,6},{8,9},{9,8},{10,11... | collective-permute-start | bytes 307208 | tf_op jit(solution)/shard_map/ppermute | solution.py:24
  20.8 3.0 %collective-permute-start.3 = (f32[25,1024]{1,0:T(8,128)S(1)}, f32[25,1024]{1,0:T(8,128)S(1)}, u32[]{:S(2)}, u32[]{:S(2)}) collective-permute-start(f32[25,1024]{1,0:T(8,128)S(1)} %get-tuple-element.40), channel_id=1, source_target_pairs={{1,2},{2,1},{5,6},{6,5},{9,10},{10,9},{13,14},{14,13},{17,18},{18,... | collective-permute-start | bytes 307208 | tf_op jit(solution)/shard_map/ppermute | solution.py:24
  23.8 4.3 %all-to-all-start = ((f32[32,1,128]{2,1,0:T(1,128)}), f32[32,1,128]{2,1,0:T(1,128)S(1)}, u32[]{:S(2)}, u32[]{:S(2)}) async-start(f32[32,1,128]{2,1,0:T(1,128)} %bitcast.4), calls=%async_computation | async-start | bytes 32768 | tf_op jit(solution)/shard_map/all_to_all | solution.py:28
  28.2 2.8 %copy-done.1 = f32[8,8,24576]{2,1,0:T(8,128)S(1)} copy-done((f32[8,8,24576]{2,1,0:T(8,128)S(1)}, f32[8,8,24576]{2,1,0:T(8,128)}, u32[]{:S(2)}) %copy-start.1) | copy-done | bytes 6291480
  30.9 5.6 %inner_first.1 = (f32[8,20480]{1,0:T(8,128)S(1)}, f32[8,16384]{1,0:T(8,128)S(1)}, f32[1,16384]{1,0:T(1,128)S(1)}) custom-call(f32[4,16384]{1,0:T(4,128)S(1)} %copy-done.12, s32[2,20480]{1,0:T(2,128)S(1)} %copy-done.13, f32[64,24576]{1,0:T(8,128)S(1)} %bitcast.13, s32[8,24576]{1,0:T(8,128)S(1)} %copy-done.6, f32[8,24576]{1,0:T(8,128)S(1)} %copy-done.8, ...), custom_call_target="tpu_custom_call" | custom-call | flops 100000000 | bytes 10000000 | tf_op jit(solution)/shard_map/inner_first/pallas_call | solution.py:646
  36.6 0.8 copy-done.16
  37.4 0.8 copy-done.27
  38.2 0.6 copy-done.42
  39.4 0.6 copy-done.20
  40.1 2.8 %copy-done.2 = f32[8,8,24576]{2,1,0:T(8,128)S(1)} copy-done((f32[8,8,24576]{2,1,0:T(8,128)S(1)}, f32[8,8,24576]{2,1,0:T(8,128)}, u32[]{:S(2)}) %copy-start.2) | copy-done | bytes 6291480
  42.9 0.9 copy-done.21
  43.8 1.0 copy-done.28
  44.8 0.7 copy-done.32
  45.5 0.8 copy-done.41
  46.4 0.8 copy-done.43
  47.2 0.7 copy-done.45
  47.9 0.7 copy-done.57
  48.7 0.7 copy-done.60
  49.3 0.7 copy-done.63
  50.0 0.7 copy-done.65
  50.6 7.6 %outer_first.1 = (f32[8,16384]{1,0:T(8,128)S(1)}, f32[8,16384]{1,0:T(8,128)S(1)}, f32[8,1024]{1,0:T(8,128)}, f32[8,1024]{1,0:T(8,128)}, f32[8,1024]{1,0:T(8,128)...) custom-call(s32[32]{0:T(128)S(1)} %copy-done.60, ...), custom_call_target="tpu_custom_call" | custom-call | flops 10000000 | bytes 5000000 | tf_op jit(solution)/shard_map/outer_first/pallas_call | solution.py:656
  58.2 0.8 copy-done.23
  59.0 0.6 copy-done.34
  59.7 0.6 copy-done.36
  60.3 0.6 copy-done.38
  62.9 4.2 %collective-permute-start.5 = (f32[8,1024]{1,0:T(8,128)}, f32[8,1024]{1,0:T(8,128)S(1)}, u32[]{:S(2)}, u32[]{:S(2)}) collective-permute-start(f32[8,1024]{1,0:T(8,128)} %get-tuple-element.48), channel_id=1, source_target_pairs={{4,8},{8,4},{12,16},{16,12},{20,24},{24,20},{5,9},{9,5},{13,17},{1... | collective-permute-start | bytes 98312 | tf_op jit(solution)/shard_map/ppermute | solution.py:24
  67.1 1.0 collective-permute-start.6
  68.0 3.0 %collective-permute-start.7 = (f32[8,1024]{1,0:T(8,128)}, f32[8,1024]{1,0:T(8,128)S(1)}, u32[]{:S(2)}, u32[]{:S(2)}) collective-permute-start(f32[8,1024]{1,0:T(8,128)} %get-tuple-element.50), channel_id=1, source_target_pairs={{1,2},{2,1},{5,6},{6,5},{9,10},{10,9},{13,14},{14,13},{17,18},{18,... | collective-permute-start | bytes 98312 | tf_op jit(solution)/shard_map/ppermute | solution.py:24
  71.0 4.1 %all-to-all-start.1 = ((f32[32,1,128]{2,1,0:T(1,128)}), f32[32,1,128]{2,1,0:T(1,128)S(1)}, u32[]{:S(2)}, u32[]{:S(2)}) async-start(f32[32,1,128]{2,1,0:T(1,128)} %bitcast.30), calls=%async_computation.1 | async-start | bytes 32768 | tf_op jit(solution)/shard_map/all_to_all | solution.py:28
  75.2 2.8 %copy-done.3 = f32[8,8,24576]{2,1,0:T(8,128)S(1)} copy-done((f32[8,8,24576]{2,1,0:T(8,128)S(1)}, f32[8,8,24576]{2,1,0:T(8,128)}, u32[]{:S(2)}) %copy-start.3) | copy-done | bytes 6291480
  78.0 1.1 copy-done.17
  79.1 4.9 %inner_second.1 = (f32[8,20480]{1,0:T(8,128)S(1)}, f32[8,16384]{1,0:T(8,128)S(1)}) custom-call(f32[8,16384]{1,0:T(8,128)S(1)} %get-tuple-element.51.refs_0_.refs_16_, s32[2,20480]{1,0:T(2,128)S(1)} %copy-done.13, f32[64,24576]{1,0:T(8,128)S(1)} %bitcast.15, s32[8,24576]{1,0:T(8,128)S(1)} %copy-done.6, f32[8,24576]{1,0:T(8,128)S(1)} %copy-done.8, ...), custom_call_target="tpu_custom_call" | custom-call | flops 100000000 | bytes 10000000 | tf_op jit(solution)/shard_map/inner_second/pallas_call | solution.py:684
  84.0 0.9 copy-done.18
  84.9 0.8 copy-done.25
  85.7 0.6 copy-done.46
  87.5 2.8 %copy-done.4 = f32[8,8,24576]{2,1,0:T(8,128)S(1)} copy-done((f32[8,8,24576]{2,1,0:T(8,128)S(1)}, f32[8,8,24576]{2,1,0:T(8,128)}, u32[]{:S(2)}) %copy-start.4) | copy-done | bytes 6291480
  90.3 0.9 copy-done.22
  91.2 1.0 copy-done.24
  92.3 1.0 copy-done.26
  93.3 0.9 copy-done.35
  94.2 0.8 copy-done.39
  95.1 0.8 copy-done.47
  95.8 0.8 copy-done.49
  96.6 0.8 copy-done.51
  97.3 0.7 copy-done.53
  98.0 0.7 copy-done.55
  98.8 6.4 %outer_second.1 = (f32[8,16384]{1,0:T(8,128)S(1)}, f32[4,16384]{1,0:T(4,128)}, f32[4,1024]{1,0:T(4,128)S(1)}, f32[4,1024]{1,0:T(4,128)S(1)}, f32[4,1024]{1,0:T(4...) custom-call(s32[32]{0:T(128)S(1)} %copy-done.61, s32[32]{0:T(128)S(1)} %copy-done.66, ...), custom_call_target="tpu_custom_call" | custom-call | flops 10000000 | bytes 5000000 | tf_op jit(solution)/shard_map/outer_second/pallas_call | solution.py:694
  105.2 4.2 %collective-permute-start.9 = (f32[4,1024]{1,0:T(4,128)S(1)}, f32[4,1024]{1,0:T(4,128)S(1)}, u32[]{:S(2)}, u32[]{:S(2)}) collective-permute-start(f32[4,1024]{1,0:T(4,128)S(1)} %get-tuple-element.62), channel_id=1, source_target_pairs={{4,8},{8,4},{12,16},{16,12},{20,24},{24,20},{5,9},{9,5},{13,17},{1... | collective-permute-start | bytes 49160 | tf_op jit(solution)/shard_map/ppermute | solution.py:24
  109.4 1.0 collective-permute-start.10
  110.4 3.0 %collective-permute-start.11 = (f32[4,1024]{1,0:T(4,128)S(1)}, f32[4,1024]{1,0:T(4,128)S(1)}, u32[]{:S(2)}, u32[]{:S(2)}) collective-permute-start(f32[4,1024]{1,0:T(4,128)S(1)} %get-tuple-element.64), channel_id=1, source_target_pairs={{1,2},{2,1},{5,6},{6,5},{9,10},{10,9},{13,14},{14,13},{17,18},{18,... | collective-permute-start | bytes 49160 | tf_op jit(solution)/shard_map/ppermute | solution.py:24
  113.4 3.5 %inner_duals.1.dual_in_ref = f32[8,24576]{1,0:T(8,128)} custom-call(f32[8,16384]{1,0:T(8,128)S(1)} %get-tuple-element.59.s_ref, s32[2,20480]{1,0:T(2,128)S(1)} %copy-done.13, f32[8,20480]{1,0:T(8,128)S(1)} %copy-done.19, s32[1,24576]{1,0:T(1,128)S(1)} %bitcast.22), custom_call_target="tpu_custom_call" | custom-call | flops 10000000 | bytes 3000000 | tf_op jit(solution)/shard_map/inner_duals/pallas_call | solution.py:720
  116.9 3.1 %outer_duals.1 = f32[8,24576]{1,0:T(8,128)} custom-call(f32[8,24576]{1,0:T(8,128)} %inner_duals.1.dual_in_ref, f32[4,1024]{1,0:T(4,128)S(1)} %collective-permute-done.8.xe, f32[4,1024]{1,0:T(4,128)S(1)} %collective-permute-done.9.xo, f32[4,1024]{1,0:T(4,128)S(1)} %collective-permute-done.10.ye, ...), custom_call_target="tpu_custom_call", output_to_operand_aliasing={{}: (0, {})} | custom-call | flops 1000000 | bytes 1000000 | tf_op jit(solution)/shard_map/outer_duals/pallas_call | solution.py:729
  (105 shorter events, 4.6 us)
Async XLA Ops:
  0.6 2.8 %copy-start = (f32[8,8,24576]{2,1,0:T(8,128)S(1)}, f32[8,8,24576]{2,1,0:T(8,128)}, u32[]{:S(2)}) copy-start(f32[8,8,24576]{2,1,0:T(8,128)} %param.19) | copy-start | bytes 18874372
  3.4 1.1 copy-start.5
  4.6 1.1 copy-start.7
  5.7 0.9 copy-start.9
  6.6 0.9 copy-start.11
  7.5 0.7 copy-start.29
  8.2 0.7 copy-start.31
  9.0 0.7 copy-start.59
  10.3 17.8 %copy-start.6 = (s32[8,24576]{1,0:T(8,128)S(1)}, s32[8,24576]{1,0:T(8,128)}, u32[]{:S(2)}) copy-start(s32[8,24576]{1,0:T(8,128)} %refs_20_.3) | copy-start | bytes 2359300
  10.3 17.8 %copy-start.8 = (f32[8,24576]{1,0:T(8,128)S(1)}, f32[8,24576]{1,0:T(8,128)}, u32[]{:S(2)}) copy-start(f32[8,24576]{1,0:T(8,128)} %refs_21_.1) | copy-start | bytes 2359300
  10.3 17.8 %copy-start.10 = (s32[24576]{0:T(1024)S(1)}, s32[24576]{0:T(1024)}, u32[]{:S(2)}) copy-start(s32[24576]{0:T(1024)} %param.22) | copy-start | bytes 294916
  10.3 17.9 %copy-start.12 = (f32[4,16384]{1,0:T(4,128)S(1)}, f32[4,16384]{1,0:T(4,128)}, u32[]{:S(2)}) copy-start(f32[4,16384]{1,0:T(4,128)} %refs_11_.1) | copy-start | bytes 786436
  10.3 17.9 %copy-start.13 = (s32[2,20480]{1,0:T(2,128)S(1)}, s32[2,20480]{1,0:T(2,128)}, u32[]{:S(2)}) copy-start(s32[2,20480]{1,0:T(2,128)} %index_ref.1) | copy-start | bytes 491524
  10.3 29.8 %copy-start.14 = (f32[4,16384]{1,0:T(4,128)S(1)}, f32[4,16384]{1,0:T(4,128)}, u32[]{:S(2)}) copy-start(f32[4,16384]{1,0:T(4,128)} %refs_26_.1) | copy-start | bytes 786436
  10.3 29.8 %copy-start.15 = (f32[4,16384]{1,0:T(4,128)S(1)}, f32[4,16384]{1,0:T(4,128)}, u32[]{:S(2)}) copy-start(f32[4,16384]{1,0:T(4,128)} %refs_27_.1) | copy-start | bytes 786436
  10.3 29.8 %copy-start.30 = (s32[4096]{0:T(1024)S(1)}, s32[4096]{0:T(1024)}, u32[]{:S(2)}) copy-start(s32[4096]{0:T(1024)} %param.17) | copy-start | bytes 49156
  15.1 24.3 %collective-permute-start = (f32[25,1024]{1,0:T(8,128)}, f32[25,1024]{1,0:T(8,128)S(1)}, u32[]{:S(2)}, u32[]{:S(2)}) collective-permute-start(f32[25,1024]{1,0:T(8,128)} %get-tuple-element.37), channel_id=1, source_target_pairs={{0,4},{4,0},{8,12},{12,8},{16,20},{20,16},{24,28},{28,24},{1,5},{5... | collective-permute-start | bytes 307208 | tf_op jit(solution)/shard_map/ppermute | solution.py:24
  15.1 24.3 %collective-permute-start.1 = (f32[25,1024]{1,0:T(8,128)}, f32[25,1024]{1,0:T(8,128)S(1)}, u32[]{:S(2)}, u32[]{:S(2)}) collective-permute-start(f32[25,1024]{1,0:T(8,128)} %get-tuple-element.38), channel_id=1, source_target_pairs={{4,8},{8,4},{12,16},{16,12},{20,24},{24,20},{5,9},{9,5},{13,17},{1... | collective-permute-start | bytes 307208 | tf_op jit(solution)/shard_map/ppermute | solution.py:24
  19.5 19.9 %collective-permute-start.2 = (f32[25,1024]{1,0:T(8,128)S(1)}, f32[25,1024]{1,0:T(8,128)S(1)}, u32[]{:S(2)}, u32[]{:S(2)}) collective-permute-start(f32[25,1024]{1,0:T(8,128)S(1)} %get-tuple-element.39), channel_id=1, source_target_pairs={{0,1},{1,0},{2,3},{3,2},{4,5},{5,4},{6,7},{7,6},{8,9},{9,8},{10,11... | collective-permute-start | bytes 307208 | tf_op jit(solution)/shard_map/ppermute | solution.py:24
  20.8 18.6 %collective-permute-start.3 = (f32[25,1024]{1,0:T(8,128)S(1)}, f32[25,1024]{1,0:T(8,128)S(1)}, u32[]{:S(2)}, u32[]{:S(2)}) collective-permute-start(f32[25,1024]{1,0:T(8,128)S(1)} %get-tuple-element.40), channel_id=1, source_target_pairs={{1,2},{2,1},{5,6},{6,5},{9,10},{10,9},{13,14},{14,13},{17,18},{18,... | collective-permute-start | bytes 307208 | tf_op jit(solution)/shard_map/ppermute | solution.py:24
  23.8 15.0 %all-to-all-start = ((f32[32,1,128]{2,1,0:T(1,128)}), f32[32,1,128]{2,1,0:T(1,128)S(1)}, u32[]{:S(2)}, u32[]{:S(2)}) async-start(f32[32,1,128]{2,1,0:T(1,128)} %bitcast.4), calls=%async_computation | async-start | bytes 32768 | tf_op jit(solution)/shard_map/all_to_all | solution.py:28
  28.2 2.8 %copy-start.1 = (f32[8,8,24576]{2,1,0:T(8,128)S(1)}, f32[8,8,24576]{2,1,0:T(8,128)}, u32[]{:S(2)}) copy-start(f32[8,8,24576]{2,1,0:T(8,128)} %param.19) | copy-start | bytes 18874372
  36.5 0.8 copy-start.16
  37.4 0.8 copy-start.27
  39.4 0.7 copy-start.20
  40.1 2.8 %copy-start.2 = (f32[8,8,24576]{2,1,0:T(8,128)S(1)}, f32[8,8,24576]{2,1,0:T(8,128)}, u32[]{:S(2)}) copy-start(f32[8,8,24576]{2,1,0:T(8,128)} %param.19) | copy-start | bytes 18874372
  42.9 0.9 copy-start.21
  43.8 1.0 copy-start.28
  44.8 0.7 copy-start.32
  45.5 0.8 copy-start.41
  46.4 0.8 copy-start.43
  47.2 0.7 copy-start.45
  47.9 0.7 copy-start.57
  58.2 0.8 copy-start.23
  62.7 24.8 %copy-start.33 = (s32[1,4096]{1,0:T(1,128)S(1)}, s32[1,4096]{1,0:T(1,128)}, u32[]{:S(2)}) copy-start(s32[1,4096]{1,0:T(1,128)} %refs_17_.1) | copy-start | bytes 49156
  62.7 24.8 %copy-start.61 = (s32[32]{0:T(128)S(1)}, s32[32]{0:T(128)}, u32[]{:S(2)}) copy-start(s32[32]{0:T(128)} %refs_0_.5) | copy-start | bytes 388
  62.7 24.8 %copy-start.64 = (s32[32]{0:T(128)S(1)}, s32[32]{0:T(128)}, u32[]{:S(2)}) copy-start(s32[32]{0:T(128)} %refs_2_.3) | copy-start | bytes 388
  62.7 24.8 %copy-start.66 = (s32[32]{0:T(128)S(1)}, s32[32]{0:T(128)}, u32[]{:S(2)}) copy-start(s32[32]{0:T(128)} %refs_1_.7) | copy-start | bytes 388
  62.7 23.0 %collective-permute-start.4 = (f32[8,1024]{1,0:T(8,128)}, f32[8,1024]{1,0:T(8,128)S(1)}, u32[]{:S(2)}, u32[]{:S(2)}) collective-permute-start(f32[8,1024]{1,0:T(8,128)} %get-tuple-element.47), channel_id=1, source_target_pairs={{0,4},{4,0},{8,12},{12,8},{16,20},{20,16},{24,28},{28,24},{1,5},{5... | collective-permute-start | bytes 98312 | tf_op jit(solution)/shard_map/ppermute | solution.py:24
  62.9 22.8 %collective-permute-start.5 = (f32[8,1024]{1,0:T(8,128)}, f32[8,1024]{1,0:T(8,128)S(1)}, u32[]{:S(2)}, u32[]{:S(2)}) collective-permute-start(f32[8,1024]{1,0:T(8,128)} %get-tuple-element.48), channel_id=1, source_target_pairs={{4,8},{8,4},{12,16},{16,12},{20,24},{24,20},{5,9},{9,5},{13,17},{1... | collective-permute-start | bytes 98312 | tf_op jit(solution)/shard_map/ppermute | solution.py:24
  67.1 19.2 %collective-permute-start.6 = (f32[8,1024]{1,0:T(8,128)}, f32[8,1024]{1,0:T(8,128)S(1)}, u32[]{:S(2)}, u32[]{:S(2)}) collective-permute-start(f32[8,1024]{1,0:T(8,128)} %get-tuple-element.49), channel_id=1, source_target_pairs={{0,1},{1,0},{2,3},{3,2},{4,5},{5,4},{6,7},{7,6},{8,9},{9,8},{10,11... | collective-permute-start | bytes 98312 | tf_op jit(solution)/shard_map/ppermute | solution.py:24
  68.0 18.9 %collective-permute-start.7 = (f32[8,1024]{1,0:T(8,128)}, f32[8,1024]{1,0:T(8,128)S(1)}, u32[]{:S(2)}, u32[]{:S(2)}) collective-permute-start(f32[8,1024]{1,0:T(8,128)} %get-tuple-element.50), channel_id=1, source_target_pairs={{1,2},{2,1},{5,6},{6,5},{9,10},{10,9},{13,14},{14,13},{17,18},{18,... | collective-permute-start | bytes 98312 | tf_op jit(solution)/shard_map/ppermute | solution.py:24
  71.0 14.6 %all-to-all-start.1 = ((f32[32,1,128]{2,1,0:T(1,128)}), f32[32,1,128]{2,1,0:T(1,128)S(1)}, u32[]{:S(2)}, u32[]{:S(2)}) async-start(f32[32,1,128]{2,1,0:T(1,128)} %bitcast.30), calls=%async_computation.1 | async-start | bytes 32768 | tf_op jit(solution)/shard_map/all_to_all | solution.py:28
  75.2 2.8 %copy-start.3 = (f32[8,8,24576]{2,1,0:T(8,128)S(1)}, f32[8,8,24576]{2,1,0:T(8,128)}, u32[]{:S(2)}) copy-start(f32[8,8,24576]{2,1,0:T(8,128)} %param.19) | copy-start | bytes 18874372
  78.0 1.1 copy-start.17
  79.1 8.5 %copy-start.37 = (f32[16,1024]{1,0:T(8,128)S(1)}, f32[16,1024]{1,0:T(8,128)}, u32[]{:S(2)}) copy-start(f32[16,1024]{1,0:T(8,128)} %copy-done.36) | copy-start | bytes 196612
  84.0 0.9 copy-start.18
  84.9 0.8 copy-start.25
  87.5 2.8 %copy-start.4 = (f32[8,8,24576]{2,1,0:T(8,128)S(1)}, f32[8,8,24576]{2,1,0:T(8,128)}, u32[]{:S(2)}) copy-start(f32[8,8,24576]{2,1,0:T(8,128)} %param.19) | copy-start | bytes 18874372
  90.3 0.9 copy-start.22
  91.2 1.0 copy-start.24
  92.3 1.0 copy-start.26
  93.3 0.9 copy-start.35
  94.2 0.8 copy-start.39
  95.1 0.8 copy-start.47
  95.8 0.8 copy-start.49
  96.6 0.8 copy-start.51
  97.3 0.7 copy-start.53
  98.0 0.7 copy-start.55
  98.8 14.6 %copy-start.19 = (f32[8,20480]{1,0:T(8,128)S(1)}, f32[8,20480]{1,0:T(8,128)}, u32[]{:S(2)}) copy-start(f32[8,20480]{1,0:T(8,128)} %copy-done.18) | copy-start | bytes 1966084
  105.1 11.8 %collective-permute-start.8 = (f32[4,1024]{1,0:T(4,128)S(1)}, f32[4,1024]{1,0:T(4,128)S(1)}, u32[]{:S(2)}, u32[]{:S(2)}) collective-permute-start(f32[4,1024]{1,0:T(4,128)S(1)} %get-tuple-element.61), channel_id=1, source_target_pairs={{0,4},{4,0},{8,12},{12,8},{16,20},{20,16},{24,28},{28,24},{1,5},{5... | collective-permute-start | bytes 49160 | tf_op jit(solution)/shard_map/ppermute | solution.py:24
  105.2 11.7 %collective-permute-start.9 = (f32[4,1024]{1,0:T(4,128)S(1)}, f32[4,1024]{1,0:T(4,128)S(1)}, u32[]{:S(2)}, u32[]{:S(2)}) collective-permute-start(f32[4,1024]{1,0:T(4,128)S(1)} %get-tuple-element.62), channel_id=1, source_target_pairs={{4,8},{8,4},{12,16},{16,12},{20,24},{24,20},{5,9},{9,5},{13,17},{1... | collective-permute-start | bytes 49160 | tf_op jit(solution)/shard_map/ppermute | solution.py:24
  109.4 7.5 %collective-permute-start.10 = (f32[4,1024]{1,0:T(4,128)S(1)}, f32[4,1024]{1,0:T(4,128)S(1)}, u32[]{:S(2)}, u32[]{:S(2)}) collective-permute-start(f32[4,1024]{1,0:T(4,128)S(1)} %get-tuple-element.63), channel_id=1, source_target_pairs={{0,1},{1,0},{2,3},{3,2},{4,5},{5,4},{6,7},{7,6},{8,9},{9,8},{10,11... | collective-permute-start | bytes 49160 | tf_op jit(solution)/shard_map/ppermute | solution.py:24
  110.4 6.5 %collective-permute-start.11 = (f32[4,1024]{1,0:T(4,128)S(1)}, f32[4,1024]{1,0:T(4,128)S(1)}, u32[]{:S(2)}, u32[]{:S(2)}) collective-permute-start(f32[4,1024]{1,0:T(4,128)S(1)} %get-tuple-element.64), channel_id=1, source_target_pairs={{1,2},{2,1},{5,6},{6,5},{9,10},{10,9},{13,14},{14,13},{17,18},{18,... | collective-permute-start | bytes 49160 | tf_op jit(solution)/shard_map/ppermute | solution.py:24
  (17 other events, 10.5 us)
where the time goes:
time: 122 us; the launch traced here: 120 us
  local copies, waits for them, and re-layouts  50.7 us (42%)
  Pallas kernels  34.6 us (28%)
  starting transfers between devices  33.6 us (28%)
    unnamed x134, local copies, waits for them, and re-layouts  50.7 us
    ppermute x12, starting transfers between devices, swapped(): return lax.ppermute(value, axis, moves)  25.2 us
    all_to_all x2, starting transfers between devices, to_all(): lax.all_to_all(rows, ('gx', 'gy'), split_axis=0, concat_axis=0, tiled=True)  8.4 us
    pallas_call x1, Pallas kernels, on_device(): pl.pallas_call(functools.partial(outer_kernel, True), name='outer_first',...  7.6 us
    pallas_call x1, Pallas kernels, on_device(): pl.pallas_call(functools.partial(outer_kernel, False), name='outer_second...  6.38 us
    pallas_call x1, Pallas kernels, on_device(): pl.pallas_call(functools.partial(inner_kernel, True), name='inner_first',...  5.59 us
    pallas_call x1, Pallas kernels, on_device(): pl.pallas_call(functools.partial(inner_kernel, False), name='inner_second...  4.93 us
    pallas_call x1, Pallas kernels, on_device(): pl.pallas_call(start_kernel, name='first_messages', in_specs=[scalars(),...  3.59 us
  transfers between devices with their start and end apart: 14, of which 0 were waited for; matrix products, arithmetic and copies ran while one was open for 0% of the time, Pallas kernels for 12%

commit v1 on v0

--- a/solution.py
+++ b/solution.py
@@ -585,7 +585,7 @@
 
 def params():
     return pltpu.CompilerParams(
-        dimension_semantics=("arbitrary",), vmem_limit_bytes=32 * 1024 * 1024
+        dimension_semantics=("arbitrary",), vmem_limit_bytes=64 * 1024 * 1024
     )
 
 

time: 122 us -> 90.6 us (0.74)
  local copies, waits for them, and re-layouts: 50.7 us -> 0 us
  Pallas kernels: 34.6 us -> 54.2 us
    unnamed x134 -> x0, local copies, waits for them, and re-layouts: 50.7 us -> none
    pallas_call x1, Pallas kernels: 4.93 us -> 8.48 us  [on_device(): pl.pallas_call(functools.partial(inner_kernel, False), name='inner_second...]
    pallas_call x1, Pallas kernels: 5.59 us -> 8.73 us  [on_device(): pl.pallas_call(functools.partial(inner_kernel, True), name='inner_first',...]
    pallas_call x1, Pallas kernels: 3.59 us -> 6.57 us  [on_device(): pl.pallas_call(start_kernel, name='first_messages', in_specs=[scalars(),...]
    pallas_call x1, Pallas kernels: 6.38 us -> 9.27 us  [on_device(): pl.pallas_call(functools.partial(outer_kernel, False), name='outer_second...]
    pallas_call x1, Pallas kernels: 3.5 us -> 5.93 us  [on_device(): pl.pallas_call(inner_dual_kernel, name='inner_duals', in_specs=[split(8,...]
    pallas_call x1, Pallas kernels: 7.6 us -> 10 us  [on_device(): pl.pallas_call(functools.partial(outer_kernel, True), name='outer_first',...]
    pallas_call x1, Pallas kernels: 3.05 us -> 5.18 us  [on_device(): pl.pallas_call(outer_dual_kernel, name='outer_duals', in_specs=[pl.BlockS...]
  transfers between devices with their start and end apart: 14 -> 14, of which waited for: 0 -> 0; matrix products, arithmetic and copies ran while one was open for 0% -> 0% of each run, Pallas kernels for 12% -> 26%
where the time goes in v1:
time: 90.6 us; the launch traced here: 88.9 us
  Pallas kernels  54.2 us (60%)
  starting transfers between devices  33.9 us (37%)
    ppermute x12, starting transfers between devices, swapped(): return lax.ppermute(value, axis, moves)  25.4 us
    pallas_call x1, Pallas kernels, on_device(): pl.pallas_call(functools.partial(outer_kernel, True), name='outer_first',...  10 us
    pallas_call x1, Pallas kernels, on_device(): pl.pallas_call(functools.partial(outer_kernel, False), name='outer_second...  9.27 us
    pallas_call x1, Pallas kernels, on_device(): pl.pallas_call(functools.partial(inner_kernel, True), name='inner_first',...  8.73 us
    all_to_all x2, starting transfers between devices, to_all(): lax.all_to_all(rows, ('gx', 'gy'), split_axis=0, concat_axis=0, tiled=True)  8.51 us
    pallas_call x1, Pallas kernels, on_device(): pl.pallas_call(functools.partial(inner_kernel, False), name='inner_second...  8.48 us
    pallas_call x1, Pallas kernels, on_device(): pl.pallas_call(start_kernel, name='first_messages', in_specs=[scalars(),...  6.57 us
    pallas_call x1, Pallas kernels, on_device(): pl.pallas_call(inner_dual_kernel, name='inner_duals', in_specs=[split(8,...  5.93 us
  transfers between devices with their start and end apart: 14, of which 0 were waited for; matrix products, arithmetic and copies ran while one was open for 0% of the time, Pallas kernels for 26%

profile of v1, /device:TPU:5, one launch (start us, length us, event | category | flops | bytes accessed | tf_op | source)
XLA Modules:
  0.0 88.9 jit_solution(16507615401660723730)
XLA Ops:
  0.6 6.6 %first_messages.1 = (f32[25,1024]{1,0:T(8,128)}, f32[25,1024]{1,0:T(8,128)}, f32[25,1024]{1,0:T(8,128)}, f32[25,1024]{1,0:T(8,128)}, f32[16,1024]{1,0:T(8,128)}, /*index=5*/f32[32,128]{1,0:T(8,128)}, f32[32,128]{1,0:T(8,128)}) custom-call(s32[32]{0:T(128)} %refs_0_.5, s32[32]{0:T(128)} %refs_2_.3, f32[4,16384]{1,0:T(4,128)} %refs_11_.1, s32[1,4096]{1,0:T(1,128)} %refs_17_.1, ...), custom_call_target="tpu_custom_call" | custom-call | flops 1000000 | bytes 4000000 | tf_op jit(solution)/shard_map/first_messages/pallas_call | solution.py:623
  7.2 0.1 collective-permute-start
  7.3 4.4 %collective-permute-start.1 = (f32[25,1024]{1,0:T(8,128)}, f32[25,1024]{1,0:T(8,128)}, u32[]{:S(2)}, u32[]{:S(2)}) collective-permute-start(f32[25,1024]{1,0:T(8,128)} %get-tuple-element.38), channel_id=1, source_target_pairs={{4,8},{8,4},{12,16},{16,12},{20,24},{24,20},{5,9},{9,5},{13,17},{1... | collective-permute-start | bytes 307208 | tf_op jit(solution)/shard_map/ppermute | solution.py:24
  11.7 1.3 %collective-permute-start.2 = (f32[25,1024]{1,0:T(8,128)}, f32[25,1024]{1,0:T(8,128)}, u32[]{:S(2)}, u32[]{:S(2)}) collective-permute-start(f32[25,1024]{1,0:T(8,128)} %get-tuple-element.39), channel_id=1, source_target_pairs={{0,1},{1,0},{2,3},{3,2},{4,5},{5,4},{6,7},{7,6},{8,9},{9,8},{10,11... | collective-permute-start | bytes 307208 | tf_op jit(solution)/shard_map/ppermute | solution.py:24
  13.0 3.0 %collective-permute-start.3 = (f32[25,1024]{1,0:T(8,128)}, f32[25,1024]{1,0:T(8,128)}, u32[]{:S(2)}, u32[]{:S(2)}) collective-permute-start(f32[25,1024]{1,0:T(8,128)} %get-tuple-element.40), channel_id=1, source_target_pairs={{1,2},{2,1},{5,6},{6,5},{9,10},{10,9},{13,14},{14,13},{17,18},{18,... | collective-permute-start | bytes 307208 | tf_op jit(solution)/shard_map/ppermute | solution.py:24
  16.0 4.3 %all-to-all-start = ((f32[32,1,128]{2,1,0:T(1,128)}), f32[32,1,128]{2,1,0:T(1,128)}, u32[]{:S(2)}, u32[]{:S(2)}) async-start(f32[32,1,128]{2,1,0:T(1,128)} %bitcast.29), calls=%async_computation | async-start | bytes 32768 | tf_op jit(solution)/shard_map/all_to_all | solution.py:28
  20.3 8.7 %inner_first.1 = (f32[8,20480]{1,0:T(8,128)}, f32[8,16384]{1,0:T(8,128)}, f32[1,16384]{1,0:T(1,128)}) custom-call(f32[4,16384]{1,0:T(4,128)} %refs_11_.1, s32[2,20480]{1,0:T(2,128)} %index_ref.1, f32[64,24576]{1,0:T(8,128)} %bitcast.13, s32[8,24576]{1,0:T(8,128)} %refs_20_.3, f32[8,24576]{1,0:T(8,128)} %refs_21_.1, s32[1,24576]{1,0:T(1,128)} %bitcast.18), custom_call_target="tpu_custom_call" | custom-call | flops 100000000 | bytes 10000000 | tf_op jit(solution)/shard_map/inner_first/pallas_call | solution.py:646
  29.0 0.0 all-to-all-done
  29.0 0.0 collective-permute-done.refs_5_.refs_6_
  29.0 0.0 collective-permute-done.1.refs_6_.refs_7_
  29.1 0.0 collective-permute-done.2.refs_7_.refs_8_
  29.1 0.0 collective-permute-done.3.refs_8_.refs_9_
  29.1 10.0 %outer_first.1 = (f32[8,16384]{1,0:T(8,128)}, f32[8,16384]{1,0:T(8,128)}, f32[8,1024]{1,0:T(8,128)}, f32[8,1024]{1,0:T(8,128)}, f32[8,1024]{1,0:T(8,128)}, /*ind...) custom-call(s32[32]{0:T(128)} %refs_0_.5, ...), custom_call_target="tpu_custom_call" | custom-call | flops 10000000 | bytes 5000000 | tf_op jit(solution)/shard_map/outer_first/pallas_call | solution.py:656
  39.1 0.1 collective-permute-start.4
  39.3 4.2 %collective-permute-start.5 = (f32[8,1024]{1,0:T(8,128)}, f32[8,1024]{1,0:T(8,128)}, u32[]{:S(2)}, u32[]{:S(2)}) collective-permute-start(f32[8,1024]{1,0:T(8,128)} %get-tuple-element.48), channel_id=1, source_target_pairs={{4,8},{8,4},{12,16},{16,12},{20,24},{24,20},{5,9},{9,5},{13,17},{1... | collective-permute-start | bytes 98312 | tf_op jit(solution)/shard_map/ppermute | solution.py:24
  43.4 1.0 %collective-permute-start.6 = (f32[8,1024]{1,0:T(8,128)}, f32[8,1024]{1,0:T(8,128)}, u32[]{:S(2)}, u32[]{:S(2)}) collective-permute-start(f32[8,1024]{1,0:T(8,128)} %get-tuple-element.49), channel_id=1, source_target_pairs={{0,1},{1,0},{2,3},{3,2},{4,5},{5,4},{6,7},{7,6},{8,9},{9,8},{10,11... | collective-permute-start | bytes 98312 | tf_op jit(solution)/shard_map/ppermute | solution.py:24
  44.4 3.0 %collective-permute-start.7 = (f32[8,1024]{1,0:T(8,128)}, f32[8,1024]{1,0:T(8,128)}, u32[]{:S(2)}, u32[]{:S(2)}) collective-permute-start(f32[8,1024]{1,0:T(8,128)} %get-tuple-element.50), channel_id=1, source_target_pairs={{1,2},{2,1},{5,6},{6,5},{9,10},{10,9},{13,14},{14,13},{17,18},{18,... | collective-permute-start | bytes 98312 | tf_op jit(solution)/shard_map/ppermute | solution.py:24
  47.4 4.2 %all-to-all-start.1 = ((f32[32,1,128]{2,1,0:T(1,128)}), f32[32,1,128]{2,1,0:T(1,128)}, u32[]{:S(2)}, u32[]{:S(2)}) async-start(f32[32,1,128]{2,1,0:T(1,128)} %bitcast.28), calls=%async_computation.1 | async-start | bytes 32768 | tf_op jit(solution)/shard_map/all_to_all | solution.py:28
  51.6 8.5 %inner_second.1 = (f32[8,20480]{1,0:T(8,128)}, f32[8,16384]{1,0:T(8,128)}) custom-call(f32[8,16384]{1,0:T(8,128)} %get-tuple-element.51.refs_0_.refs_16_, s32[2,20480]{1,0:T(2,128)} %index_ref.1, f32[64,24576]{1,0:T(8,128)} %bitcast.15, s32[8,24576]{1,0:T(8,128)} %refs_20_.3, f32[8,24576]{1,0:T(8,128)} %refs_21_.1, s32[1,24576]{1,0:T(1,128)} %bitcast.20, ...), custom_call_target="tpu_custom_call" | custom-call | flops 100000000 | bytes 10000000 | tf_op jit(solution)/shard_map/inner_second/pallas_call | solution.py:684
  60.1 0.0 all-to-all-done.1
  60.1 0.0 collective-permute-done.4.refs_10_
  60.1 0.0 collective-permute-done.5.refs_11_
  60.1 0.0 collective-permute-done.6.refs_12_
  60.2 0.0 collective-permute-done.7.refs_13_
  60.2 9.3 %outer_second.1 = (f32[8,16384]{1,0:T(8,128)}, f32[4,16384]{1,0:T(4,128)}, f32[4,1024]{1,0:T(4,128)}, f32[4,1024]{1,0:T(4,128)}, f32[4,1024]{1,0:T(4,128)}, /*in...) custom-call(s32[32]{0:T(128)} %refs_0_.5, s32[32]{0:T(128)} %refs_1_.7, s32[32]{0:T(128)} %refs_2_.3, ...), custom_call_target="tpu_custom_call" | custom-call | flops 10000000 | bytes 5000000 | tf_op jit(solution)/shard_map/outer_second/pallas_call | solution.py:694
  69.4 0.1 collective-permute-start.8
  69.6 4.2 %collective-permute-start.9 = (f32[4,1024]{1,0:T(4,128)}, f32[4,1024]{1,0:T(4,128)}, u32[]{:S(2)}, u32[]{:S(2)}) collective-permute-start(f32[4,1024]{1,0:T(4,128)} %get-tuple-element.62), channel_id=1, source_target_pairs={{4,8},{8,4},{12,16},{16,12},{20,24},{24,20},{5,9},{9,5},{13,17},{1... | collective-permute-start | bytes 49160 | tf_op jit(solution)/shard_map/ppermute | solution.py:24
  73.8 1.0 %collective-permute-start.10 = (f32[4,1024]{1,0:T(4,128)}, f32[4,1024]{1,0:T(4,128)}, u32[]{:S(2)}, u32[]{:S(2)}) collective-permute-start(f32[4,1024]{1,0:T(4,128)} %get-tuple-element.63), channel_id=1, source_target_pairs={{0,1},{1,0},{2,3},{3,2},{4,5},{5,4},{6,7},{7,6},{8,9},{9,8},{10,11... | collective-permute-start | bytes 49160 | tf_op jit(solution)/shard_map/ppermute | solution.py:24
  74.8 3.0 %collective-permute-start.11 = (f32[4,1024]{1,0:T(4,128)}, f32[4,1024]{1,0:T(4,128)}, u32[]{:S(2)}, u32[]{:S(2)}) collective-permute-start(f32[4,1024]{1,0:T(4,128)} %get-tuple-element.64), channel_id=1, source_target_pairs={{1,2},{2,1},{5,6},{6,5},{9,10},{10,9},{13,14},{14,13},{17,18},{18,... | collective-permute-start | bytes 49160 | tf_op jit(solution)/shard_map/ppermute | solution.py:24
  77.8 5.9 %inner_duals.1.dual_in_ref = f32[8,24576]{1,0:T(8,128)} custom-call(f32[8,16384]{1,0:T(8,128)} %get-tuple-element.59.s_ref, s32[2,20480]{1,0:T(2,128)} %index_ref.1, f32[8,20480]{1,0:T(8,128)} %get-tuple-element.60.y_ref, s32[1,24576]{1,0:T(1,128)} %bitcast.22), custom_call_target="tpu_custom_call" | custom-call | flops 10000000 | bytes 3000000 | tf_op jit(solution)/shard_map/inner_duals/pallas_call | solution.py:720
  83.7 0.0 collective-permute-done.8.xe
  83.7 0.0 collective-permute-done.9.xo
  83.7 0.0 collective-permute-done.10.ye
  83.7 0.0 collective-permute-done.11.yo
  83.7 5.2 %outer_duals.1 = f32[8,24576]{1,0:T(8,128)} custom-call(f32[8,24576]{1,0:T(8,128)} %inner_duals.1.dual_in_ref, f32[4,1024]{1,0:T(4,128)} %collective-permute-done.8.xe, f32[4,1024]{1,0:T(4,128)} %collective-permute-done.9.xo, f32[4,1024]{1,0:T(4,128)} %collective-permute-done.10.ye, ...), custom_call_target="tpu_custom_call", output_to_operand_aliasing={{}: (0, {})} | custom-call | flops 1000000 | bytes 1000000 | tf_op jit(solution)/shard_map/outer_duals/pallas_call | solution.py:729
Async XLA Ops:
  7.2 21.8 %collective-permute-start = (f32[25,1024]{1,0:T(8,128)}, f32[25,1024]{1,0:T(8,128)}, u32[]{:S(2)}, u32[]{:S(2)}) collective-permute-start(f32[25,1024]{1,0:T(8,128)} %get-tuple-element.37), channel_id=1, source_target_pairs={{0,4},{4,0},{8,12},{12,8},{16,20},{20,16},{24,28},{28,24},{1,5},{5... | collective-permute-start | bytes 307208 | tf_op jit(solution)/shard_map/ppermute | solution.py:24
  7.3 21.8 %collective-permute-start.1 = (f32[25,1024]{1,0:T(8,128)}, f32[25,1024]{1,0:T(8,128)}, u32[]{:S(2)}, u32[]{:S(2)}) collective-permute-start(f32[25,1024]{1,0:T(8,128)} %get-tuple-element.38), channel_id=1, source_target_pairs={{4,8},{8,4},{12,16},{16,12},{20,24},{24,20},{5,9},{9,5},{13,17},{1... | collective-permute-start | bytes 307208 | tf_op jit(solution)/shard_map/ppermute | solution.py:24
  11.7 17.4 %collective-permute-start.2 = (f32[25,1024]{1,0:T(8,128)}, f32[25,1024]{1,0:T(8,128)}, u32[]{:S(2)}, u32[]{:S(2)}) collective-permute-start(f32[25,1024]{1,0:T(8,128)} %get-tuple-element.39), channel_id=1, source_target_pairs={{0,1},{1,0},{2,3},{3,2},{4,5},{5,4},{6,7},{7,6},{8,9},{9,8},{10,11... | collective-permute-start | bytes 307208 | tf_op jit(solution)/shard_map/ppermute | solution.py:24
  13.0 16.1 %collective-permute-start.3 = (f32[25,1024]{1,0:T(8,128)}, f32[25,1024]{1,0:T(8,128)}, u32[]{:S(2)}, u32[]{:S(2)}) collective-permute-start(f32[25,1024]{1,0:T(8,128)} %get-tuple-element.40), channel_id=1, source_target_pairs={{1,2},{2,1},{5,6},{6,5},{9,10},{10,9},{13,14},{14,13},{17,18},{18,... | collective-permute-start | bytes 307208 | tf_op jit(solution)/shard_map/ppermute | solution.py:24
  16.0 13.1 %all-to-all-start = ((f32[32,1,128]{2,1,0:T(1,128)}), f32[32,1,128]{2,1,0:T(1,128)}, u32[]{:S(2)}, u32[]{:S(2)}) async-start(f32[32,1,128]{2,1,0:T(1,128)} %bitcast.29), calls=%async_computation | async-start | bytes 32768 | tf_op jit(solution)/shard_map/all_to_all | solution.py:28
  39.1 21.0 %collective-permute-start.4 = (f32[8,1024]{1,0:T(8,128)}, f32[8,1024]{1,0:T(8,128)}, u32[]{:S(2)}, u32[]{:S(2)}) collective-permute-start(f32[8,1024]{1,0:T(8,128)} %get-tuple-element.47), channel_id=1, source_target_pairs={{0,4},{4,0},{8,12},{12,8},{16,20},{20,16},{24,28},{28,24},{1,5},{5... | collective-permute-start | bytes 98312 | tf_op jit(solution)/shard_map/ppermute | solution.py:24
  39.3 20.9 %collective-permute-start.5 = (f32[8,1024]{1,0:T(8,128)}, f32[8,1024]{1,0:T(8,128)}, u32[]{:S(2)}, u32[]{:S(2)}) collective-permute-start(f32[8,1024]{1,0:T(8,128)} %get-tuple-element.48), channel_id=1, source_target_pairs={{4,8},{8,4},{12,16},{16,12},{20,24},{24,20},{5,9},{9,5},{13,17},{1... | collective-permute-start | bytes 98312 | tf_op jit(solution)/shard_map/ppermute | solution.py:24
  43.4 16.7 %collective-permute-start.6 = (f32[8,1024]{1,0:T(8,128)}, f32[8,1024]{1,0:T(8,128)}, u32[]{:S(2)}, u32[]{:S(2)}) collective-permute-start(f32[8,1024]{1,0:T(8,128)} %get-tuple-element.49), channel_id=1, source_target_pairs={{0,1},{1,0},{2,3},{3,2},{4,5},{5,4},{6,7},{7,6},{8,9},{9,8},{10,11... | collective-permute-start | bytes 98312 | tf_op jit(solution)/shard_map/ppermute | solution.py:24
  44.4 15.7 %collective-permute-start.7 = (f32[8,1024]{1,0:T(8,128)}, f32[8,1024]{1,0:T(8,128)}, u32[]{:S(2)}, u32[]{:S(2)}) collective-permute-start(f32[8,1024]{1,0:T(8,128)} %get-tuple-element.50), channel_id=1, source_target_pairs={{1,2},{2,1},{5,6},{6,5},{9,10},{10,9},{13,14},{14,13},{17,18},{18,... | collective-permute-start | bytes 98312 | tf_op jit(solution)/shard_map/ppermute | solution.py:24
  47.4 12.7 %all-to-all-start.1 = ((f32[32,1,128]{2,1,0:T(1,128)}), f32[32,1,128]{2,1,0:T(1,128)}, u32[]{:S(2)}, u32[]{:S(2)}) async-start(f32[32,1,128]{2,1,0:T(1,128)} %bitcast.28), calls=%async_computation.1 | async-start | bytes 32768 | tf_op jit(solution)/shard_map/all_to_all | solution.py:28
  69.4 14.3 %collective-permute-start.8 = (f32[4,1024]{1,0:T(4,128)}, f32[4,1024]{1,0:T(4,128)}, u32[]{:S(2)}, u32[]{:S(2)}) collective-permute-start(f32[4,1024]{1,0:T(4,128)} %get-tuple-element.61), channel_id=1, source_target_pairs={{0,4},{4,0},{8,12},{12,8},{16,20},{20,16},{24,28},{28,24},{1,5},{5... | collective-permute-start | bytes 49160 | tf_op jit(solution)/shard_map/ppermute | solution.py:24
  69.6 14.1 %collective-permute-start.9 = (f32[4,1024]{1,0:T(4,128)}, f32[4,1024]{1,0:T(4,128)}, u32[]{:S(2)}, u32[]{:S(2)}) collective-permute-start(f32[4,1024]{1,0:T(4,128)} %get-tuple-element.62), channel_id=1, source_target_pairs={{4,8},{8,4},{12,16},{16,12},{20,24},{24,20},{5,9},{9,5},{13,17},{1... | collective-permute-start | bytes 49160 | tf_op jit(solution)/shard_map/ppermute | solution.py:24
  73.8 9.9 %collective-permute-start.10 = (f32[4,1024]{1,0:T(4,128)}, f32[4,1024]{1,0:T(4,128)}, u32[]{:S(2)}, u32[]{:S(2)}) collective-permute-start(f32[4,1024]{1,0:T(4,128)} %get-tuple-element.63), channel_id=1, source_target_pairs={{0,1},{1,0},{2,3},{3,2},{4,5},{5,4},{6,7},{7,6},{8,9},{9,8},{10,11... | collective-permute-start | bytes 49160 | tf_op jit(solution)/shard_map/ppermute | solution.py:24
  74.8 9.0 %collective-permute-start.11 = (f32[4,1024]{1,0:T(4,128)}, f32[4,1024]{1,0:T(4,128)}, u32[]{:S(2)}, u32[]{:S(2)}) collective-permute-start(f32[4,1024]{1,0:T(4,128)} %get-tuple-element.64), channel_id=1, source_target_pairs={{1,2},{2,1},{5,6},{6,5},{9,10},{10,9},{13,14},{14,13},{17,18},{18,... | collective-permute-start | bytes 49160 | tf_op jit(solution)/shard_map/ppermute | solution.py:24

commit v2 on v1

v2 whole, which is shorter than its diff:
```python
import functools

import jax
import jax.numpy as jnp
from jax import lax
from jax.experimental import pallas as pl
from jax.experimental.pallas import tpu as pltpu
from jax.sharding import PartitionSpec as P

F32 = jnp.float32
BF16 = jnp.bfloat16
BLK = 256
LANES = 128
GROUP = 8
PAIR = 2 * BLK
STATIC_ROWS = 25
CHUNKS = 4


def swapped(value, axis, first):
    count = lax.axis_size(axis)
    moves = []
    for low in range(first, count - 1, 2):
        moves += [(low, low + 1), (low + 1, low)]
    return lax.ppermute(value, axis, moves)


def to_all(rows):
    return lax.all_to_all(rows, ("gx", "gy"), split_axis=0, concat_axis=0, tiled=True)


def take_lanes(table, lane):
    return jnp.take_along_axis(table, lane, axis=1, mode="promise_in_bounds")


def pick(tables, index, tiles):
    lane, tile = (index & (LANES - 1), index >> 7)
    found = None
    for h in tiles:
        got = take_lanes(tables[h], lane)
        found = got if found is None else jnp.where(tile == h, got, found)
    return found


def spread8(row, rows=8):
    return jnp.broadcast_to(row, (rows, row.shape[-1]))


def one_hot(index, sublane):
    low = spread8(index & (LANES - 1), 16).astype(F32).astype(BF16)
    column = jnp.concatenate([low] * (LANES // 16), axis=0)
    return jnp.where(column == sublane, jnp.ones((), BF16), jnp.zeros((), BF16))


def contract(left, right):
    return lax.dot_general(
        left.astype(BF16), right, (((1,), (1,)), ((), ())), preferred_element_type=F32
    )


def halves(values):
    high = values.astype(BF16).astype(F32)
    return high, values - high


def sublanes():
    return lax.broadcasted_iota(jnp.int32, (LANES, LANES), 0).astype(F32).astype(BF16)


def folded(first, second, distance, mask):
    return jnp.where(
        mask,
        first + pltpu.roll(first, 8 - distance, 0),
        second + pltpu.roll(second, distance, 0),
    )


def product(kkt_ref, cols, target):
    row = lax.broadcasted_iota(jnp.int32, (8, LANES), 0)
    terms = [kkt_ref[8 * i : 8 * i + 8, cols] * target for i in range(8)]
    upper = row < 4
    quads = [
        jnp.where(upper, terms[i], terms[i + 4]) + pltpu.roll(jnp.where(upper, terms[i + 4], terms[i]), 4, 0)
        for i in range(4)
    ]
    even_two = (row & 2) == 0
    twos = [folded(quads[i], quads[i + 2], 2, even_two) for i in range(2)]
    return folded(twos[0], twos[1], 1, (row & 1) == 0)


def doubled(block):
    return block if block.shape[0] == 8 else jnp.concatenate([block, block], axis=0)


def tiles_of(states):
    return [states[:, h * LANES : (h + 1) * LANES] for h in range(states.shape[1] // LANES)]


def lanes(start):
    return pl.ds(pl.multiple_of(start, LANES), LANES)


def upper_half():
    return lax.broadcasted_iota(jnp.int32, (8, LANES), 0) < 4


def inner_ends_of(tables, index_ref, base, cols, t, upper):
    near = index_ref[0:1, cols] - base
    far = index_ref[1:2, cols] - base
    tiles = (0, 1) if t < 2 else (2, 3) if t > 2 else (0, 1, 2, 3)
    both = jnp.where(upper, spread8(near), spread8(far))
    return pick(tables, both, tiles), near, far, tiles


def chunk_copies(sources, buffers, sems, chunk, width):
    spot = pl.ds(chunk * width, width)
    return [
        pltpu.make_async_copy(source.at[:, spot], buffer.at[:, spot], sems.at[k, chunk])
        for k, (source, buffer) in enumerate(zip(sources, buffers))
    ]


def inner_kernel(first, *refs):
    if first:
        s_ref, index_ref, lev_ref, kkt_hbm, act_hbm, lim_hbm, y_hbm, acc_ref, w_ref, *rest = refs
        kkt_ref, act_ref, lim_ref, y_ref, sems, out_sems = rest
        sources, buffers = ((kkt_hbm, act_hbm, lim_hbm), (kkt_ref, act_ref, lim_ref))
        old_ref = None
    else:
        s_ref, index_ref, lev_ref, kkt_hbm, act_hbm, lim_hbm, old_hbm, y_hbm, acc_ref, *rest = refs
        kkt_ref, act_ref, lim_ref, old_ref, y_ref, sems, out_sems = rest
        sources, buffers = ((kkt_hbm, act_hbm, lim_hbm, old_hbm), (kkt_ref, act_ref, lim_ref, old_ref))
        w_ref = None
    upper = upper_half()
    row16 = lax.broadcasted_iota(jnp.int32, (16, LANES), 0)
    sublane = sublanes()
    bus_count = s_ref.shape[1]
    inner = index_ref.shape[1]
    groups = bus_count // (GROUP * BLK)
    chunk = inner // CHUNKS
    for c in range(CHUNKS):
        for copy in chunk_copies(sources, buffers, sems, c, chunk):
            copy.start()
    buses, branches = (bus_count // groups, inner // groups)
    per_pair = branches // (GROUP // 2)
    per_chunk = groups // CHUNKS

    def group(g):
        for p in range(GROUP // 2):
            base = g * buses + p * PAIR
            tables = [doubled(s_ref[:, lanes(base + h * LANES)]) for h in range(4)]
            sums = [jnp.zeros((8, LANES), F32)] * 4
            weights = jnp.zeros((16, LANES), F32)
            for t in range(per_pair // LANES):
                cols = lanes(g * branches + p * per_pair + t * LANES)
                ends, near, far, tiles = inner_ends_of(tables, index_ref, base, cols, t, upper)
                penalty = 0.25 * lev_ref[0:1, cols].astype(F32)
                if first:
                    scaled, target = (None, ends)
                else:
                    scaled = old_ref[:, cols] - ends
                    target = ends - scaled
                flows = product(kkt_ref, cols, target)
                flows = jnp.where(act_ref[:, cols] == 1, lim_ref[:, cols], flows)
                y = flows if first else flows + scaled
                y_ref[:, cols] = y
                high, low = halves(spread8(penalty) * y)
                from_part = jnp.where(upper, high, pltpu.roll(low, 4, 0))
                to_part = jnp.where(upper, pltpu.roll(high, 4, 0), low)
                near_tile, far_tile = (spread8(near >> 7), spread8(far >> 7))
                left = [
                    jnp.concatenate(
                        [
                            jnp.where(near_tile == h, from_part, 0.0),
                            jnp.where(far_tile == h, to_part, 0.0),
                        ],
                        axis=1,
                    )
                    for h in tiles
                ]
                if first:
                    level = spread8(penalty, 16)
                    left.append(
                        jnp.concatenate(
                            [
                                jnp.where(spread8(near >> 7, 16) == row16, level, 0.0),
                                jnp.where(spread8(far >> 7, 16) == row16, level, 0.0),
                            ],
                            axis=1,
                        )
                    )
                right = jnp.concatenate([one_hot(near, sublane), one_hot(far, sublane)], axis=1)
                out = contract(jnp.concatenate(left, axis=0), right)
                for place, h in enumerate(tiles):
                    sums[h] = sums[h] + out[8 * place : 8 * place + 8]
                if first:
                    weights = weights + out[8 * len(tiles) :]
            for h in range(4):
                spot = lanes(base + h * LANES)
                acc_ref[:, spot] = sums[h]
                if first:
                    w_ref[0:1, spot] = weights[h : h + 1]

    for c in range(CHUNKS):
        for copy in chunk_copies(sources, buffers, sems, c, chunk):
            copy.wait()

        @pl.loop(c * per_chunk, (c + 1) * per_chunk)
        def _(g):
            group(g)

        spot = pl.ds(c * chunk, chunk)
        pltpu.make_async_copy(y_ref.at[:, spot], y_hbm.at[:, spot], out_sems.at[c]).start()
    for c in range(CHUNKS):
        spot = pl.ds(c * chunk, chunk)
        pltpu.make_async_copy(y_ref.at[:, spot], y_hbm.at[:, spot], out_sems.at[c]).wait()


def list_places(list_ref, g, base):
    count = list_ref.shape[1] // 4
    return [list_ref[0:1, lanes(k * count + g * LANES)] - base for k in range(4)]


def list_picks(tables, places, upper):
    picks = []
    for k in (0, 2):
        both = jnp.where(upper, spread8(places[k]), spread8(places[k + 1]))
        picks.append(pick(tables, both, range(len(tables))))
    return picks


def even_sides():
    return lax.axis_index("gx") % 2 == 0, lax.axis_index("gy") % 2 == 0


def slots(outs, block):
    even_x, even_y = even_sides()
    wanted = (
        jnp.where(even_x, 1, 0),
        jnp.where(even_x, 0, 1),
        jnp.where(even_y, 3, 2),
        jnp.where(even_y, 2, 3),
    )
    return [(ref, block == want) for ref, want in zip(outs, wanted)]


def write_ghosts(outs, picks, g):
    even_x, even_y = even_sides()
    spot = lanes(g * LANES)
    for out_even, out_odd, even, both in (
        (outs[0], outs[1], even_x, picks[0]),
        (outs[2], outs[3], even_y, picks[1]),
    ):
        out_even[0:4, spot] = jnp.where(even, both[:4], both[4:])
        out_odd[0:4, spot] = jnp.where(even, both[4:], both[:4])


def read_ghost(got, block, spot):
    even_x, even_y = even_sides()
    by_even = jnp.where(even_x, block == 1, block == 0) | jnp.where(even_y, block == 3, block == 2)
    return jnp.where(
        block < 2,
        jnp.where(by_even, got[0][0:4, spot], got[1][0:4, spot]),
        jnp.where(by_even, got[2][0:4, spot], got[3][0:4, spot]),
    )


def hv_states(s_ref, hv_bus_ref, work_ref):
    lane = lax.broadcasted_iota(jnp.int32, (1, LANES), 1)

    def body(t, carry):
        bus = hv_bus_ref[t]
        row = s_ref[2:3, lanes((bus >> 7) * LANES)]
        work_ref[pl.ds(t, 1), :] = jnp.where(lane == (bus & (LANES - 1)), row, 0.0)
        return carry

    lax.fori_loop(0, work_ref.shape[0], body, 0, unroll=8)
    return jnp.broadcast_to(jnp.sum(work_ref[...], axis=1, keepdims=True), work_ref.shape)


def as_row(values, width, offset):
    count = values.shape[0]
    wide = jnp.broadcast_to(values[:, :1], (count, width))
    lane = lax.broadcasted_iota(jnp.int32, (count, width), 1)
    own = lax.broadcasted_iota(jnp.int32, (count, width), 0)
    return jnp.sum(jnp.where(lane == own + offset, wide, 0.0), axis=0, keepdims=True)


def write_hv(out_ref, values, penalties):
    width = out_ref.shape[-1]
    row = as_row(values, width, 0) + as_row(penalties, width, values.shape[0])
    out_ref[...] = jnp.broadcast_to(row, out_ref.shape)


def start_kernel(
    bus_ref, level_ref, s_ref, list_ref, from_ref, kkt_ref, act_ref, lim_ref, lev_ref,
    xe_ref, xo_ref, ye_ref, yo_ref, z_ref, hv_ref, hv_own_ref, hv_pen_ref, work_ref, turn_ref,
):
    outs = (xe_ref, xo_ref, ye_ref, yo_ref)
    upper = upper_half()
    values = hv_states(s_ref, bus_ref, work_ref)
    hv_own_ref[...] = values

    def body(t, carry):
        hv_pen_ref[pl.ds(t, 1), :] = jnp.full((1, LANES), level_ref[t], jnp.int32).astype(F32) * 0.25
        return carry

    lax.fori_loop(0, hv_pen_ref.shape[0], body, 0, unroll=8)
    write_hv(hv_ref, values, hv_pen_ref[...])
    groups = s_ref.shape[1] // (GROUP * BLK)
    buses, cross = (GROUP * BLK, from_ref.shape[1] // groups)
    per_list = xe_ref.shape[1] // cross

    @pl.loop(0, groups)
    def _(g):
        base = g * buses
        tables = [doubled(s_ref[:, lanes(base + h * LANES)]) for h in range(buses // LANES)]
        picks = list_picks(tables, list_places(list_ref, g, base), upper)
        z_ref[0:8, lanes(g * LANES)] = picks[0]
        z_ref[8:16, lanes(g * LANES)] = picks[1]
        write_ghosts(outs, picks, g)
        found = []
        for t in range(cross // LANES):
            cols = lanes(g * cross + t * LANES)
            index = spread8(from_ref[0:1, cols] - (base + t * PAIR))
            ends = pick(tables[4 * t : 4 * t + 4], index, range(4))
            fixed = act_ref[:, cols] == 1
            part = jnp.where(fixed, lim_ref[:, cols], product(kkt_ref, cols, jnp.where(upper, ends, 0.0)))
            for i in range(8):
                turn_ref[64 * t + 8 * i : 64 * t + 8 * i + 8, :] = kkt_ref[8 * i : 8 * i + 8, cols]
            block = [
                jnp.where(fixed, 0.0, turn_ref[pl.ds(64 * t + 4 + j, 8, stride=8), :])[4:] for j in range(4)
            ]
            found.append((part[4:], block, 0.25 * lev_ref[0:1, cols].astype(F32)))
        for ref, here in slots(outs, g // per_list):

            @pl.when(here)
            def _():
                for t, (part, block, penalty) in enumerate(found):
                    spot = lanes((g % per_list) * cross + t * LANES)
                    ref[4:8, spot] = part
                    for j in range(4):
                        ref[8 + 4 * j : 12 + 4 * j, spot] = block[j]
                    ref[24:25, spot] = penalty


def far_hv(first, bus_ref, partner_ref, all_ref, own, penalty, scaled, sum_ref, weight_ref, work_ref, other_ref):
    count = work_ref.shape[0]
    width = all_ref.shape[-1]
    lane = lax.broadcasted_iota(jnp.int32, (1, LANES), 1)
    wide = lax.broadcasted_iota(jnp.int32, (1, width), 1)

    def narrow(row):
        return functools.reduce(jnp.add, [row[:, k : k + LANES] for k in range(0, width, LANES)])

    def fetch(t, carry):
        partner = partner_ref[t]
        device, place = (partner // count, partner % count)
        row = all_ref[pl.ds(device, 1), :]
        work_ref[pl.ds(t, 1), :] = narrow(jnp.where(wide == place, row, 0.0))
        other_ref[pl.ds(t, 1), :] = narrow(jnp.where(wide == place + count, row, 0.0))
        return carry

    lax.fori_loop(0, count, fetch, 0, unroll=8)
    far_value = jnp.sum(work_ref[...], axis=1, keepdims=True)
    far_penalty = jnp.sum(other_ref[...], axis=1, keepdims=True)
    flow = (penalty * own - far_penalty * far_value) / (penalty + far_penalty)
    y = flow if first else flow + scaled
    work_ref[...] = penalty * y
    other_ref[...] = penalty
    sum_ref[...] = jnp.zeros_like(sum_ref)
    if first:
        weight_ref[...] = jnp.zeros_like(weight_ref)

    def place_terms(t, carry):
        bus = bus_ref[t]
        spot = lanes((bus >> 7) * LANES)
        here = lane == (bus & (LANES - 1))
        sum_ref[0:1, spot] += jnp.where(here, work_ref[pl.ds(t, 1), :], 0.0)
        if first:
            weight_ref[0:1, spot] += jnp.where(here, other_ref[pl.ds(t, 1), :], 0.0)
        return carry

    lax.fori_loop(0, count, place_terms, 0, unroll=8)
    return y


def outer_kernel(first, *refs):
    if first:
        (
            bus_ref, partner_ref, all_ref, own_ref, hv_pen_ref, xe, xo, ye, yo, acc_ref, weight_in_ref,
            s_ref, list_ref, from_ref, kkt_ref, act_ref, lim_ref, lev_ref, z_ref, target_ref, prior_ref,
            new_ref, inv_ref, oxe, oxo, oye, oyo, yc_ref, ym_ref, zn_ref, hv_ref, hv_scaled_ref, hv_own_ref,
            sum_ref, hv_weight_ref, work_ref, other_ref,
        ) = refs
        now = (xe, xo, ye, yo)
        scaled = None
    else:
        (
            bus_ref, partner_ref, all_ref, own_ref, hv_pen_ref, scaled_ref, xe, xo, ye, yo, nxe, nxo, nye, nyo,
            acc_ref, inv_ref, s_ref, list_ref, from_ref, kkt_ref, act_ref, lim_ref, lev_ref, z_ref, yc_old_ref,
            ym_old_ref, target_ref, prior_ref,
            new_ref, state_ref, oxe, oxo, oye, oyo, yc_ref, hv_dual_ref,
            sum_ref, work_ref, other_ref,
        ) = refs
        now = (nxe, nxo, nye, nyo)
        hv_weight_ref = None
        scaled = scaled_ref[...]
    fixed_parts = (xe, xo, ye, yo)
    outs = (oxe, oxo, oye, oyo)
    upper = upper_half()
    row8 = lax.broadcasted_iota(jnp.int32, (8, LANES), 0)
    row16 = lax.broadcasted_iota(jnp.int32, (16, LANES), 0)
    power = (row8 == 2) | (row8 == 6)
    sublane = sublanes()
    even_x, even_y = even_sides()
    groups = s_ref.shape[1] // (GROUP * BLK)
    buses, cross = (GROUP * BLK, from_ref.shape[1] // groups)
    per_list = xe.shape[1] // cross
    count = buses // LANES
    hv_y = far_hv(
        first, bus_ref, partner_ref, all_ref, own_ref[...], hv_pen_ref[...], scaled, sum_ref, hv_weight_ref,
        work_ref, other_ref,
    )

    @pl.loop(0, groups)
    def _(g):
        base = g * buses
        tables = [doubled(s_ref[:, lanes(base + h * LANES)]) for h in range(count)]
        places = list_places(list_ref, g, base)
        sums = [None] * count
        weights = [None] * count
        outputs = []
        for t in range(cross // LANES):
            cols = lanes(g * cross + t * LANES)
            ghost = read_ghost(now, g // per_list, lanes((g % per_list) * cross + t * LANES))
            near = from_ref[0:1, cols] - (base + t * PAIR)
            ends = pick(tables[4 * t : 4 * t + 4], spread8(near), range(4))
            ends = jnp.where(upper, ends, doubled(ghost))
            penalty = 0.25 * lev_ref[0:1, cols].astype(F32)
            if first:
                scaled, target = (None, ends)
            else:
                scaled = yc_old_ref[:, cols] - ends
                target = ends - scaled
            flows = product(kkt_ref, cols, target)
            flows = jnp.where(act_ref[:, cols] == 1, lim_ref[:, cols], flows)
            y = flows if first else flows + scaled
            yc_ref[:, cols] = y
            outputs.append(y)
            high, low = halves(spread8(penalty) * y)
            part = jnp.where(upper, high, pltpu.roll(low, 4, 0))
            tile = spread8(near >> 7)
            left = [jnp.where(tile == h, part, 0.0) for h in range(4)]
            if first:
                left.append(jnp.where(spread8(near >> 7, 16) == row16, spread8(penalty, 16), 0.0))
            out = contract(jnp.concatenate(left, axis=0), one_hot(near, sublane))
            for h in range(4):
                sums[4 * t + h] = out[8 * h : 8 * h + 8]
                if first:
                    weights[4 * t + h] = out[32 + h : 33 + h]

        spot = lanes(g * LANES)
        lefts, rights = ([], [])
        for k, (even, pair) in enumerate(((even_x, 0), (even_x, 1), (even_y, 0), (even_y, 1))):
            start = 0 if k < 2 else 2
            from_even = even if pair == 0 else jnp.logical_not(even)

            def received(parts, rows):
                return jnp.where(from_even, parts[start][rows, spot], parts[start + 1][rows, spot])

            rows = slice(4 * k, 4 * k + 4)
            held = z_ref[rows, spot]
            if first:
                scaled, target = (None, held)
            else:
                scaled = ym_old_ref[rows, spot] - held
                target = held - scaled
            flows = received(now, slice(4, 8))
            for j in range(4):
                flows = flows + received(fixed_parts, slice(8 + 4 * j, 12 + 4 * j)) * spread8(target[j : j + 1], 4)
            penalty = received(fixed_parts, slice(24, 25))
            y = flows if first else flows + scaled
            if first:
                ym_ref[rows, spot] = y
            high, low = halves(spread8(penalty, 4) * y)
            part = jnp.concatenate([high, low], axis=0)
            tile = spread8(places[k] >> 7)
            left = [jnp.where(tile == h, part, 0.0) for h in range(count)]
            if first:
                left.append(jnp.where(spread8(places[k] >> 7, 16) == row16, spread8(penalty, 16), 0.0))
            lefts.append(jnp.concatenate(left, axis=0))
            rights.append(one_hot(places[k], sublane))
        out = contract(jnp.concatenate(lefts[:2], axis=1), jnp.concatenate(rights[:2], axis=1))
        out = out + contract(jnp.concatenate(lefts[2:], axis=1), jnp.concatenate(rights[2:], axis=1))

        fresh = []
        for h in range(count):
            cols = lanes(base + h * LANES)
            total = acc_ref[:, cols] + sums[h] + out[8 * h : 8 * h + 8]
            total = total + pltpu.roll(total, 4, 0)
            total = total + jnp.where(power, spread8(sum_ref[0:1, cols]), 0.0)
            prior = doubled(prior_ref[:, cols])
            total = total + prior * doubled(target_ref[:, cols])
            if first:
                weight = weight_in_ref[0:1, cols] + weights[h] + out[8 * count + h : 8 * count + h + 1]
                weight = spread8(weight) + jnp.where(power, spread8(hv_weight_ref[0:1, cols]), 0.0) + prior
                inverse = 1.0 / weight
                inv_ref[:, cols] = inverse
            else:
                inverse = inv_ref[:, cols]
            state = total * inverse
            new_ref[:, cols] = state
            if not first:
                state_ref[:, cols] = state[:4]
            fresh.append(state)

        picks = list_picks(fresh, places, upper)
        write_ghosts(outs, picks, g)
        if first:
            zn_ref[0:8, spot] = picks[0]
            zn_ref[8:16, spot] = picks[1]
            parts = []
            for t in range(cross // LANES):
                cols = lanes(g * cross + t * LANES)
                near = from_ref[0:1, cols] - (base + t * PAIR)
                ends = pick(fresh[4 * t : 4 * t + 4], spread8(near), range(4))
                target = 2.0 * ends - outputs[t]
                part = product(kkt_ref, cols, jnp.where(upper, target, 0.0))
                parts.append(jnp.where(act_ref[:, cols] == 1, lim_ref[:, cols], part)[4:])
            for ref, here in slots(outs, g // per_list):

                @pl.when(here)
                def _():
                    for t, part in enumerate(parts):
                        ref[4:8, lanes((g % per_list) * cross + t * LANES)] = part

    reached = hv_states(new_ref, bus_ref, work_ref)
    left_over = hv_y - reached
    penalty = hv_pen_ref[...]
    if first:
        hv_scaled_ref[...] = left_over
        hv_own_ref[...] = reached - left_over
        write_hv(hv_ref, reached - left_over, penalty)
    else:
        row = as_row(penalty * left_over, LANES, 0)
        hv_dual_ref[...] = row[:, : hv_dual_ref.shape[1]]


def inner_dual_kernel(s_ref, index_ref, y_ref, lev_ref, dual_ref):
    upper = upper_half()
    groups = s_ref.shape[1] // (GROUP * BLK)
    branches = index_ref.shape[1] // groups
    per_pair = branches // (GROUP // 2)

    @pl.loop(0, groups)
    def _(g):
        for p in range(GROUP // 2):
            base = g * GROUP * BLK + p * PAIR
            tables = [s_ref[:, lanes(base + h * LANES)] for h in range(4)]
            for t in range(per_pair // LANES):
                cols = lanes(g * branches + p * per_pair + t * LANES)
                ends, _, _, _ = inner_ends_of(tables, index_ref, base, cols, t, upper)
                penalty = 0.25 * lev_ref[0:1, cols].astype(F32)
                dual_ref[:, cols] = spread8(penalty) * (y_ref[:, cols] - ends)


def outer_dual_kernel(dual_in_ref, xe, xo, ye, yo, s_ref, from_ref, y_ref, lev_ref, dual_ref):
    upper = upper_half()
    groups = s_ref.shape[1] // (GROUP * BLK)
    cross = from_ref.shape[1] // groups
    per_list = xe.shape[1] // cross

    @pl.loop(0, groups)
    def _(g):
        for t in range(cross // LANES):
            base = g * GROUP * BLK + t * PAIR
            cols = lanes(g * cross + t * LANES)
            ghost = read_ghost((xe, xo, ye, yo), g // per_list, lanes((g % per_list) * cross + t * LANES))
            near = from_ref[0:1, cols] - base
            tables = [s_ref[:, lanes(base + h * LANES)] for h in range(4)]
            ends = pick(tables, spread8(near), range(4))
            ends = jnp.where(upper, ends, doubled(ghost))
            penalty = 0.25 * lev_ref[0:1, cols].astype(F32)
            dual_ref[:, cols] = spread8(penalty) * (y_ref[:, cols] - ends)


def part(rows, width, index=0):
    return pl.BlockSpec((rows, width), lambda g: (0, index))


def scalars():
    return pl.BlockSpec(memory_space=pltpu.SMEM)


def in_place():
    return pl.BlockSpec(memory_space=pl.ANY)


def shape_of(*dims):
    return jax.ShapeDtypeStruct(dims, F32)


def params():
    return pltpu.CompilerParams(
        dimension_semantics=("arbitrary",), vmem_limit_bytes=24 * 1024 * 1024
    )


def cost(flops, moved):
    return pl.CostEstimate(flops=flops, bytes_accessed=moved, transcendentals=0)


def on_device(
    bus_start, bus_target, bus_weight, inner_ends, cross_from, boundary_lists, kkt_map, active_set, limits,
    penalty_level, hv_bus, hv_partner, hv_level,
):
    def hbm(x):
        return pltpu.with_memory_space_constraint(x, pltpu.HBM)

    bus_start, bus_target, bus_weight, inner_ends, boundary_lists, active_set, limits = map(
        hbm, (bus_start, bus_target, bus_weight, inner_ends, boundary_lists, active_set, limits)
    )
    hv_bus, hv_partner, hv_level = map(hbm, (hv_bus, hv_partner, hv_level))
    _, bus_count = bus_start.shape
    list_len = boundary_lists.shape[1] // 4
    inner = inner_ends.shape[1]
    cross = cross_from.shape[0]
    branches = kkt_map.shape[2]
    terms = hv_bus.shape[0]
    devices = lax.axis_size("gx") * lax.axis_size("gy")
    behind = inner // cross
    hv_width = max(LANES, 2 * terms)
    kkt = hbm(kkt_map.reshape(64, branches))
    from_row = hbm(cross_from.reshape(1, cross))
    level_row = hbm(penalty_level.reshape(1, branches))
    lists = part(1, 4 * list_len)
    level_in = part(1, inner)
    cross_args = (from_row, kkt, active_set, limits, level_row)
    cross_specs = [part(1, cross), part(64, cross, behind), part(8, cross, behind), part(8, cross, behind), part(1, cross, behind)]
    hv_block = (terms, LANES)
    hv_all_spec = part(devices, hv_width)
    hv_spec = part(*hv_block)
    state_spec, state4_spec, row_spec = (part(8, bus_count), part(4, bus_count), part(1, bus_count))
    held_spec = part(16, list_len)
    common = dict(grid=(1,), compiler_params=params())

    *sent, held, hv_rows, hv_own, hv_pen = pl.pallas_call(
        start_kernel,
        name="first_messages",
        in_specs=[scalars(), scalars(), state4_spec, lists] + cross_specs,
        out_shape=[shape_of(STATIC_ROWS, list_len)] * 4
        + [shape_of(16, list_len), shape_of(devices, hv_width), shape_of(*hv_block), shape_of(*hv_block)],
        out_specs=[part(STATIC_ROWS, list_len)] * 4 + [held_spec, hv_all_spec, hv_spec, hv_spec],
        scratch_shapes=[
            pltpu.VMEM(hv_block, F32),
            pltpu.VMEM((64 * (GROUP // 2), LANES), F32),
        ],
        cost_estimate=cost(10**6, 4 * 10**6),
        **common,
    )(hv_bus, hv_level, bus_start, boundary_lists, *cross_args)

    def exchange(messages):
        xe, xo, ye, yo = messages
        xo = swapped(xo, "gx", 1)
        yo = swapped(yo, "gy", 1)
        xe = swapped(xe, "gx", 0)
        ye = swapped(ye, "gy", 0)
        return (xe, xo, ye, yo)

    def buffers(count):
        kinds = [F32, jnp.int32, F32, F32][:count]
        return (
            [pltpu.VMEM((64 if k == 0 else 8, inner), kind) for k, kind in enumerate(kinds)]
            + [pltpu.VMEM((8, inner), F32)]
            + [pltpu.SemaphoreType.DMA((count, CHUNKS)), pltpu.SemaphoreType.DMA((CHUNKS,))]
        )

    first_got = exchange(sent)
    hv_all = to_all(hv_rows)
    y_inner, sums, weights = pl.pallas_call(
        functools.partial(inner_kernel, True),
        name="inner_first",
        in_specs=[state4_spec, part(2, inner), level_in] + [in_place()] * 3,
        out_shape=[shape_of(8, inner), shape_of(8, bus_count), shape_of(1, bus_count)],
        out_specs=[in_place(), state_spec, row_spec],
        scratch_shapes=buffers(3),
        cost_estimate=cost(10**8, 10**7),
        **common,
    )(bus_start, inner_ends, level_row, kkt, active_set, limits)
    message = part(8, list_len)
    state, inverse, *rest = pl.pallas_call(
        functools.partial(outer_kernel, True),
        name="outer_first",
        in_specs=[scalars()] * 2
        + [hv_all_spec, hv_spec, hv_spec]
        + [part(STATIC_ROWS, list_len)] * 4
        + [state_spec, row_spec, state4_spec, lists]
        + cross_specs
        + [held_spec, state4_spec, state4_spec],
        out_shape=[shape_of(8, bus_count), shape_of(8, bus_count)]
        + [shape_of(8, list_len)] * 4
        + [shape_of(8, cross), pltpu.HBM((16, list_len), F32), pltpu.HBM((16, list_len), F32)]
        + [shape_of(devices, hv_width), pltpu.HBM(hv_block, F32), pltpu.HBM(hv_block, F32)],
        out_specs=[state_spec, state_spec]
        + [message] * 4
        + [part(8, cross), held_spec, held_spec]
        + [hv_all_spec, hv_spec, hv_spec],
        scratch_shapes=[pltpu.VMEM((1, bus_count), F32)] * 2 + [pltpu.VMEM(hv_block, F32)] * 2,
        cost_estimate=cost(10**7, 5 * 10**6),
        **common,
    )(
        hv_bus, hv_partner, hv_all, hv_own, hv_pen, *first_got, sums, weights, bus_start, boundary_lists,
        *cross_args, held, bus_target, bus_weight,
    )
    sent, (y_cross, y_mirror, held, hv_rows, hv_scaled, hv_own) = (rest[:4], rest[4:])
    y_mirror, held, hv_scaled, hv_own = map(hbm, (y_mirror, held, hv_scaled, hv_own))

    second_got = exchange(sent)
    hv_all = to_all(hv_rows)
    y_inner, sums = pl.pallas_call(
        functools.partial(inner_kernel, False),
        name="inner_second",
        in_specs=[state_spec, part(2, inner), level_in] + [in_place()] * 4,
        out_shape=[shape_of(8, inner), shape_of(8, bus_count)],
        out_specs=[in_place(), state_spec],
        scratch_shapes=buffers(4),
        cost_estimate=cost(10**8, 10**7),
        **common,
    )(state, inner_ends, level_row, kkt, active_set, limits, y_inner)
    last = part(4, list_len)
    state, bus_state, *rest = pl.pallas_call(
        functools.partial(outer_kernel, False),
        name="outer_second",
        in_specs=[scalars()] * 2
        + [hv_all_spec, hv_spec, hv_spec, hv_spec]
        + [part(STATIC_ROWS, list_len)] * 4
        + [message] * 4
        + [state_spec, state_spec, state_spec, lists]
        + cross_specs
        + [held_spec, part(8, cross), held_spec, state4_spec, state4_spec],
        out_shape=[shape_of(8, bus_count), shape_of(4, bus_count)]
        + [shape_of(4, list_len)] * 4
        + [shape_of(8, cross), shape_of(1, terms)],
        out_specs=[state_spec, state4_spec] + [last] * 4 + [part(8, cross), part(1, terms)],
        scratch_shapes=[pltpu.VMEM((1, bus_count), F32)] + [pltpu.VMEM(hv_block, F32)] * 2,
        cost_estimate=cost(10**7, 5 * 10**6),
        **common,
    )(
        hv_bus, hv_partner, hv_all, hv_own, hv_pen, hv_scaled, *first_got, *second_got, sums, inverse, state,
        boundary_lists, *cross_args, held, y_cross, y_mirror, bus_target, bus_weight,
    )
    sent, (y_cross, hv_dual) = (rest[:4], rest[4:])

    last_got = exchange(sent)
    duals = pl.pallas_call(
        inner_dual_kernel,
        name="inner_duals",
        in_specs=[state_spec, part(2, inner), part(8, inner), level_in],
        out_shape=shape_of(8, branches),
        out_specs=part(8, inner),
        cost_estimate=cost(10**7, 3 * 10**6),
        **common,
    )(state, inner_ends, y_inner, level_row)
    duals = pl.pallas_call(
        outer_dual_kernel,
        name="outer_duals",
        in_specs=[in_place()] + [last] * 4 + [state_spec, part(1, cross), part(8, cross), part(1, cross, behind)],
        out_shape=shape_of(8, branches),
        out_specs=part(8, cross, behind),
        input_output_aliases={0: 0},
        cost_estimate=cost(10**6, 10**6),
        **common,
    )(duals, *last_got, state, from_row, y_cross, level_row)
    return (bus_state, duals, hv_dual.reshape(terms))


def solution(mesh):
    return jax.shard_map(
        on_device,
        mesh=mesh,
        in_specs=(
            P(None, ("gx", "gy")),
            P(None, ("gx", "gy")),
            P(None, ("gx", "gy")),
            P(None, ("gx", "gy")),
            P(("gx", "gy")),
            P(("gx", "gy"), None),
            P(None, None, ("gx", "gy")),
            P(None, ("gx", "gy")),
            P(None, ("gx", "gy")),
            P(("gx", "gy")),
            P(("gx", "gy")),
            P(("gx", "gy")),
            P(("gx", "gy")),
        ),
        out_specs=(P(None, ("gx", "gy")), P(None, ("gx", "gy")), P(("gx", "gy"))),
        check_vma=False,
    )
```

time: 90.6 us -> 74.8 us (0.83); the launches traced: 88.9 us -> 74.3 us
  Pallas kernels: 54.2 us -> 39.8 us
    pallas_call x2, Pallas kernels: 11.1 us -> 5.53 us  [the longest x1 3.26 us: on_device(): pl.pallas_call(inner_dual_kernel, name='inner_duals', in_specs=[state_spe...]
    pallas_call x1, Pallas kernels: 9.27 us -> 6.33 us  [on_device(): pl.pallas_call(functools.partial(outer_kernel, False), name='outer_second...]
    pallas_call x1, Pallas kernels: 6.57 us -> 3.91 us  [on_device(): pl.pallas_call(start_kernel, name='first_messages', in_specs=[scalars(),...]
    pallas_call x1, Pallas kernels: 10 us -> 7.6 us  [on_device(): pl.pallas_call(functools.partial(outer_kernel, True), name='outer_first',...]
where the time goes in v2:
time: 74.8 us; the launch traced here: 74.3 us
  Pallas kernels  39.8 us (53%)
  starting transfers between devices  33.7 us (45%)
  between operations  0.81 us (1%)
    ppermute x12, starting transfers between devices, swapped(): return lax.ppermute(value, axis, moves)  25.2 us
    all_to_all x2, starting transfers between devices, to_all(): lax.all_to_all(rows, ('gx', 'gy'), split_axis=0, concat_axis=0, tiled=True)  8.46 us
    pallas_call x1, Pallas kernels, on_device(): pl.pallas_call(functools.partial(inner_kernel, True), name='inner_first',...  8.46 us
    pallas_call x1, Pallas kernels, on_device(): pl.pallas_call(functools.partial(inner_kernel, False), name='inner_second...  7.95 us
    pallas_call x1, Pallas kernels, on_device(): pl.pallas_call(functools.partial(outer_kernel, True), name='outer_first',...  7.6 us
    pallas_call x1, Pallas kernels, on_device(): pl.pallas_call(functools.partial(outer_kernel, False), name='outer_second...  6.33 us
    pallas_call x1, Pallas kernels, on_device(): pl.pallas_call(start_kernel, name='first_messages', in_specs=[scalars(),...  3.91 us
    pallas_call x1, Pallas kernels, on_device(): pl.pallas_call(inner_dual_kernel, name='inner_duals', in_specs=[state_spe...  3.26 us
  transfers between devices with their start and end apart: 14, of which 0 were waited for; matrix products, arithmetic and copies ran while one was open for 0% of the time, Pallas kernels for 26%

profile of v2, /device:TPU:5, one launch (start us, length us, event | category | flops | bytes accessed | tf_op | source)
XLA Modules:
  0.0 74.3 jit_solution(4792103078130531167)
XLA Ops:
  0.6 3.9 %first_messages.1 = (f32[25,1024]{1,0:T(8,128)S(1)}, f32[25,1024]{1,0:T(8,128)S(1)}, f32[25,1024]{1,0:T(8,128)S(1)}, f32[25,1024]{1,0:T(8,128)S(1)}, f32[16,1024...) custom-call(s32[32]{0:T(128)} %refs_0_.5, s32[32]{0:T(128)} %level_ref.1, ...), custom_call_target="tpu_custom_call" | custom-call | flops 1000000 | bytes 4000000 | tf_op jit(solution)/shard_map/first_messages/pallas_call | solution.py:648
  4.5 0.0 collective-permute-start
  4.5 4.4 %collective-permute-start.1 = (f32[25,1024]{1,0:T(8,128)S(1)}, f32[25,1024]{1,0:T(8,128)S(1)}, u32[]{:S(2)}, u32[]{:S(2)}) collective-permute-start(f32[25,1024]{1,0:T(8,128)S(1)} %get-tuple-element.40), channel_id=1, source_target_pairs={{4,8},{8,4},{12,16},{16,12},{20,24},{24,20},{5,9},{9,5},{13,17},{1... | collective-permute-start | bytes 307208 | tf_op jit(solution)/shard_map/ppermute | solution.py:25
  8.9 1.3 %collective-permute-start.2 = (f32[25,1024]{1,0:T(8,128)S(1)}, f32[25,1024]{1,0:T(8,128)S(1)}, u32[]{:S(2)}, u32[]{:S(2)}) collective-permute-start(f32[25,1024]{1,0:T(8,128)S(1)} %get-tuple-element.41), channel_id=1, source_target_pairs={{0,1},{1,0},{2,3},{3,2},{4,5},{5,4},{6,7},{7,6},{8,9},{9,8},{10,11... | collective-permute-start | bytes 307208 | tf_op jit(solution)/shard_map/ppermute | solution.py:25
  10.2 3.0 %collective-permute-start.3 = (f32[25,1024]{1,0:T(8,128)S(1)}, f32[25,1024]{1,0:T(8,128)S(1)}, u32[]{:S(2)}, u32[]{:S(2)}) collective-permute-start(f32[25,1024]{1,0:T(8,128)S(1)} %get-tuple-element.42), channel_id=1, source_target_pairs={{1,2},{2,1},{5,6},{6,5},{9,10},{10,9},{13,14},{14,13},{17,18},{18,... | collective-permute-start | bytes 307208 | tf_op jit(solution)/shard_map/ppermute | solution.py:25
  13.3 4.3 %all-to-all-start = ((f32[32,1,128]{2,1,0:T(1,128)}), f32[32,1,128]{2,1,0:T(1,128)S(1)}, u32[]{:S(2)}, u32[]{:S(2)}) async-start(f32[32,1,128]{2,1,0:T(1,128)} %bitcast.4), calls=%async_computation | async-start | bytes 32768 | tf_op jit(solution)/shard_map/all_to_all | solution.py:29
  17.5 8.5 %inner_first.1 = (f32[8,20480]{1,0:T(8,128)S(1)}, f32[8,16384]{1,0:T(8,128)S(1)}, f32[1,16384]{1,0:T(1,128)S(1)}) custom-call(f32[4,16384]{1,0:T(4,128)} %refs_11_.1, s32[2,20480]{1,0:T(2,128)} %index_ref.1, s32[1,24576]{1,0:T(1,128)} %bitcast.19, f32[64,24576]{1,0:T(8,128)} %bitcast.14, s32[8,24576]{1,0:T(8,128)} %refs_20_.3, f32[8,24576]{1,0:T(8,128)} %refs_21_.1), custom_call_target="tpu_custom_call" | custom-call | flops 100000000 | bytes 10000000 | tf_op jit(solution)/shard_map/inner_first/pallas_call | solution.py:681
  26.0 0.0 all-to-all-done
  26.0 0.0 collective-permute-done.refs_5_.refs_6_
  26.0 0.0 collective-permute-done.1.refs_6_.refs_7_
  26.0 0.0 collective-permute-done.2.refs_7_.refs_8_
  26.0 0.0 collective-permute-done.3.refs_8_.refs_9_
  26.0 7.6 %outer_first.1 = (f32[8,16384]{1,0:T(8,128)S(1)}, f32[8,16384]{1,0:T(8,128)S(1)}, f32[8,1024]{1,0:T(8,128)}, f32[8,1024]{1,0:T(8,128)}, f32[8,1024]{1,0:T(8,128)...) custom-call(s32[32]{0:T(128)} %refs_0_.5, ...), custom_call_target="tpu_custom_call" | custom-call | flops 10000000 | bytes 5000000 | tf_op jit(solution)/shard_map/outer_first/pallas_call | solution.py:692
  33.6 0.1 collective-permute-start.4
  33.7 4.2 %collective-permute-start.5 = (f32[8,1024]{1,0:T(8,128)}, f32[8,1024]{1,0:T(8,128)}, u32[]{:S(2)}, u32[]{:S(2)}) collective-permute-start(f32[8,1024]{1,0:T(8,128)} %get-tuple-element.50), channel_id=1, source_target_pairs={{4,8},{8,4},{12,16},{16,12},{20,24},{24,20},{5,9},{9,5},{13,17},{1... | collective-permute-start | bytes 98312 | tf_op jit(solution)/shard_map/ppermute | solution.py:25
  37.9 1.0 %collective-permute-start.6 = (f32[8,1024]{1,0:T(8,128)}, f32[8,1024]{1,0:T(8,128)}, u32[]{:S(2)}, u32[]{:S(2)}) collective-permute-start(f32[8,1024]{1,0:T(8,128)} %get-tuple-element.51), channel_id=1, source_target_pairs={{0,1},{1,0},{2,3},{3,2},{4,5},{5,4},{6,7},{7,6},{8,9},{9,8},{10,11... | collective-permute-start | bytes 98312 | tf_op jit(solution)/shard_map/ppermute | solution.py:25
  38.9 3.0 %collective-permute-start.7 = (f32[8,1024]{1,0:T(8,128)}, f32[8,1024]{1,0:T(8,128)}, u32[]{:S(2)}, u32[]{:S(2)}) collective-permute-start(f32[8,1024]{1,0:T(8,128)} %get-tuple-element.52), channel_id=1, source_target_pairs={{1,2},{2,1},{5,6},{6,5},{9,10},{10,9},{13,14},{14,13},{17,18},{18,... | collective-permute-start | bytes 98312 | tf_op jit(solution)/shard_map/ppermute | solution.py:25
  41.9 4.2 %all-to-all-start.1 = ((f32[32,1,128]{2,1,0:T(1,128)}), f32[32,1,128]{2,1,0:T(1,128)}, u32[]{:S(2)}, u32[]{:S(2)}) async-start(f32[32,1,128]{2,1,0:T(1,128)} %bitcast.7), calls=%async_computation.1 | async-start | bytes 32768 | tf_op jit(solution)/shard_map/all_to_all | solution.py:29
  46.1 7.9 %inner_second.1 = (f32[8,20480]{1,0:T(8,128)S(1)}, f32[8,16384]{1,0:T(8,128)S(1)}) custom-call(f32[8,16384]{1,0:T(8,128)S(1)} %get-tuple-element.53.refs_0_.refs_16_, s32[2,20480]{1,0:T(2,128)} %index_ref.1, s32[1,24576]{1,0:T(1,128)} %bitcast.21, f32[64,24576]{1,0:T(8,128)} %bitcast.16, s32[8,24576]{1,0:T(8,128)} %refs_20_.3, f32[8,24576]{1,0:T(8,128)} %refs_21_.1, ...), custom_call_target="tpu_custom_call" | custom-call | flops 100000000 | bytes 10000000 | tf_op jit(solution)/shard_map/inner_second/pallas_call | solution.py:721
  54.1 0.0 all-to-all-done.1
  54.1 0.0 collective-permute-done.4.refs_10_
  54.1 0.0 collective-permute-done.5.refs_11_
  54.1 0.0 collective-permute-done.6.refs_12_
  54.1 0.0 collective-permute-done.7.refs_13_
  54.1 6.3 %outer_second.1 = (f32[8,16384]{1,0:T(8,128)S(1)}, f32[4,16384]{1,0:T(4,128)}, f32[4,1024]{1,0:T(4,128)S(1)}, f32[4,1024]{1,0:T(4,128)S(1)}, f32[4,1024]{1,0:T(4...) custom-call(s32[32]{0:T(128)} %refs_0_.5, s32[32]{0:T(128)} %refs_1_.7, ...), custom_call_target="tpu_custom_call" | custom-call | flops 10000000 | bytes 5000000 | tf_op jit(solution)/shard_map/outer_second/pallas_call | solution.py:732
  60.5 0.1 collective-permute-start.8
  60.6 4.2 %collective-permute-start.9 = (f32[4,1024]{1,0:T(4,128)S(1)}, f32[4,1024]{1,0:T(4,128)S(1)}, u32[]{:S(2)}, u32[]{:S(2)}) collective-permute-start(f32[4,1024]{1,0:T(4,128)S(1)} %get-tuple-element.64), channel_id=1, source_target_pairs={{4,8},{8,4},{12,16},{16,12},{20,24},{24,20},{5,9},{9,5},{13,17},{1... | collective-permute-start | bytes 49160 | tf_op jit(solution)/shard_map/ppermute | solution.py:25
  64.7 1.0 %collective-permute-start.10 = (f32[4,1024]{1,0:T(4,128)S(1)}, f32[4,1024]{1,0:T(4,128)S(1)}, u32[]{:S(2)}, u32[]{:S(2)}) collective-permute-start(f32[4,1024]{1,0:T(4,128)S(1)} %get-tuple-element.65), channel_id=1, source_target_pairs={{0,1},{1,0},{2,3},{3,2},{4,5},{5,4},{6,7},{7,6},{8,9},{9,8},{10,11... | collective-permute-start | bytes 49160 | tf_op jit(solution)/shard_map/ppermute | solution.py:25
  65.7 3.0 %collective-permute-start.11 = (f32[4,1024]{1,0:T(4,128)S(1)}, f32[4,1024]{1,0:T(4,128)S(1)}, u32[]{:S(2)}, u32[]{:S(2)}) collective-permute-start(f32[4,1024]{1,0:T(4,128)S(1)} %get-tuple-element.66), channel_id=1, source_target_pairs={{1,2},{2,1},{5,6},{6,5},{9,10},{10,9},{13,14},{14,13},{17,18},{18,... | collective-permute-start | bytes 49160 | tf_op jit(solution)/shard_map/ppermute | solution.py:25
  68.7 3.3 %inner_duals.1.dual_in_ref = f32[8,24576]{1,0:T(8,128)} custom-call(f32[8,16384]{1,0:T(8,128)S(1)} %get-tuple-element.61.s_ref, s32[2,20480]{1,0:T(2,128)} %index_ref.1, f32[8,20480]{1,0:T(8,128)S(1)} %get-tuple-element.62.y_ref, s32[1,24576]{1,0:T(1,128)} %bitcast.23), custom_call_target="tpu_custom_call" | custom-call | flops 10000000 | bytes 3000000 | tf_op jit(solution)/shard_map/inner_duals/pallas_call | solution.py:756
  72.0 0.0 collective-permute-done.8.xe
  72.0 0.0 collective-permute-done.9.xo
  72.0 0.0 collective-permute-done.10.ye
  72.0 0.0 collective-permute-done.11.yo
  72.0 2.3 %outer_duals.1 = f32[8,24576]{1,0:T(8,128)} custom-call(f32[8,24576]{1,0:T(8,128)} %inner_duals.1.dual_in_ref, f32[4,1024]{1,0:T(4,128)S(1)} %collective-permute-done.8.xe, f32[4,1024]{1,0:T(4,128)S(1)} %collective-permute-done.9.xo, f32[4,1024]{1,0:T(4,128)S(1)} %collective-permute-done.10.ye, ...), custom_call_target="tpu_custom_call", output_to_operand_aliasing={{}: (0, {})} | custom-call | flops 1000000 | bytes 1000000 | tf_op jit(solution)/shard_map/outer_duals/pallas_call | solution.py:765
Async XLA Ops:
  4.5 21.5 %collective-permute-start = (f32[25,1024]{1,0:T(8,128)S(1)}, f32[25,1024]{1,0:T(8,128)S(1)}, u32[]{:S(2)}, u32[]{:S(2)}) collective-permute-start(f32[25,1024]{1,0:T(8,128)S(1)} %get-tuple-element.39), channel_id=1, source_target_pairs={{0,4},{4,0},{8,12},{12,8},{16,20},{20,16},{24,28},{28,24},{1,5},{5... | collective-permute-start | bytes 307208 | tf_op jit(solution)/shard_map/ppermute | solution.py:25
  4.5 21.5 %collective-permute-start.1 = (f32[25,1024]{1,0:T(8,128)S(1)}, f32[25,1024]{1,0:T(8,128)S(1)}, u32[]{:S(2)}, u32[]{:S(2)}) collective-permute-start(f32[25,1024]{1,0:T(8,128)S(1)} %get-tuple-element.40), channel_id=1, source_target_pairs={{4,8},{8,4},{12,16},{16,12},{20,24},{24,20},{5,9},{9,5},{13,17},{1... | collective-permute-start | bytes 307208 | tf_op jit(solution)/shard_map/ppermute | solution.py:25
  8.9 17.1 %collective-permute-start.2 = (f32[25,1024]{1,0:T(8,128)S(1)}, f32[25,1024]{1,0:T(8,128)S(1)}, u32[]{:S(2)}, u32[]{:S(2)}) collective-permute-start(f32[25,1024]{1,0:T(8,128)S(1)} %get-tuple-element.41), channel_id=1, source_target_pairs={{0,1},{1,0},{2,3},{3,2},{4,5},{5,4},{6,7},{7,6},{8,9},{9,8},{10,11... | collective-permute-start | bytes 307208 | tf_op jit(solution)/shard_map/ppermute | solution.py:25
  10.2 15.8 %collective-permute-start.3 = (f32[25,1024]{1,0:T(8,128)S(1)}, f32[25,1024]{1,0:T(8,128)S(1)}, u32[]{:S(2)}, u32[]{:S(2)}) collective-permute-start(f32[25,1024]{1,0:T(8,128)S(1)} %get-tuple-element.42), channel_id=1, source_target_pairs={{1,2},{2,1},{5,6},{6,5},{9,10},{10,9},{13,14},{14,13},{17,18},{18,... | collective-permute-start | bytes 307208 | tf_op jit(solution)/shard_map/ppermute | solution.py:25
  13.3 12.7 %all-to-all-start = ((f32[32,1,128]{2,1,0:T(1,128)}), f32[32,1,128]{2,1,0:T(1,128)S(1)}, u32[]{:S(2)}, u32[]{:S(2)}) async-start(f32[32,1,128]{2,1,0:T(1,128)} %bitcast.4), calls=%async_computation | async-start | bytes 32768 | tf_op jit(solution)/shard_map/all_to_all | solution.py:29
  33.6 20.5 %collective-permute-start.4 = (f32[8,1024]{1,0:T(8,128)}, f32[8,1024]{1,0:T(8,128)}, u32[]{:S(2)}, u32[]{:S(2)}) collective-permute-start(f32[8,1024]{1,0:T(8,128)} %get-tuple-element.49), channel_id=1, source_target_pairs={{0,4},{4,0},{8,12},{12,8},{16,20},{20,16},{24,28},{28,24},{1,5},{5... | collective-permute-start | bytes 98312 | tf_op jit(solution)/shard_map/ppermute | solution.py:25
  33.7 20.4 %collective-permute-start.5 = (f32[8,1024]{1,0:T(8,128)}, f32[8,1024]{1,0:T(8,128)}, u32[]{:S(2)}, u32[]{:S(2)}) collective-permute-start(f32[8,1024]{1,0:T(8,128)} %get-tuple-element.50), channel_id=1, source_target_pairs={{4,8},{8,4},{12,16},{16,12},{20,24},{24,20},{5,9},{9,5},{13,17},{1... | collective-permute-start | bytes 98312 | tf_op jit(solution)/shard_map/ppermute | solution.py:25
  37.9 16.2 %collective-permute-start.6 = (f32[8,1024]{1,0:T(8,128)}, f32[8,1024]{1,0:T(8,128)}, u32[]{:S(2)}, u32[]{:S(2)}) collective-permute-start(f32[8,1024]{1,0:T(8,128)} %get-tuple-element.51), channel_id=1, source_target_pairs={{0,1},{1,0},{2,3},{3,2},{4,5},{5,4},{6,7},{7,6},{8,9},{9,8},{10,11... | collective-permute-start | bytes 98312 | tf_op jit(solution)/shard_map/ppermute | solution.py:25
  38.9 15.2 %collective-permute-start.7 = (f32[8,1024]{1,0:T(8,128)}, f32[8,1024]{1,0:T(8,128)}, u32[]{:S(2)}, u32[]{:S(2)}) collective-permute-start(f32[8,1024]{1,0:T(8,128)} %get-tuple-element.52), channel_id=1, source_target_pairs={{1,2},{2,1},{5,6},{6,5},{9,10},{10,9},{13,14},{14,13},{17,18},{18,... | collective-permute-start | bytes 98312 | tf_op jit(solution)/shard_map/ppermute | solution.py:25
  41.9 12.2 %all-to-all-start.1 = ((f32[32,1,128]{2,1,0:T(1,128)}), f32[32,1,128]{2,1,0:T(1,128)}, u32[]{:S(2)}, u32[]{:S(2)}) async-start(f32[32,1,128]{2,1,0:T(1,128)} %bitcast.7), calls=%async_computation.1 | async-start | bytes 32768 | tf_op jit(solution)/shard_map/all_to_all | solution.py:29
  60.5 11.5 %collective-permute-start.8 = (f32[4,1024]{1,0:T(4,128)S(1)}, f32[4,1024]{1,0:T(4,128)S(1)}, u32[]{:S(2)}, u32[]{:S(2)}) collective-permute-start(f32[4,1024]{1,0:T(4,128)S(1)} %get-tuple-element.63), channel_id=1, source_target_pairs={{0,4},{4,0},{8,12},{12,8},{16,20},{20,16},{24,28},{28,24},{1,5},{5... | collective-permute-start | bytes 49160 | tf_op jit(solution)/shard_map/ppermute | solution.py:25
  60.6 11.4 %collective-permute-start.9 = (f32[4,1024]{1,0:T(4,128)S(1)}, f32[4,1024]{1,0:T(4,128)S(1)}, u32[]{:S(2)}, u32[]{:S(2)}) collective-permute-start(f32[4,1024]{1,0:T(4,128)S(1)} %get-tuple-element.64), channel_id=1, source_target_pairs={{4,8},{8,4},{12,16},{16,12},{20,24},{24,20},{5,9},{9,5},{13,17},{1... | collective-permute-start | bytes 49160 | tf_op jit(solution)/shard_map/ppermute | solution.py:25
  64.7 7.3 %collective-permute-start.10 = (f32[4,1024]{1,0:T(4,128)S(1)}, f32[4,1024]{1,0:T(4,128)S(1)}, u32[]{:S(2)}, u32[]{:S(2)}) collective-permute-start(f32[4,1024]{1,0:T(4,128)S(1)} %get-tuple-element.65), channel_id=1, source_target_pairs={{0,1},{1,0},{2,3},{3,2},{4,5},{5,4},{6,7},{7,6},{8,9},{9,8},{10,11... | collective-permute-start | bytes 49160 | tf_op jit(solution)/shard_map/ppermute | solution.py:25
  65.7 6.3 %collective-permute-start.11 = (f32[4,1024]{1,0:T(4,128)S(1)}, f32[4,1024]{1,0:T(4,128)S(1)}, u32[]{:S(2)}, u32[]{:S(2)}) collective-permute-start(f32[4,1024]{1,0:T(4,128)S(1)} %get-tuple-element.66), channel_id=1, source_target_pairs={{1,2},{2,1},{5,6},{6,5},{9,10},{10,9},{13,14},{14,13},{17,18},{18,... | collective-permute-start | bytes 49160 | tf_op jit(solution)/shard_map/ppermute | solution.py:25

commit v3 on v2

--- a/solution.py
+++ b/solution.py
@@ -13,8 +13,8 @@
 LANES = 128
 GROUP = 8
 PAIR = 2 * BLK
+SPAN = 64
 STATIC_ROWS = 25
-CHUNKS = 4
 
 
 def swapped(value, axis, first):
@@ -30,7 +30,19 @@
 
 
 def take_lanes(table, lane):
-    return jnp.take_along_axis(table, lane, axis=1, mode="promise_in_bounds")
+    return lax.gather(
+        table,
+        lane[..., None],
+        lax.GatherDimensionNumbers(
+            offset_dims=(),
+            collapsed_slice_dims=(1,),
+            start_index_map=(1,),
+            operand_batching_dims=(0,),
+            start_indices_batching_dims=(0,),
+        ),
+        (1, 1),
+        mode=lax.GatherScatterMode.PROMISE_IN_BOUNDS,
+    )
 
 
 def pick(tables, index, tiles):
@@ -47,8 +59,9 @@
 
 
 def one_hot(index, sublane):
-    low = spread8(index & (LANES - 1), 16).astype(F32).astype(BF16)
-    column = jnp.concatenate([low] * (LANES // 16), axis=0)
+    length = sublane.shape[0]
+    low = spread8(index & (length - 1), 16).astype(F32).astype(BF16)
+    column = jnp.concatenate([low] * (length // 16), axis=0)
     return jnp.where(column == sublane, jnp.ones((), BF16), jnp.zeros((), BF16))
 
 
@@ -63,8 +76,8 @@
     return high, values - high
 
 
-def sublanes():
-    return lax.broadcasted_iota(jnp.int32, (LANES, LANES), 0).astype(F32).astype(BF16)
+def sublanes(length):
+    return lax.broadcasted_iota(jnp.int32, (length, LANES), 0).astype(F32).astype(BF16)
 
 
 def folded(first, second, distance, mask):
@@ -112,15 +125,40 @@
     return pick(tables, both, tiles), near, far, tiles
 
 
+def fetching(kernel, spots):
+    def wrapped(*refs):
+        *refs, sems = refs
+        buffers = refs[len(refs) - len(spots) :]
+        refs = list(refs[: len(refs) - len(spots)])
+        copies = []
+        for k, ((place, first), buffer) in enumerate(zip(spots.items(), buffers)):
+            source = refs[place].at[:, pl.ds(first, buffer.shape[1])]
+            copies.append(pltpu.make_async_copy(source, buffer, sems.at[k]))
+            copies[-1].start()
+            refs[place] = buffer
+
+        def ready():
+            for copy in copies:
+                copy.wait()
+
+        kernel(ready, *refs)
+
+    return wrapped
+
+
+def fetched(*shapes):
+    return [pltpu.VMEM(shape, kind) for shape, kind in shapes] + [pltpu.SemaphoreType.DMA((len(shapes),))]
+
+
 def chunk_copies(sources, buffers, sems, chunk, width):
-    spot = pl.ds(chunk * width, width)
+    spot = pl.ds(pl.multiple_of(chunk * width, LANES), width)
     return [
         pltpu.make_async_copy(source.at[:, spot], buffer.at[:, spot], sems.at[k, chunk])
         for k, (source, buffer) in enumerate(zip(sources, buffers))
     ]
 
 
-def inner_kernel(first, *refs):
+def inner_kernel(first, ready, *refs):
     if first:
         s_ref, index_ref, lev_ref, kkt_hbm, act_hbm, lim_hbm, y_hbm, acc_ref, w_ref, *rest = refs
         kkt_ref, act_ref, lim_ref, y_ref, sems, out_sems = rest
@@ -133,24 +171,27 @@
         w_ref = None
     upper = upper_half()
     row16 = lax.broadcasted_iota(jnp.int32, (16, LANES), 0)
-    sublane = sublanes()
+    sublane = sublanes(SPAN)
     bus_count = s_ref.shape[1]
     inner = index_ref.shape[1]
     groups = bus_count // (GROUP * BLK)
-    chunk = inner // CHUNKS
-    for c in range(CHUNKS):
-        for copy in chunk_copies(sources, buffers, sems, c, chunk):
-            copy.start()
     buses, branches = (bus_count // groups, inner // groups)
     per_pair = branches // (GROUP // 2)
-    per_chunk = groups // CHUNKS
+
+    @pl.loop(0, groups)
+    def _(g):
+        for copy in chunk_copies(sources, buffers, sems, g, branches):
+            copy.start()
+
+    ready()
 
     def group(g):
         for p in range(GROUP // 2):
             base = g * buses + p * PAIR
             tables = [doubled(s_ref[:, lanes(base + h * LANES)]) for h in range(4)]
-            sums = [jnp.zeros((8, LANES), F32)] * 4
-            weights = jnp.zeros((16, LANES), F32)
+            sums = [jnp.zeros((8, SPAN), F32)] * (PAIR // SPAN)
+            weights = jnp.zeros((16, SPAN), F32)
+            jobs = []
             for t in range(per_pair // LANES):
                 cols = lanes(g * branches + p * per_pair + t * LANES)
                 ends, near, far, tiles = inner_ends_of(tables, index_ref, base, cols, t, upper)
@@ -167,7 +208,9 @@
                 high, low = halves(spread8(penalty) * y)
                 from_part = jnp.where(upper, high, pltpu.roll(low, 4, 0))
                 to_part = jnp.where(upper, pltpu.roll(high, 4, 0), low)
-                near_tile, far_tile = (spread8(near >> 7), spread8(far >> 7))
+                near_span, far_span = (near >> 6, far >> 6)
+                near_tile, far_tile = (spread8(near_span), spread8(far_span))
+                spans = [2 * h + half for h in tiles for half in range(2)]
                 left = [
                     jnp.concatenate(
                         [
@@ -176,44 +219,52 @@
                         ],
                         axis=1,
                     )
-                    for h in tiles
+                    for h in spans
                 ]
                 if first:
                     level = spread8(penalty, 16)
                     left.append(
                         jnp.concatenate(
                             [
-                                jnp.where(spread8(near >> 7, 16) == row16, level, 0.0),
-                                jnp.where(spread8(far >> 7, 16) == row16, level, 0.0),
+                                jnp.where(spread8(near_span, 16) == row16, level, 0.0),
+                                jnp.where(spread8(far_span, 16) == row16, level, 0.0),
                             ],
                             axis=1,
                         )
                     )
                 right = jnp.concatenate([one_hot(near, sublane), one_hot(far, sublane)], axis=1)
-                out = contract(jnp.concatenate(left, axis=0), right)
-                for place, h in enumerate(tiles):
+                jobs.append((jnp.concatenate(left, axis=0).astype(BF16), right, spans))
+            for left, right, spans in jobs:
+                out = contract(left, right)
+                for place, h in enumerate(spans):
                     sums[h] = sums[h] + out[8 * place : 8 * place + 8]
                 if first:
-                    weights = weights + out[8 * len(tiles) :]
+                    weights = weights + out[8 * len(spans) :]
             for h in range(4):
                 spot = lanes(base + h * LANES)
-                acc_ref[:, spot] = sums[h]
+                acc_ref[:, spot] = jnp.concatenate([sums[2 * h], sums[2 * h + 1]], axis=1)
                 if first:
-                    w_ref[0:1, spot] = weights[h : h + 1]
-
-    for c in range(CHUNKS):
-        for copy in chunk_copies(sources, buffers, sems, c, chunk):
-            copy.wait()
-
-        @pl.loop(c * per_chunk, (c + 1) * per_chunk)
-        def _(g):
-            group(g)
-
-        spot = pl.ds(c * chunk, chunk)
-        pltpu.make_async_copy(y_ref.at[:, spot], y_hbm.at[:, spot], out_sems.at[c]).start()
-    for c in range(CHUNKS):
-        spot = pl.ds(c * chunk, chunk)
-        pltpu.make_async_copy(y_ref.at[:, spot], y_hbm.at[:, spot], out_sems.at[c]).wait()
+                    w_ref[0:1, spot] = jnp.concatenate(
+                        [weights[2 * h : 2 * h + 1], weights[2 * h + 1 : 2 * h + 2]], axis=1
+                    )
+
+    def out_copy(g):
+        spot = pl.ds(pl.multiple_of(g * branches, LANES), branches)
+        return pltpu.make_async_copy(y_ref.at[:, spot], y_hbm.at[:, spot], out_sems.at[g])
+
+    @pl.loop(0, groups, step=2)
+    def _(start):
+        for g in range(2):
+            for copy in chunk_copies(sources, buffers, sems, start + g, branches):
+                copy.wait()
+        for g in range(2):
+            group(start + g)
+        for g in range(2):
+            out_copy(start + g).start()
+
+    @pl.loop(0, groups)
+    def _(g):
+        out_copy(g).wait()
 
 
 def list_places(list_ref, g, base):
@@ -311,7 +362,7 @@
     buses, cross = (GROUP * BLK, from_ref.shape[1] // groups)
     per_list = xe_ref.shape[1] // cross
 
-    @pl.loop(0, groups)
+    @pl.loop(0, groups, unroll=2)
     def _(g):
         base = g * buses
         tables = [doubled(s_ref[:, lanes(base + h * LANES)]) for h in range(buses // LANES)]
@@ -412,7 +463,7 @@
     row8 = lax.broadcasted_iota(jnp.int32, (8, LANES), 0)
     row16 = lax.broadcasted_iota(jnp.int32, (16, LANES), 0)
     power = (row8 == 2) | (row8 == 6)
-    sublane = sublanes()
+    sublane = sublanes(LANES)
     even_x, even_y = even_sides()
     groups = s_ref.shape[1] // (GROUP * BLK)
     buses, cross = (GROUP * BLK, from_ref.shape[1] // groups)
@@ -423,7 +474,7 @@
         work_ref, other_ref,
     )
 
-    @pl.loop(0, groups)
+    @pl.loop(0, groups, unroll=2)
     def _(g):
         base = g * buses
         tables = [doubled(s_ref[:, lanes(base + h * LANES)]) for h in range(count)]
@@ -553,7 +604,7 @@
     branches = index_ref.shape[1] // groups
     per_pair = branches // (GROUP // 2)
 
-    @pl.loop(0, groups)
+    @pl.loop(0, groups, unroll=2)
     def _(g):
         for p in range(GROUP // 2):
             base = g * GROUP * BLK + p * PAIR
@@ -571,7 +622,7 @@
     cross = from_ref.shape[1] // groups
     per_list = xe.shape[1] // cross
 
-    @pl.loop(0, groups)
+    @pl.loop(0, groups, unroll=2)
     def _(g):
         for t in range(cross // LANES):
             base = g * GROUP * BLK + t * PAIR
@@ -630,6 +681,7 @@
     terms = hv_bus.shape[0]
     devices = lax.axis_size("gx") * lax.axis_size("gy")
     behind = inner // cross
+    groups = bus_count // (GROUP * BLK)
     hv_width = max(LANES, 2 * terms)
     kkt = hbm(kkt_map.reshape(64, branches))
     from_row = hbm(cross_from.reshape(1, cross))
@@ -673,18 +725,19 @@
         return (
             [pltpu.VMEM((64 if k == 0 else 8, inner), kind) for k, kind in enumerate(kinds)]
             + [pltpu.VMEM((8, inner), F32)]
-            + [pltpu.SemaphoreType.DMA((count, CHUNKS)), pltpu.SemaphoreType.DMA((CHUNKS,))]
+            + [pltpu.SemaphoreType.DMA((count, groups)), pltpu.SemaphoreType.DMA((groups,))]
         )
 
+    inner_small = (((2, inner), jnp.int32), ((1, inner), jnp.int32))
     first_got = exchange(sent)
     hv_all = to_all(hv_rows)
     y_inner, sums, weights = pl.pallas_call(
-        functools.partial(inner_kernel, True),
+        fetching(functools.partial(inner_kernel, True), {0: 0, 1: 0, 2: 0}),
         name="inner_first",
-        in_specs=[state4_spec, part(2, inner), level_in] + [in_place()] * 3,
+        in_specs=[in_place()] * 6,
         out_shape=[shape_of(8, inner), shape_of(8, bus_count), shape_of(1, bus_count)],
         out_specs=[in_place(), state_spec, row_spec],
-        scratch_shapes=buffers(3),
+        scratch_shapes=buffers(3) + fetched(((4, bus_count), F32), *inner_small),
         cost_estimate=cost(10**8, 10**7),
         **common,
     )(bus_start, inner_ends, level_row, kkt, active_set, limits)
@@ -719,12 +772,12 @@
     second_got = exchange(sent)
     hv_all = to_all(hv_rows)
     y_inner, sums = pl.pallas_call(
-        functools.partial(inner_kernel, False),
+        fetching(functools.partial(inner_kernel, False), {0: 0, 1: 0, 2: 0}),
         name="inner_second",
-        in_specs=[state_spec, part(2, inner), level_in] + [in_place()] * 4,
+        in_specs=[in_place()] * 7,
         out_shape=[shape_of(8, inner), shape_of(8, bus_count)],
         out_specs=[in_place(), state_spec],
-        scratch_shapes=buffers(4),
+        scratch_shapes=buffers(4) + fetched(((8, bus_count), F32), *inner_small),
         cost_estimate=cost(10**8, 10**7),
         **common,
     )(state, inner_ends, level_row, kkt, active_set, limits, y_inner)

time: 74.8 us -> 69.3 us (0.926)
  Pallas kernels: 39.8 us -> 34.3 us
    pallas_call x2, Pallas kernels: 16.4 us -> 13 us  [the longest x1 6.54 us: on_device(): pl.pallas_call(fetching(functools.partial(inner_kernel, False), {0: 0, 1:...]
    pallas_call x1, Pallas kernels: 6.33 us -> 5.08 us  [on_device(): pl.pallas_call(functools.partial(outer_kernel, False), name='outer_second...]
  transfers between devices with their start and end apart: 14 -> 14, of which waited for: 0 -> 0; matrix products, arithmetic and copies ran while one was open for 0% -> 0% of each run, Pallas kernels for 26% -> 23%
where the time goes in v3:
time: 69.3 us; the launch traced here: 68.8 us
  Pallas kernels  34.3 us (49%)
  starting transfers between devices  33.7 us (49%)
  between operations  0.81 us (1%)
    ppermute x12, starting transfers between devices, swapped(): return lax.ppermute(value, axis, moves)  25.2 us
    all_to_all x2, starting transfers between devices, to_all(): lax.all_to_all(rows, ('gx', 'gy'), split_axis=0, concat_axis=0, tiled=True)  8.45 us
    pallas_call x1, Pallas kernels, on_device(): pl.pallas_call(functools.partial(outer_kernel, True), name='outer_first',...  7.46 us
    pallas_call x1, Pallas kernels, on_device(): pl.pallas_call(fetching(functools.partial(inner_kernel, False), {0: 0, 1:...  6.54 us
    pallas_call x1, Pallas kernels, on_device(): pl.pallas_call(fetching(functools.partial(inner_kernel, True), {0: 0, 1:...  6.45 us
    pallas_call x1, Pallas kernels, on_device(): pl.pallas_call(functools.partial(outer_kernel, False), name='outer_second...  5.08 us
    pallas_call x1, Pallas kernels, on_device(): pl.pallas_call(start_kernel, name='first_messages', in_specs=[scalars(),...  3.87 us
    pallas_call x1, Pallas kernels, on_device(): pl.pallas_call(inner_dual_kernel, name='inner_duals', in_specs=[state_spe...  2.96 us
  transfers between devices with their start and end apart: 14, of which 0 were waited for; matrix products, arithmetic and copies ran while one was open for 0% of the time, Pallas kernels for 23%

profile of v3, /device:TPU:5, one launch (start us, length us, event | category | flops | bytes accessed | tf_op | source)
XLA Modules:
  0.0 68.8 jit_solution(17795435756506935990)
XLA Ops:
  0.6 3.9 %first_messages.1 = (f32[25,1024]{1,0:T(8,128)S(1)}, f32[25,1024]{1,0:T(8,128)S(1)}, f32[25,1024]{1,0:T(8,128)S(1)}, f32[25,1024]{1,0:T(8,128)S(1)}, f32[16,1024...) custom-call(s32[32]{0:T(128)} %refs_0_.5, s32[32]{0:T(128)} %level_ref.1, ...), custom_call_target="tpu_custom_call" | custom-call | flops 1000000 | bytes 4000000 | tf_op jit(solution)/shard_map/first_messages/pallas_call | solution.py:700
  4.5 0.0 collective-permute-start
  4.5 4.4 %collective-permute-start.1 = (f32[25,1024]{1,0:T(8,128)S(1)}, f32[25,1024]{1,0:T(8,128)S(1)}, u32[]{:S(2)}, u32[]{:S(2)}) collective-permute-start(f32[25,1024]{1,0:T(8,128)S(1)} %get-tuple-element.40), channel_id=1, source_target_pairs={{4,8},{8,4},{12,16},{16,12},{20,24},{24,20},{5,9},{9,5},{13,17},{1... | collective-permute-start | bytes 307208 | tf_op jit(solution)/shard_map/ppermute | solution.py:25
  8.9 1.3 %collective-permute-start.2 = (f32[25,1024]{1,0:T(8,128)S(1)}, f32[25,1024]{1,0:T(8,128)S(1)}, u32[]{:S(2)}, u32[]{:S(2)}) collective-permute-start(f32[25,1024]{1,0:T(8,128)S(1)} %get-tuple-element.41), channel_id=1, source_target_pairs={{0,1},{1,0},{2,3},{3,2},{4,5},{5,4},{6,7},{7,6},{8,9},{9,8},{10,11... | collective-permute-start | bytes 307208 | tf_op jit(solution)/shard_map/ppermute | solution.py:25
  10.2 3.0 %collective-permute-start.3 = (f32[25,1024]{1,0:T(8,128)S(1)}, f32[25,1024]{1,0:T(8,128)S(1)}, u32[]{:S(2)}, u32[]{:S(2)}) collective-permute-start(f32[25,1024]{1,0:T(8,128)S(1)} %get-tuple-element.42), channel_id=1, source_target_pairs={{1,2},{2,1},{5,6},{6,5},{9,10},{10,9},{13,14},{14,13},{17,18},{18,... | collective-permute-start | bytes 307208 | tf_op jit(solution)/shard_map/ppermute | solution.py:25
  13.2 4.3 %all-to-all-start = ((f32[32,1,128]{2,1,0:T(1,128)}), f32[32,1,128]{2,1,0:T(1,128)S(1)}, u32[]{:S(2)}, u32[]{:S(2)}) async-start(f32[32,1,128]{2,1,0:T(1,128)} %bitcast.4), calls=%async_computation | async-start | bytes 32768 | tf_op jit(solution)/shard_map/all_to_all | solution.py:29
  17.5 6.4 %inner_first.1 = (f32[8,20480]{1,0:T(8,128)S(1)}, f32[8,16384]{1,0:T(8,128)S(1)}, f32[1,16384]{1,0:T(1,128)S(1)}) custom-call(f32[4,16384]{1,0:T(4,128)} %refs_11_.1, s32[2,20480]{1,0:T(2,128)} %index_ref.1, s32[1,24576]{1,0:T(1,128)} %bitcast.19, f32[64,24576]{1,0:T(8,128)} %bitcast.14, s32[8,24576]{1,0:T(8,128)} %refs_20_.3, f32[8,24576]{1,0:T(8,128)} %refs_21_.1), custom_call_target="tpu_custom_call" | custom-call | flops 100000000 | bytes 10000000 | tf_op jit(solution)/shard_map/inner_first/pallas_call | solution.py:734
  23.9 0.0 all-to-all-done
  23.9 0.0 collective-permute-done.refs_5_.refs_6_
  24.0 0.0 collective-permute-done.1.refs_6_.refs_7_
  24.0 0.0 collective-permute-done.2.refs_7_.refs_8_
  24.0 0.0 collective-permute-done.3.refs_8_.refs_9_
  24.0 7.5 %outer_first.1 = (f32[8,16384]{1,0:T(8,128)S(1)}, f32[8,16384]{1,0:T(8,128)S(1)}, f32[8,1024]{1,0:T(8,128)}, f32[8,1024]{1,0:T(8,128)}, f32[8,1024]{1,0:T(8,128)...) custom-call(s32[32]{0:T(128)} %refs_0_.5, ...), custom_call_target="tpu_custom_call" | custom-call | flops 10000000 | bytes 5000000 | tf_op jit(solution)/shard_map/outer_first/pallas_call | solution.py:745
  31.5 0.3 collective-permute-start.4
  31.8 4.0 %collective-permute-start.5 = (f32[8,1024]{1,0:T(8,128)}, f32[8,1024]{1,0:T(8,128)}, u32[]{:S(2)}, u32[]{:S(2)}) collective-permute-start(f32[8,1024]{1,0:T(8,128)} %get-tuple-element.50), channel_id=1, source_target_pairs={{4,8},{8,4},{12,16},{16,12},{20,24},{24,20},{5,9},{9,5},{13,17},{1... | collective-permute-start | bytes 98312 | tf_op jit(solution)/shard_map/ppermute | solution.py:25
  35.7 1.0 %collective-permute-start.6 = (f32[8,1024]{1,0:T(8,128)}, f32[8,1024]{1,0:T(8,128)}, u32[]{:S(2)}, u32[]{:S(2)}) collective-permute-start(f32[8,1024]{1,0:T(8,128)} %get-tuple-element.51), channel_id=1, source_target_pairs={{0,1},{1,0},{2,3},{3,2},{4,5},{5,4},{6,7},{7,6},{8,9},{9,8},{10,11... | collective-permute-start | bytes 98312 | tf_op jit(solution)/shard_map/ppermute | solution.py:25
  36.7 3.0 %collective-permute-start.7 = (f32[8,1024]{1,0:T(8,128)}, f32[8,1024]{1,0:T(8,128)}, u32[]{:S(2)}, u32[]{:S(2)}) collective-permute-start(f32[8,1024]{1,0:T(8,128)} %get-tuple-element.52), channel_id=1, source_target_pairs={{1,2},{2,1},{5,6},{6,5},{9,10},{10,9},{13,14},{14,13},{17,18},{18,... | collective-permute-start | bytes 98312 | tf_op jit(solution)/shard_map/ppermute | solution.py:25
  39.7 4.2 %all-to-all-start.1 = ((f32[32,1,128]{2,1,0:T(1,128)}), f32[32,1,128]{2,1,0:T(1,128)}, u32[]{:S(2)}, u32[]{:S(2)}) async-start(f32[32,1,128]{2,1,0:T(1,128)} %bitcast.7), calls=%async_computation.1 | async-start | bytes 32768 | tf_op jit(solution)/shard_map/all_to_all | solution.py:29
  43.9 6.5 %inner_second.1 = (f32[8,20480]{1,0:T(8,128)S(1)}, f32[8,16384]{1,0:T(8,128)S(1)}) custom-call(f32[8,16384]{1,0:T(8,128)S(1)} %get-tuple-element.53.refs_0_.refs_16_, s32[2,20480]{1,0:T(2,128)} %index_ref.1, s32[1,24576]{1,0:T(1,128)} %bitcast.21, f32[64,24576]{1,0:T(8,128)} %bitcast.16, s32[8,24576]{1,0:T(8,128)} %refs_20_.3, f32[8,24576]{1,0:T(8,128)} %refs_21_.1, ...), custom_call_target="tpu_custom_call" | custom-call | flops 100000000 | bytes 10000000 | tf_op jit(solution)/shard_map/inner_second/pallas_call | solution.py:774
  50.5 0.0 all-to-all-done.1
  50.5 0.0 collective-permute-done.4.refs_10_
  50.5 0.0 collective-permute-done.5.refs_11_
  50.5 0.0 collective-permute-done.6.refs_12_
  50.5 0.0 collective-permute-done.7.refs_13_
  50.5 5.1 %outer_second.1 = (f32[8,16384]{1,0:T(8,128)S(1)}, f32[4,16384]{1,0:T(4,128)}, f32[4,1024]{1,0:T(4,128)S(1)}, f32[4,1024]{1,0:T(4,128)S(1)}, f32[4,1024]{1,0:T(4...) custom-call(s32[32]{0:T(128)} %refs_0_.5, s32[32]{0:T(128)} %refs_1_.7, ...), custom_call_target="tpu_custom_call" | custom-call | flops 10000000 | bytes 5000000 | tf_op jit(solution)/shard_map/outer_second/pallas_call | solution.py:785
  55.6 0.2 collective-permute-start.8
  55.8 4.1 %collective-permute-start.9 = (f32[4,1024]{1,0:T(4,128)S(1)}, f32[4,1024]{1,0:T(4,128)S(1)}, u32[]{:S(2)}, u32[]{:S(2)}) collective-permute-start(f32[4,1024]{1,0:T(4,128)S(1)} %get-tuple-element.64), channel_id=1, source_target_pairs={{4,8},{8,4},{12,16},{16,12},{20,24},{24,20},{5,9},{9,5},{13,17},{1... | collective-permute-start | bytes 49160 | tf_op jit(solution)/shard_map/ppermute | solution.py:25
  59.9 1.0 %collective-permute-start.10 = (f32[4,1024]{1,0:T(4,128)S(1)}, f32[4,1024]{1,0:T(4,128)S(1)}, u32[]{:S(2)}, u32[]{:S(2)}) collective-permute-start(f32[4,1024]{1,0:T(4,128)S(1)} %get-tuple-element.65), channel_id=1, source_target_pairs={{0,1},{1,0},{2,3},{3,2},{4,5},{5,4},{6,7},{7,6},{8,9},{9,8},{10,11... | collective-permute-start | bytes 49160 | tf_op jit(solution)/shard_map/ppermute | solution.py:25
  60.9 3.0 %collective-permute-start.11 = (f32[4,1024]{1,0:T(4,128)S(1)}, f32[4,1024]{1,0:T(4,128)S(1)}, u32[]{:S(2)}, u32[]{:S(2)}) collective-permute-start(f32[4,1024]{1,0:T(4,128)S(1)} %get-tuple-element.66), channel_id=1, source_target_pairs={{1,2},{2,1},{5,6},{6,5},{9,10},{10,9},{13,14},{14,13},{17,18},{18,... | collective-permute-start | bytes 49160 | tf_op jit(solution)/shard_map/ppermute | solution.py:25
  63.9 3.0 %inner_duals.1.dual_in_ref = f32[8,24576]{1,0:T(8,128)} custom-call(f32[8,16384]{1,0:T(8,128)S(1)} %get-tuple-element.61.s_ref, s32[2,20480]{1,0:T(2,128)} %index_ref.1, f32[8,20480]{1,0:T(8,128)S(1)} %get-tuple-element.62.y_ref, s32[1,24576]{1,0:T(1,128)} %bitcast.23), custom_call_target="tpu_custom_call" | custom-call | flops 10000000 | bytes 3000000 | tf_op jit(solution)/shard_map/inner_duals/pallas_call | solution.py:809
  66.8 0.0 collective-permute-done.8.xe
  66.8 0.0 collective-permute-done.9.xo
  66.8 0.0 collective-permute-done.10.ye
  66.9 0.0 collective-permute-done.11.yo
  66.9 2.0 %outer_duals.1 = f32[8,24576]{1,0:T(8,128)} custom-call(f32[8,24576]{1,0:T(8,128)} %inner_duals.1.dual_in_ref, f32[4,1024]{1,0:T(4,128)S(1)} %collective-permute-done.8.xe, f32[4,1024]{1,0:T(4,128)S(1)} %collective-permute-done.9.xo, f32[4,1024]{1,0:T(4,128)S(1)} %collective-permute-done.10.ye, ...), custom_call_target="tpu_custom_call", output_to_operand_aliasing={{}: (0, {})} | custom-call | flops 1000000 | bytes 1000000 | tf_op jit(solution)/shard_map/outer_duals/pallas_call | solution.py:818
Async XLA Ops:
  4.5 19.4 %collective-permute-start = (f32[25,1024]{1,0:T(8,128)S(1)}, f32[25,1024]{1,0:T(8,128)S(1)}, u32[]{:S(2)}, u32[]{:S(2)}) collective-permute-start(f32[25,1024]{1,0:T(8,128)S(1)} %get-tuple-element.39), channel_id=1, source_target_pairs={{0,4},{4,0},{8,12},{12,8},{16,20},{20,16},{24,28},{28,24},{1,5},{5... | collective-permute-start | bytes 307208 | tf_op jit(solution)/shard_map/ppermute | solution.py:25
  4.5 19.5 %collective-permute-start.1 = (f32[25,1024]{1,0:T(8,128)S(1)}, f32[25,1024]{1,0:T(8,128)S(1)}, u32[]{:S(2)}, u32[]{:S(2)}) collective-permute-start(f32[25,1024]{1,0:T(8,128)S(1)} %get-tuple-element.40), channel_id=1, source_target_pairs={{4,8},{8,4},{12,16},{16,12},{20,24},{24,20},{5,9},{9,5},{13,17},{1... | collective-permute-start | bytes 307208 | tf_op jit(solution)/shard_map/ppermute | solution.py:25
  8.9 15.1 %collective-permute-start.2 = (f32[25,1024]{1,0:T(8,128)S(1)}, f32[25,1024]{1,0:T(8,128)S(1)}, u32[]{:S(2)}, u32[]{:S(2)}) collective-permute-start(f32[25,1024]{1,0:T(8,128)S(1)} %get-tuple-element.41), channel_id=1, source_target_pairs={{0,1},{1,0},{2,3},{3,2},{4,5},{5,4},{6,7},{7,6},{8,9},{9,8},{10,11... | collective-permute-start | bytes 307208 | tf_op jit(solution)/shard_map/ppermute | solution.py:25
  10.2 13.8 %collective-permute-start.3 = (f32[25,1024]{1,0:T(8,128)S(1)}, f32[25,1024]{1,0:T(8,128)S(1)}, u32[]{:S(2)}, u32[]{:S(2)}) collective-permute-start(f32[25,1024]{1,0:T(8,128)S(1)} %get-tuple-element.42), channel_id=1, source_target_pairs={{1,2},{2,1},{5,6},{6,5},{9,10},{10,9},{13,14},{14,13},{17,18},{18,... | collective-permute-start | bytes 307208 | tf_op jit(solution)/shard_map/ppermute | solution.py:25
  13.2 10.7 %all-to-all-start = ((f32[32,1,128]{2,1,0:T(1,128)}), f32[32,1,128]{2,1,0:T(1,128)S(1)}, u32[]{:S(2)}, u32[]{:S(2)}) async-start(f32[32,1,128]{2,1,0:T(1,128)} %bitcast.4), calls=%async_computation | async-start | bytes 32768 | tf_op jit(solution)/shard_map/all_to_all | solution.py:29
  31.5 19.0 %collective-permute-start.4 = (f32[8,1024]{1,0:T(8,128)}, f32[8,1024]{1,0:T(8,128)}, u32[]{:S(2)}, u32[]{:S(2)}) collective-permute-start(f32[8,1024]{1,0:T(8,128)} %get-tuple-element.49), channel_id=1, source_target_pairs={{0,4},{4,0},{8,12},{12,8},{16,20},{20,16},{24,28},{28,24},{1,5},{5... | collective-permute-start | bytes 98312 | tf_op jit(solution)/shard_map/ppermute | solution.py:25
  31.8 18.8 %collective-permute-start.5 = (f32[8,1024]{1,0:T(8,128)}, f32[8,1024]{1,0:T(8,128)}, u32[]{:S(2)}, u32[]{:S(2)}) collective-permute-start(f32[8,1024]{1,0:T(8,128)} %get-tuple-element.50), channel_id=1, source_target_pairs={{4,8},{8,4},{12,16},{16,12},{20,24},{24,20},{5,9},{9,5},{13,17},{1... | collective-permute-start | bytes 98312 | tf_op jit(solution)/shard_map/ppermute | solution.py:25
  35.7 14.8 %collective-permute-start.6 = (f32[8,1024]{1,0:T(8,128)}, f32[8,1024]{1,0:T(8,128)}, u32[]{:S(2)}, u32[]{:S(2)}) collective-permute-start(f32[8,1024]{1,0:T(8,128)} %get-tuple-element.51), channel_id=1, source_target_pairs={{0,1},{1,0},{2,3},{3,2},{4,5},{5,4},{6,7},{7,6},{8,9},{9,8},{10,11... | collective-permute-start | bytes 98312 | tf_op jit(solution)/shard_map/ppermute | solution.py:25
  36.7 13.8 %collective-permute-start.7 = (f32[8,1024]{1,0:T(8,128)}, f32[8,1024]{1,0:T(8,128)}, u32[]{:S(2)}, u32[]{:S(2)}) collective-permute-start(f32[8,1024]{1,0:T(8,128)} %get-tuple-element.52), channel_id=1, source_target_pairs={{1,2},{2,1},{5,6},{6,5},{9,10},{10,9},{13,14},{14,13},{17,18},{18,... | collective-permute-start | bytes 98312 | tf_op jit(solution)/shard_map/ppermute | solution.py:25
  39.7 10.8 %all-to-all-start.1 = ((f32[32,1,128]{2,1,0:T(1,128)}), f32[32,1,128]{2,1,0:T(1,128)}, u32[]{:S(2)}, u32[]{:S(2)}) async-start(f32[32,1,128]{2,1,0:T(1,128)} %bitcast.7), calls=%async_computation.1 | async-start | bytes 32768 | tf_op jit(solution)/shard_map/all_to_all | solution.py:29
  55.6 11.2 %collective-permute-start.8 = (f32[4,1024]{1,0:T(4,128)S(1)}, f32[4,1024]{1,0:T(4,128)S(1)}, u32[]{:S(2)}, u32[]{:S(2)}) collective-permute-start(f32[4,1024]{1,0:T(4,128)S(1)} %get-tuple-element.63), channel_id=1, source_target_pairs={{0,4},{4,0},{8,12},{12,8},{16,20},{20,16},{24,28},{28,24},{1,5},{5... | collective-permute-start | bytes 49160 | tf_op jit(solution)/shard_map/ppermute | solution.py:25
  55.8 11.0 %collective-permute-start.9 = (f32[4,1024]{1,0:T(4,128)S(1)}, f32[4,1024]{1,0:T(4,128)S(1)}, u32[]{:S(2)}, u32[]{:S(2)}) collective-permute-start(f32[4,1024]{1,0:T(4,128)S(1)} %get-tuple-element.64), channel_id=1, source_target_pairs={{4,8},{8,4},{12,16},{16,12},{20,24},{24,20},{5,9},{9,5},{13,17},{1... | collective-permute-start | bytes 49160 | tf_op jit(solution)/shard_map/ppermute | solution.py:25
  59.9 7.0 %collective-permute-start.10 = (f32[4,1024]{1,0:T(4,128)S(1)}, f32[4,1024]{1,0:T(4,128)S(1)}, u32[]{:S(2)}, u32[]{:S(2)}) collective-permute-start(f32[4,1024]{1,0:T(4,128)S(1)} %get-tuple-element.65), channel_id=1, source_target_pairs={{0,1},{1,0},{2,3},{3,2},{4,5},{5,4},{6,7},{7,6},{8,9},{9,8},{10,11... | collective-permute-start | bytes 49160 | tf_op jit(solution)/shard_map/ppermute | solution.py:25
  60.9 6.0 %collective-permute-start.11 = (f32[4,1024]{1,0:T(4,128)S(1)}, f32[4,1024]{1,0:T(4,128)S(1)}, u32[]{:S(2)}, u32[]{:S(2)}) collective-permute-start(f32[4,1024]{1,0:T(4,128)S(1)} %get-tuple-element.66), channel_id=1, source_target_pairs={{1,2},{2,1},{5,6},{6,5},{9,10},{10,9},{13,14},{14,13},{17,18},{18,... | collective-permute-start | bytes 49160 | tf_op jit(solution)/shard_map/ppermute | solution.py:25

commit v4 on v3

--- a/solution.py
+++ b/solution.py
@@ -284,15 +284,20 @@
     return lax.axis_index("gx") % 2 == 0, lax.axis_index("gy") % 2 == 0
 
 
-def slots(outs, block):
+def write_blocks(outs, kept, rows):
     even_x, even_y = even_sides()
-    wanted = (
-        jnp.where(even_x, 1, 0),
-        jnp.where(even_x, 0, 1),
-        jnp.where(even_y, 3, 2),
-        jnp.where(even_y, 2, 3),
-    )
-    return [(ref, block == want) for ref, want in zip(outs, wanted)]
+    count = outs[0].shape[1]
+
+    def block(k):
+        return kept[rows, k * count : (k + 1) * count]
+
+    for out, even, at_even, at_odd in (
+        (outs[0], even_x, 1, 0),
+        (outs[1], even_x, 0, 1),
+        (outs[2], even_y, 3, 2),
+        (outs[3], even_y, 2, 3),
+    ):
+        out[rows, :] = jnp.where(even, block(at_even), block(at_odd))
 
 
 def write_ghosts(outs, picks, g):
@@ -345,7 +350,7 @@
 
 def start_kernel(
     bus_ref, level_ref, s_ref, list_ref, from_ref, kkt_ref, act_ref, lim_ref, lev_ref,
-    xe_ref, xo_ref, ye_ref, yo_ref, z_ref, hv_ref, hv_own_ref, hv_pen_ref, work_ref, turn_ref,
+    xe_ref, xo_ref, ye_ref, yo_ref, z_ref, hv_ref, hv_own_ref, hv_pen_ref, work_ref, turn_ref, kept_ref,
 ):
     outs = (xe_ref, xo_ref, ye_ref, yo_ref)
     upper = upper_half()
@@ -360,7 +365,6 @@
     write_hv(hv_ref, values, hv_pen_ref[...])
     groups = s_ref.shape[1] // (GROUP * BLK)
     buses, cross = (GROUP * BLK, from_ref.shape[1] // groups)
-    per_list = xe_ref.shape[1] // cross
 
     @pl.loop(0, groups, unroll=2)
     def _(g):
@@ -370,7 +374,6 @@
         z_ref[0:8, lanes(g * LANES)] = picks[0]
         z_ref[8:16, lanes(g * LANES)] = picks[1]
         write_ghosts(outs, picks, g)
-        found = []
         for t in range(cross // LANES):
             cols = lanes(g * cross + t * LANES)
             index = spread8(from_ref[0:1, cols] - (base + t * PAIR))
@@ -382,17 +385,13 @@
             block = [
                 jnp.where(fixed, 0.0, turn_ref[pl.ds(64 * t + 4 + j, 8, stride=8), :])[4:] for j in range(4)
             ]
-            found.append((part[4:], block, 0.25 * lev_ref[0:1, cols].astype(F32)))
-        for ref, here in slots(outs, g // per_list):
-
-            @pl.when(here)
-            def _():
-                for t, (part, block, penalty) in enumerate(found):
-                    spot = lanes((g % per_list) * cross + t * LANES)
-                    ref[4:8, spot] = part
-                    for j in range(4):
-                        ref[8 + 4 * j : 12 + 4 * j, spot] = block[j]
-                    ref[24:25, spot] = penalty
+            kept_ref[0:8, cols] = part
+            for j in range(4):
+                kept_ref[8 + 4 * j : 12 + 4 * j, cols] = block[j]
+            kept_ref[24:25, cols] = 0.25 * lev_ref[0:1, cols].astype(F32)
+
+    for rows in (slice(4, 8), slice(8, 24), slice(24, 25)):
+        write_blocks(outs, kept_ref, rows)
 
 
 def far_hv(first, bus_ref, partner_ref, all_ref, own, penalty, scaled, sum_ref, weight_ref, work_ref, other_ref):
@@ -442,7 +441,7 @@
             bus_ref, partner_ref, all_ref, own_ref, hv_pen_ref, xe, xo, ye, yo, acc_ref, weight_in_ref,
             s_ref, list_ref, from_ref, kkt_ref, act_ref, lim_ref, lev_ref, z_ref, target_ref, prior_ref,
             new_ref, inv_ref, oxe, oxo, oye, oyo, yc_ref, ym_ref, zn_ref, hv_ref, hv_scaled_ref, hv_own_ref,
-            sum_ref, hv_weight_ref, work_ref, other_ref,
+            sum_ref, hv_weight_ref, work_ref, other_ref, kept_ref,
         ) = refs
         now = (xe, xo, ye, yo)
         scaled = None
@@ -474,7 +473,7 @@
         work_ref, other_ref,
     )
 
-    @pl.loop(0, groups, unroll=2)
+    @pl.loop(0, groups, unroll=4)
     def _(g):
         base = g * buses
         tables = [doubled(s_ref[:, lanes(base + h * LANES)]) for h in range(count)]
@@ -571,21 +570,16 @@
         if first:
             zn_ref[0:8, spot] = picks[0]
             zn_ref[8:16, spot] = picks[1]
-            parts = []
             for t in range(cross // LANES):
                 cols = lanes(g * cross + t * LANES)
                 near = from_ref[0:1, cols] - (base + t * PAIR)
                 ends = pick(fresh[4 * t : 4 * t + 4], spread8(near), range(4))
                 target = 2.0 * ends - outputs[t]
                 part = product(kkt_ref, cols, jnp.where(upper, target, 0.0))
-                parts.append(jnp.where(act_ref[:, cols] == 1, lim_ref[:, cols], part)[4:])
-            for ref, here in slots(outs, g // per_list):
-
-                @pl.when(here)
-                def _():
-                    for t, part in enumerate(parts):
-                        ref[4:8, lanes((g % per_list) * cross + t * LANES)] = part
-
+                kept_ref[:, cols] = jnp.where(act_ref[:, cols] == 1, lim_ref[:, cols], part)
+
+    if first:
+        write_blocks(outs, kept_ref, slice(4, 8))
     reached = hv_states(new_ref, bus_ref, work_ref)
     left_over = hv_y - reached
     penalty = hv_pen_ref[...]
@@ -604,7 +598,7 @@
     branches = index_ref.shape[1] // groups
     per_pair = branches // (GROUP // 2)
 
-    @pl.loop(0, groups, unroll=2)
+    @pl.loop(0, groups, unroll=4)
     def _(g):
         for p in range(GROUP // 2):
             base = g * GROUP * BLK + p * PAIR
@@ -622,7 +616,7 @@
     cross = from_ref.shape[1] // groups
     per_list = xe.shape[1] // cross
 
-    @pl.loop(0, groups, unroll=2)
+    @pl.loop(0, groups, unroll=8)
     def _(g):
         for t in range(cross // LANES):
             base = g * GROUP * BLK + t * PAIR
@@ -707,6 +701,7 @@
         scratch_shapes=[
             pltpu.VMEM(hv_block, F32),
             pltpu.VMEM((64 * (GROUP // 2), LANES), F32),
+            pltpu.VMEM((STATIC_ROWS, cross), F32),
         ],
         cost_estimate=cost(10**6, 4 * 10**6),
         **common,
@@ -759,7 +754,7 @@
         + [message] * 4
         + [part(8, cross), held_spec, held_spec]
         + [hv_all_spec, hv_spec, hv_spec],
-        scratch_shapes=[pltpu.VMEM((1, bus_count), F32)] * 2 + [pltpu.VMEM(hv_block, F32)] * 2,
+        scratch_shapes=[pltpu.VMEM((1, bus_count), F32)] * 2 + [pltpu.VMEM(hv_block, F32)] * 2 + [pltpu.VMEM((8, cross), F32)],
         cost_estimate=cost(10**7, 5 * 10**6),
         **common,
     )(

time: 69.3 us -> 65.4 us (0.944)
  Pallas kernels: 34.3 us -> 30.5 us
    pallas_call x1, Pallas kernels: 7.46 us -> 5.11 us  [on_device(): pl.pallas_call(functools.partial(outer_kernel, True), name='outer_first',...]
  transfers between devices with their start and end apart: 14 -> 14, of which waited for: 0 -> 0; matrix products, arithmetic and copies ran while one was open for 0% -> 0% of each run, Pallas kernels for 23% -> 24%
where the time goes in v4:
time: 65.4 us; the launch traced here: 65 us
  starting transfers between devices  33.7 us (52%)
  Pallas kernels  30.5 us (47%)
  between operations  0.81 us (1%)
    ppermute x12, starting transfers between devices, swapped(): return lax.ppermute(value, axis, moves)  25.2 us
    all_to_all x2, starting transfers between devices, to_all(): lax.all_to_all(rows, ('gx', 'gy'), split_axis=0, concat_axis=0, tiled=True)  8.46 us
    pallas_call x1, Pallas kernels, on_device(): pl.pallas_call(fetching(functools.partial(inner_kernel, False), {0: 0, 1:...  6.55 us
    pallas_call x1, Pallas kernels, on_device(): pl.pallas_call(fetching(functools.partial(inner_kernel, True), {0: 0, 1:...  6.44 us
    pallas_call x1, Pallas kernels, on_device(): pl.pallas_call(functools.partial(outer_kernel, True), name='outer_first',...  5.11 us
    pallas_call x1, Pallas kernels, on_device(): pl.pallas_call(functools.partial(outer_kernel, False), name='outer_second...  4.55 us
    pallas_call x1, Pallas kernels, on_device(): pl.pallas_call(start_kernel, name='first_messages', in_specs=[scalars(),...  3.27 us
    pallas_call x1, Pallas kernels, on_device(): pl.pallas_call(inner_dual_kernel, name='inner_duals', in_specs=[state_spe...  2.83 us
  transfers between devices with their start and end apart: 14, of which 0 were waited for; matrix products, arithmetic and copies ran while one was open for 0% of the time, Pallas kernels for 24%

profile of v4, /device:TPU:5, one launch (start us, length us, event | category | flops | bytes accessed | tf_op | source)
XLA Modules:
  0.0 65.0 jit_solution(6923318108466283350)
XLA Ops:
  0.6 3.3 %first_messages.1 = (f32[25,1024]{1,0:T(8,128)S(1)}, f32[25,1024]{1,0:T(8,128)S(1)}, f32[25,1024]{1,0:T(8,128)S(1)}, f32[25,1024]{1,0:T(8,128)S(1)}, f32[16,1024...) custom-call(s32[32]{0:T(128)} %refs_0_.5, s32[32]{0:T(128)} %level_ref.1, ...), custom_call_target="tpu_custom_call" | custom-call | flops 1000000 | bytes 4000000 | tf_op jit(solution)/shard_map/first_messages/pallas_call | solution.py:694
  3.9 0.0 collective-permute-start
  3.9 4.4 %collective-permute-start.1 = (f32[25,1024]{1,0:T(8,128)S(1)}, f32[25,1024]{1,0:T(8,128)S(1)}, u32[]{:S(2)}, u32[]{:S(2)}) collective-permute-start(f32[25,1024]{1,0:T(8,128)S(1)} %get-tuple-element.40), channel_id=1, source_target_pairs={{4,8},{8,4},{12,16},{16,12},{20,24},{24,20},{5,9},{9,5},{13,17},{1... | collective-permute-start | bytes 307208 | tf_op jit(solution)/shard_map/ppermute | solution.py:25
  8.3 1.3 %collective-permute-start.2 = (f32[25,1024]{1,0:T(8,128)S(1)}, f32[25,1024]{1,0:T(8,128)S(1)}, u32[]{:S(2)}, u32[]{:S(2)}) collective-permute-start(f32[25,1024]{1,0:T(8,128)S(1)} %get-tuple-element.41), channel_id=1, source_target_pairs={{0,1},{1,0},{2,3},{3,2},{4,5},{5,4},{6,7},{7,6},{8,9},{9,8},{10,11... | collective-permute-start | bytes 307208 | tf_op jit(solution)/shard_map/ppermute | solution.py:25
  9.6 3.0 %collective-permute-start.3 = (f32[25,1024]{1,0:T(8,128)S(1)}, f32[25,1024]{1,0:T(8,128)S(1)}, u32[]{:S(2)}, u32[]{:S(2)}) collective-permute-start(f32[25,1024]{1,0:T(8,128)S(1)} %get-tuple-element.42), channel_id=1, source_target_pairs={{1,2},{2,1},{5,6},{6,5},{9,10},{10,9},{13,14},{14,13},{17,18},{18,... | collective-permute-start | bytes 307208 | tf_op jit(solution)/shard_map/ppermute | solution.py:25
  12.6 4.3 %all-to-all-start = ((f32[32,1,128]{2,1,0:T(1,128)}), f32[32,1,128]{2,1,0:T(1,128)S(1)}, u32[]{:S(2)}, u32[]{:S(2)}) async-start(f32[32,1,128]{2,1,0:T(1,128)} %bitcast.4), calls=%async_computation | async-start | bytes 32768 | tf_op jit(solution)/shard_map/all_to_all | solution.py:29
  16.9 6.4 %inner_first.1 = (f32[8,20480]{1,0:T(8,128)S(1)}, f32[8,16384]{1,0:T(8,128)S(1)}, f32[1,16384]{1,0:T(1,128)S(1)}) custom-call(f32[4,16384]{1,0:T(4,128)} %refs_11_.1, s32[2,20480]{1,0:T(2,128)} %index_ref.1, s32[1,24576]{1,0:T(1,128)} %bitcast.19, f32[64,24576]{1,0:T(8,128)} %bitcast.14, s32[8,24576]{1,0:T(8,128)} %refs_20_.3, f32[8,24576]{1,0:T(8,128)} %refs_21_.1), custom_call_target="tpu_custom_call" | custom-call | flops 100000000 | bytes 10000000 | tf_op jit(solution)/shard_map/inner_first/pallas_call | solution.py:729
  23.3 0.0 all-to-all-done
  23.3 0.0 collective-permute-done.refs_5_.refs_6_
  23.4 0.0 collective-permute-done.1.refs_6_.refs_7_
  23.4 0.0 collective-permute-done.2.refs_7_.refs_8_
  23.4 0.0 collective-permute-done.3.refs_8_.refs_9_
  23.4 5.1 %outer_first.1 = (f32[8,16384]{1,0:T(8,128)S(1)}, f32[8,16384]{1,0:T(8,128)S(1)}, f32[8,1024]{1,0:T(8,128)}, f32[8,1024]{1,0:T(8,128)}, f32[8,1024]{1,0:T(8,128)...) custom-call(s32[32]{0:T(128)} %refs_0_.5, ...), custom_call_target="tpu_custom_call" | custom-call | flops 10000000 | bytes 5000000 | tf_op jit(solution)/shard_map/outer_first/pallas_call | solution.py:740
  28.5 0.3 collective-permute-start.4
  28.8 4.0 %collective-permute-start.5 = (f32[8,1024]{1,0:T(8,128)}, f32[8,1024]{1,0:T(8,128)}, u32[]{:S(2)}, u32[]{:S(2)}) collective-permute-start(f32[8,1024]{1,0:T(8,128)} %get-tuple-element.50), channel_id=1, source_target_pairs={{4,8},{8,4},{12,16},{16,12},{20,24},{24,20},{5,9},{9,5},{13,17},{1... | collective-permute-start | bytes 98312 | tf_op jit(solution)/shard_map/ppermute | solution.py:25
  32.8 1.0 %collective-permute-start.6 = (f32[8,1024]{1,0:T(8,128)}, f32[8,1024]{1,0:T(8,128)}, u32[]{:S(2)}, u32[]{:S(2)}) collective-permute-start(f32[8,1024]{1,0:T(8,128)} %get-tuple-element.51), channel_id=1, source_target_pairs={{0,1},{1,0},{2,3},{3,2},{4,5},{5,4},{6,7},{7,6},{8,9},{9,8},{10,11... | collective-permute-start | bytes 98312 | tf_op jit(solution)/shard_map/ppermute | solution.py:25
  33.8 3.0 %collective-permute-start.7 = (f32[8,1024]{1,0:T(8,128)}, f32[8,1024]{1,0:T(8,128)}, u32[]{:S(2)}, u32[]{:S(2)}) collective-permute-start(f32[8,1024]{1,0:T(8,128)} %get-tuple-element.52), channel_id=1, source_target_pairs={{1,2},{2,1},{5,6},{6,5},{9,10},{10,9},{13,14},{14,13},{17,18},{18,... | collective-permute-start | bytes 98312 | tf_op jit(solution)/shard_map/ppermute | solution.py:25
  36.8 4.2 %all-to-all-start.1 = ((f32[32,1,128]{2,1,0:T(1,128)}), f32[32,1,128]{2,1,0:T(1,128)}, u32[]{:S(2)}, u32[]{:S(2)}) async-start(f32[32,1,128]{2,1,0:T(1,128)} %bitcast.7), calls=%async_computation.1 | async-start | bytes 32768 | tf_op jit(solution)/shard_map/all_to_all | solution.py:29
  41.0 6.5 %inner_second.1 = (f32[8,20480]{1,0:T(8,128)S(1)}, f32[8,16384]{1,0:T(8,128)S(1)}) custom-call(f32[8,16384]{1,0:T(8,128)S(1)} %get-tuple-element.53.refs_0_.refs_16_, s32[2,20480]{1,0:T(2,128)} %index_ref.1, s32[1,24576]{1,0:T(1,128)} %bitcast.21, f32[64,24576]{1,0:T(8,128)} %bitcast.16, s32[8,24576]{1,0:T(8,128)} %refs_20_.3, f32[8,24576]{1,0:T(8,128)} %refs_21_.1, ...), custom_call_target="tpu_custom_call" | custom-call | flops 100000000 | bytes 10000000 | tf_op jit(solution)/shard_map/inner_second/pallas_call | solution.py:769
  47.5 0.0 all-to-all-done.1
  47.5 0.0 collective-permute-done.4.refs_10_
  47.6 0.0 collective-permute-done.5.refs_11_
  47.6 0.0 collective-permute-done.6.refs_12_
  47.6 0.0 collective-permute-done.7.refs_13_
  47.6 4.5 %outer_second.1 = (f32[8,16384]{1,0:T(8,128)S(1)}, f32[4,16384]{1,0:T(4,128)}, f32[4,1024]{1,0:T(4,128)S(1)}, f32[4,1024]{1,0:T(4,128)S(1)}, f32[4,1024]{1,0:T(4...) custom-call(s32[32]{0:T(128)} %refs_0_.5, s32[32]{0:T(128)} %refs_1_.7, ...), custom_call_target="tpu_custom_call" | custom-call | flops 10000000 | bytes 5000000 | tf_op jit(solution)/shard_map/outer_second/pallas_call | solution.py:780
  52.1 0.2 collective-permute-start.8
  52.3 4.1 %collective-permute-start.9 = (f32[4,1024]{1,0:T(4,128)S(1)}, f32[4,1024]{1,0:T(4,128)S(1)}, u32[]{:S(2)}, u32[]{:S(2)}) collective-permute-start(f32[4,1024]{1,0:T(4,128)S(1)} %get-tuple-element.64), channel_id=1, source_target_pairs={{4,8},{8,4},{12,16},{16,12},{20,24},{24,20},{5,9},{9,5},{13,17},{1... | collective-permute-start | bytes 49160 | tf_op jit(solution)/shard_map/ppermute | solution.py:25
  56.4 1.0 %collective-permute-start.10 = (f32[4,1024]{1,0:T(4,128)S(1)}, f32[4,1024]{1,0:T(4,128)S(1)}, u32[]{:S(2)}, u32[]{:S(2)}) collective-permute-start(f32[4,1024]{1,0:T(4,128)S(1)} %get-tuple-element.65), channel_id=1, source_target_pairs={{0,1},{1,0},{2,3},{3,2},{4,5},{5,4},{6,7},{7,6},{8,9},{9,8},{10,11... | collective-permute-start | bytes 49160 | tf_op jit(solution)/shard_map/ppermute | solution.py:25
  57.4 3.0 %collective-permute-start.11 = (f32[4,1024]{1,0:T(4,128)S(1)}, f32[4,1024]{1,0:T(4,128)S(1)}, u32[]{:S(2)}, u32[]{:S(2)}) collective-permute-start(f32[4,1024]{1,0:T(4,128)S(1)} %get-tuple-element.66), channel_id=1, source_target_pairs={{1,2},{2,1},{5,6},{6,5},{9,10},{10,9},{13,14},{14,13},{17,18},{18,... | collective-permute-start | bytes 49160 | tf_op jit(solution)/shard_map/ppermute | solution.py:25
  60.4 2.8 %inner_duals.1.dual_in_ref = f32[8,24576]{1,0:T(8,128)} custom-call(f32[8,16384]{1,0:T(8,128)S(1)} %get-tuple-element.61.s_ref, s32[2,20480]{1,0:T(2,128)} %index_ref.1, f32[8,20480]{1,0:T(8,128)S(1)} %get-tuple-element.62.y_ref, s32[1,24576]{1,0:T(1,128)} %bitcast.23), custom_call_target="tpu_custom_call" | custom-call | flops 10000000 | bytes 3000000 | tf_op jit(solution)/shard_map/inner_duals/pallas_call | solution.py:804
  63.2 0.0 collective-permute-done.8.xe
  63.2 0.0 collective-permute-done.9.xo
  63.2 0.0 collective-permute-done.10.ye
  63.2 0.0 collective-permute-done.11.yo
  63.2 1.7 %outer_duals.1 = f32[8,24576]{1,0:T(8,128)} custom-call(f32[8,24576]{1,0:T(8,128)} %inner_duals.1.dual_in_ref, f32[4,1024]{1,0:T(4,128)S(1)} %collective-permute-done.8.xe, f32[4,1024]{1,0:T(4,128)S(1)} %collective-permute-done.9.xo, f32[4,1024]{1,0:T(4,128)S(1)} %collective-permute-done.10.ye, ...), custom_call_target="tpu_custom_call", output_to_operand_aliasing={{}: (0, {})} | custom-call | flops 1000000 | bytes 1000000 | tf_op jit(solution)/shard_map/outer_duals/pallas_call | solution.py:813
Async XLA Ops:
  3.9 19.4 %collective-permute-start = (f32[25,1024]{1,0:T(8,128)S(1)}, f32[25,1024]{1,0:T(8,128)S(1)}, u32[]{:S(2)}, u32[]{:S(2)}) collective-permute-start(f32[25,1024]{1,0:T(8,128)S(1)} %get-tuple-element.39), channel_id=1, source_target_pairs={{0,4},{4,0},{8,12},{12,8},{16,20},{20,16},{24,28},{28,24},{1,5},{5... | collective-permute-start | bytes 307208 | tf_op jit(solution)/shard_map/ppermute | solution.py:25
  3.9 19.4 %collective-permute-start.1 = (f32[25,1024]{1,0:T(8,128)S(1)}, f32[25,1024]{1,0:T(8,128)S(1)}, u32[]{:S(2)}, u32[]{:S(2)}) collective-permute-start(f32[25,1024]{1,0:T(8,128)S(1)} %get-tuple-element.40), channel_id=1, source_target_pairs={{4,8},{8,4},{12,16},{16,12},{20,24},{24,20},{5,9},{9,5},{13,17},{1... | collective-permute-start | bytes 307208 | tf_op jit(solution)/shard_map/ppermute | solution.py:25
  8.3 15.1 %collective-permute-start.2 = (f32[25,1024]{1,0:T(8,128)S(1)}, f32[25,1024]{1,0:T(8,128)S(1)}, u32[]{:S(2)}, u32[]{:S(2)}) collective-permute-start(f32[25,1024]{1,0:T(8,128)S(1)} %get-tuple-element.41), channel_id=1, source_target_pairs={{0,1},{1,0},{2,3},{3,2},{4,5},{5,4},{6,7},{7,6},{8,9},{9,8},{10,11... | collective-permute-start | bytes 307208 | tf_op jit(solution)/shard_map/ppermute | solution.py:25
  9.6 13.8 %collective-permute-start.3 = (f32[25,1024]{1,0:T(8,128)S(1)}, f32[25,1024]{1,0:T(8,128)S(1)}, u32[]{:S(2)}, u32[]{:S(2)}) collective-permute-start(f32[25,1024]{1,0:T(8,128)S(1)} %get-tuple-element.42), channel_id=1, source_target_pairs={{1,2},{2,1},{5,6},{6,5},{9,10},{10,9},{13,14},{14,13},{17,18},{18,... | collective-permute-start | bytes 307208 | tf_op jit(solution)/shard_map/ppermute | solution.py:25
  12.6 10.7 %all-to-all-start = ((f32[32,1,128]{2,1,0:T(1,128)}), f32[32,1,128]{2,1,0:T(1,128)S(1)}, u32[]{:S(2)}, u32[]{:S(2)}) async-start(f32[32,1,128]{2,1,0:T(1,128)} %bitcast.4), calls=%async_computation | async-start | bytes 32768 | tf_op jit(solution)/shard_map/all_to_all | solution.py:29
  28.5 19.1 %collective-permute-start.4 = (f32[8,1024]{1,0:T(8,128)}, f32[8,1024]{1,0:T(8,128)}, u32[]{:S(2)}, u32[]{:S(2)}) collective-permute-start(f32[8,1024]{1,0:T(8,128)} %get-tuple-element.49), channel_id=1, source_target_pairs={{0,4},{4,0},{8,12},{12,8},{16,20},{20,16},{24,28},{28,24},{1,5},{5... | collective-permute-start | bytes 98312 | tf_op jit(solution)/shard_map/ppermute | solution.py:25
  28.8 18.8 %collective-permute-start.5 = (f32[8,1024]{1,0:T(8,128)}, f32[8,1024]{1,0:T(8,128)}, u32[]{:S(2)}, u32[]{:S(2)}) collective-permute-start(f32[8,1024]{1,0:T(8,128)} %get-tuple-element.50), channel_id=1, source_target_pairs={{4,8},{8,4},{12,16},{16,12},{20,24},{24,20},{5,9},{9,5},{13,17},{1... | collective-permute-start | bytes 98312 | tf_op jit(solution)/shard_map/ppermute | solution.py:25
  32.8 14.8 %collective-permute-start.6 = (f32[8,1024]{1,0:T(8,128)}, f32[8,1024]{1,0:T(8,128)}, u32[]{:S(2)}, u32[]{:S(2)}) collective-permute-start(f32[8,1024]{1,0:T(8,128)} %get-tuple-element.51), channel_id=1, source_target_pairs={{0,1},{1,0},{2,3},{3,2},{4,5},{5,4},{6,7},{7,6},{8,9},{9,8},{10,11... | collective-permute-start | bytes 98312 | tf_op jit(solution)/shard_map/ppermute | solution.py:25
  33.8 13.8 %collective-permute-start.7 = (f32[8,1024]{1,0:T(8,128)}, f32[8,1024]{1,0:T(8,128)}, u32[]{:S(2)}, u32[]{:S(2)}) collective-permute-start(f32[8,1024]{1,0:T(8,128)} %get-tuple-element.52), channel_id=1, source_target_pairs={{1,2},{2,1},{5,6},{6,5},{9,10},{10,9},{13,14},{14,13},{17,18},{18,... | collective-permute-start | bytes 98312 | tf_op jit(solution)/shard_map/ppermute | solution.py:25
  36.8 10.8 %all-to-all-start.1 = ((f32[32,1,128]{2,1,0:T(1,128)}), f32[32,1,128]{2,1,0:T(1,128)}, u32[]{:S(2)}, u32[]{:S(2)}) async-start(f32[32,1,128]{2,1,0:T(1,128)} %bitcast.7), calls=%async_computation.1 | async-start | bytes 32768 | tf_op jit(solution)/shard_map/all_to_all | solution.py:29
  52.1 11.1 %collective-permute-start.8 = (f32[4,1024]{1,0:T(4,128)S(1)}, f32[4,1024]{1,0:T(4,128)S(1)}, u32[]{:S(2)}, u32[]{:S(2)}) collective-permute-start(f32[4,1024]{1,0:T(4,128)S(1)} %get-tuple-element.63), channel_id=1, source_target_pairs={{0,4},{4,0},{8,12},{12,8},{16,20},{20,16},{24,28},{28,24},{1,5},{5... | collective-permute-start | bytes 49160 | tf_op jit(solution)/shard_map/ppermute | solution.py:25
  52.3 10.9 %collective-permute-start.9 = (f32[4,1024]{1,0:T(4,128)S(1)}, f32[4,1024]{1,0:T(4,128)S(1)}, u32[]{:S(2)}, u32[]{:S(2)}) collective-permute-start(f32[4,1024]{1,0:T(4,128)S(1)} %get-tuple-element.64), channel_id=1, source_target_pairs={{4,8},{8,4},{12,16},{16,12},{20,24},{24,20},{5,9},{9,5},{13,17},{1... | collective-permute-start | bytes 49160 | tf_op jit(solution)/shard_map/ppermute | solution.py:25
  56.4 6.8 %collective-permute-start.10 = (f32[4,1024]{1,0:T(4,128)S(1)}, f32[4,1024]{1,0:T(4,128)S(1)}, u32[]{:S(2)}, u32[]{:S(2)}) collective-permute-start(f32[4,1024]{1,0:T(4,128)S(1)} %get-tuple-element.65), channel_id=1, source_target_pairs={{0,1},{1,0},{2,3},{3,2},{4,5},{5,4},{6,7},{7,6},{8,9},{9,8},{10,11... | collective-permute-start | bytes 49160 | tf_op jit(solution)/shard_map/ppermute | solution.py:25
  57.4 5.8 %collective-permute-start.11 = (f32[4,1024]{1,0:T(4,128)S(1)}, f32[4,1024]{1,0:T(4,128)S(1)}, u32[]{:S(2)}, u32[]{:S(2)}) collective-permute-start(f32[4,1024]{1,0:T(4,128)S(1)} %get-tuple-element.66), channel_id=1, source_target_pairs={{1,2},{2,1},{5,6},{6,5},{9,10},{10,9},{13,14},{14,13},{17,18},{18,... | collective-permute-start | bytes 49160 | tf_op jit(solution)/shard_map/ppermute | solution.py:25

commit v5 on v4

--- a/solution.py
+++ b/solution.py
@@ -330,7 +330,7 @@
         work_ref[pl.ds(t, 1), :] = jnp.where(lane == (bus & (LANES - 1)), row, 0.0)
         return carry
 
-    lax.fori_loop(0, work_ref.shape[0], body, 0, unroll=8)
+    lax.fori_loop(0, work_ref.shape[0], body, 0, unroll=32)
     return jnp.broadcast_to(jnp.sum(work_ref[...], axis=1, keepdims=True), work_ref.shape)
 
 
@@ -361,12 +361,12 @@
         hv_pen_ref[pl.ds(t, 1), :] = jnp.full((1, LANES), level_ref[t], jnp.int32).astype(F32) * 0.25
         return carry
 
-    lax.fori_loop(0, hv_pen_ref.shape[0], body, 0, unroll=8)
+    lax.fori_loop(0, hv_pen_ref.shape[0], body, 0, unroll=32)
     write_hv(hv_ref, values, hv_pen_ref[...])
     groups = s_ref.shape[1] // (GROUP * BLK)
     buses, cross = (GROUP * BLK, from_ref.shape[1] // groups)
 
-    @pl.loop(0, groups, unroll=2)
+    @pl.loop(0, groups, unroll=4)
     def _(g):
         base = g * buses
         tables = [doubled(s_ref[:, lanes(base + h * LANES)]) for h in range(buses // LANES)]
@@ -411,7 +411,7 @@
         other_ref[pl.ds(t, 1), :] = narrow(jnp.where(wide == place + count, row, 0.0))
         return carry
 
-    lax.fori_loop(0, count, fetch, 0, unroll=8)
+    lax.fori_loop(0, count, fetch, 0, unroll=32)
     far_value = jnp.sum(work_ref[...], axis=1, keepdims=True)
     far_penalty = jnp.sum(other_ref[...], axis=1, keepdims=True)
     flow = (penalty * own - far_penalty * far_value) / (penalty + far_penalty)
@@ -431,7 +431,7 @@
             weight_ref[0:1, spot] += jnp.where(here, other_ref[pl.ds(t, 1), :], 0.0)
         return carry
 
-    lax.fori_loop(0, count, place_terms, 0, unroll=8)
+    lax.fori_loop(0, count, place_terms, 0, unroll=32)
     return y
 
 
@@ -473,7 +473,7 @@
         work_ref, other_ref,
     )
 
-    @pl.loop(0, groups, unroll=4)
+    @pl.loop(0, groups, unroll=8)
     def _(g):
         base = g * buses
         tables = [doubled(s_ref[:, lanes(base + h * LANES)]) for h in range(count)]

time: 65.4 us -> 63.9 us (0.977)
  Pallas kernels: 30.5 us -> 28.9 us
    pallas_call x1, Pallas kernels: 4.55 us -> 3.83 us  [on_device(): pl.pallas_call(functools.partial(outer_kernel, False), name='outer_second...]
  transfers between devices with their start and end apart: 14 -> 14, of which waited for: 0 -> 0; matrix products, arithmetic and copies ran while one was open for 0% -> 0% of each run, Pallas kernels for 24% -> 25%
where the time goes in v5:
time: 63.9 us; the launch traced here: 63.4 us
  starting transfers between devices  33.7 us (53%)
  Pallas kernels  28.9 us (45%)
  between operations  0.81 us (1%)
    ppermute x12, starting transfers between devices, swapped(): return lax.ppermute(value, axis, moves)  25.2 us
    all_to_all x2, starting transfers between devices, to_all(): lax.all_to_all(rows, ('gx', 'gy'), split_axis=0, concat_axis=0, tiled=True)  8.46 us
    pallas_call x1, Pallas kernels, on_device(): pl.pallas_call(fetching(functools.partial(inner_kernel, False), {0: 0, 1:...  6.54 us
    pallas_call x1, Pallas kernels, on_device(): pl.pallas_call(fetching(functools.partial(inner_kernel, True), {0: 0, 1:...  6.46 us
    pallas_call x1, Pallas kernels, on_device(): pl.pallas_call(functools.partial(outer_kernel, True), name='outer_first',...  4.48 us
    pallas_call x1, Pallas kernels, on_device(): pl.pallas_call(functools.partial(outer_kernel, False), name='outer_second...  3.83 us
    pallas_call x1, Pallas kernels, on_device(): pl.pallas_call(start_kernel, name='first_messages', in_specs=[scalars(),...  3.02 us
    pallas_call x1, Pallas kernels, on_device(): pl.pallas_call(inner_dual_kernel, name='inner_duals', in_specs=[state_spe...  2.83 us
  transfers between devices with their start and end apart: 14, of which 0 were waited for; matrix products, arithmetic and copies ran while one was open for 0% of the time, Pallas kernels for 25%

profile of v5, /device:TPU:5, one launch (start us, length us, event | category | flops | bytes accessed | tf_op | source)
XLA Modules:
  0.0 63.4 jit_solution(6228390010091671383)
XLA Ops:
  0.6 3.0 %first_messages.1 = (f32[25,1024]{1,0:T(8,128)S(1)}, f32[25,1024]{1,0:T(8,128)S(1)}, f32[25,1024]{1,0:T(8,128)S(1)}, f32[25,1024]{1,0:T(8,128)S(1)}, f32[16,1024...) custom-call(s32[32]{0:T(128)} %refs_0_.5, s32[32]{0:T(128)} %level_ref.1, ...), custom_call_target="tpu_custom_call" | custom-call | flops 1000000 | bytes 4000000 | tf_op jit(solution)/shard_map/first_messages/pallas_call | solution.py:694
  3.6 0.0 collective-permute-start
  3.7 4.4 %collective-permute-start.1 = (f32[25,1024]{1,0:T(8,128)S(1)}, f32[25,1024]{1,0:T(8,128)S(1)}, u32[]{:S(2)}, u32[]{:S(2)}) collective-permute-start(f32[25,1024]{1,0:T(8,128)S(1)} %get-tuple-element.40), channel_id=1, source_target_pairs={{4,8},{8,4},{12,16},{16,12},{20,24},{24,20},{5,9},{9,5},{13,17},{1... | collective-permute-start | bytes 307208 | tf_op jit(solution)/shard_map/ppermute | solution.py:25
  8.0 1.3 %collective-permute-start.2 = (f32[25,1024]{1,0:T(8,128)S(1)}, f32[25,1024]{1,0:T(8,128)S(1)}, u32[]{:S(2)}, u32[]{:S(2)}) collective-permute-start(f32[25,1024]{1,0:T(8,128)S(1)} %get-tuple-element.41), channel_id=1, source_target_pairs={{0,1},{1,0},{2,3},{3,2},{4,5},{5,4},{6,7},{7,6},{8,9},{9,8},{10,11... | collective-permute-start | bytes 307208 | tf_op jit(solution)/shard_map/ppermute | solution.py:25
  9.3 3.0 %collective-permute-start.3 = (f32[25,1024]{1,0:T(8,128)S(1)}, f32[25,1024]{1,0:T(8,128)S(1)}, u32[]{:S(2)}, u32[]{:S(2)}) collective-permute-start(f32[25,1024]{1,0:T(8,128)S(1)} %get-tuple-element.42), channel_id=1, source_target_pairs={{1,2},{2,1},{5,6},{6,5},{9,10},{10,9},{13,14},{14,13},{17,18},{18,... | collective-permute-start | bytes 307208 | tf_op jit(solution)/shard_map/ppermute | solution.py:25
  12.4 4.3 %all-to-all-start = ((f32[32,1,128]{2,1,0:T(1,128)}), f32[32,1,128]{2,1,0:T(1,128)S(1)}, u32[]{:S(2)}, u32[]{:S(2)}) async-start(f32[32,1,128]{2,1,0:T(1,128)} %bitcast.4), calls=%async_computation | async-start | bytes 32768 | tf_op jit(solution)/shard_map/all_to_all | solution.py:29
  16.6 6.5 %inner_first.1 = (f32[8,20480]{1,0:T(8,128)S(1)}, f32[8,16384]{1,0:T(8,128)S(1)}, f32[1,16384]{1,0:T(1,128)S(1)}) custom-call(f32[4,16384]{1,0:T(4,128)} %refs_11_.1, s32[2,20480]{1,0:T(2,128)} %index_ref.1, s32[1,24576]{1,0:T(1,128)} %bitcast.19, f32[64,24576]{1,0:T(8,128)} %bitcast.14, s32[8,24576]{1,0:T(8,128)} %refs_20_.3, f32[8,24576]{1,0:T(8,128)} %refs_21_.1), custom_call_target="tpu_custom_call" | custom-call | flops 100000000 | bytes 10000000 | tf_op jit(solution)/shard_map/inner_first/pallas_call | solution.py:729
  23.1 0.0 all-to-all-done
  23.1 0.0 collective-permute-done.refs_5_.refs_6_
  23.1 0.0 collective-permute-done.1.refs_6_.refs_7_
  23.1 0.0 collective-permute-done.2.refs_7_.refs_8_
  23.1 0.0 collective-permute-done.3.refs_8_.refs_9_
  23.1 4.5 %outer_first.1 = (f32[8,16384]{1,0:T(8,128)S(1)}, f32[8,16384]{1,0:T(8,128)S(1)}, f32[8,1024]{1,0:T(8,128)}, f32[8,1024]{1,0:T(8,128)}, f32[8,1024]{1,0:T(8,128)...) custom-call(s32[32]{0:T(128)} %refs_0_.5, ...), custom_call_target="tpu_custom_call" | custom-call | flops 10000000 | bytes 5000000 | tf_op jit(solution)/shard_map/outer_first/pallas_call | solution.py:740
  27.6 0.3 collective-permute-start.4
  28.0 4.0 %collective-permute-start.5 = (f32[8,1024]{1,0:T(8,128)}, f32[8,1024]{1,0:T(8,128)}, u32[]{:S(2)}, u32[]{:S(2)}) collective-permute-start(f32[8,1024]{1,0:T(8,128)} %get-tuple-element.50), channel_id=1, source_target_pairs={{4,8},{8,4},{12,16},{16,12},{20,24},{24,20},{5,9},{9,5},{13,17},{1... | collective-permute-start | bytes 98312 | tf_op jit(solution)/shard_map/ppermute | solution.py:25
  31.9 1.0 %collective-permute-start.6 = (f32[8,1024]{1,0:T(8,128)}, f32[8,1024]{1,0:T(8,128)}, u32[]{:S(2)}, u32[]{:S(2)}) collective-permute-start(f32[8,1024]{1,0:T(8,128)} %get-tuple-element.51), channel_id=1, source_target_pairs={{0,1},{1,0},{2,3},{3,2},{4,5},{5,4},{6,7},{7,6},{8,9},{9,8},{10,11... | collective-permute-start | bytes 98312 | tf_op jit(solution)/shard_map/ppermute | solution.py:25
  32.9 3.0 %collective-permute-start.7 = (f32[8,1024]{1,0:T(8,128)}, f32[8,1024]{1,0:T(8,128)}, u32[]{:S(2)}, u32[]{:S(2)}) collective-permute-start(f32[8,1024]{1,0:T(8,128)} %get-tuple-element.52), channel_id=1, source_target_pairs={{1,2},{2,1},{5,6},{6,5},{9,10},{10,9},{13,14},{14,13},{17,18},{18,... | collective-permute-start | bytes 98312 | tf_op jit(solution)/shard_map/ppermute | solution.py:25
  35.9 4.2 %all-to-all-start.1 = ((f32[32,1,128]{2,1,0:T(1,128)}), f32[32,1,128]{2,1,0:T(1,128)}, u32[]{:S(2)}, u32[]{:S(2)}) async-start(f32[32,1,128]{2,1,0:T(1,128)} %bitcast.7), calls=%async_computation.1 | async-start | bytes 32768 | tf_op jit(solution)/shard_map/all_to_all | solution.py:29
  40.1 6.5 %inner_second.1 = (f32[8,20480]{1,0:T(8,128)S(1)}, f32[8,16384]{1,0:T(8,128)S(1)}) custom-call(f32[8,16384]{1,0:T(8,128)S(1)} %get-tuple-element.53.refs_0_.refs_16_, s32[2,20480]{1,0:T(2,128)} %index_ref.1, s32[1,24576]{1,0:T(1,128)} %bitcast.21, f32[64,24576]{1,0:T(8,128)} %bitcast.16, s32[8,24576]{1,0:T(8,128)} %refs_20_.3, f32[8,24576]{1,0:T(8,128)} %refs_21_.1, ...), custom_call_target="tpu_custom_call" | custom-call | flops 100000000 | bytes 10000000 | tf_op jit(solution)/shard_map/inner_second/pallas_call | solution.py:769
  46.7 0.0 all-to-all-done.1
  46.7 0.0 collective-permute-done.4.refs_10_
  46.7 0.0 collective-permute-done.5.refs_11_
  46.7 0.0 collective-permute-done.6.refs_12_
  46.7 0.0 collective-permute-done.7.refs_13_
  46.7 3.8 %outer_second.1 = (f32[8,16384]{1,0:T(8,128)S(1)}, f32[4,16384]{1,0:T(4,128)}, f32[4,1024]{1,0:T(4,128)S(1)}, f32[4,1024]{1,0:T(4,128)S(1)}, f32[4,1024]{1,0:T(4...) custom-call(s32[32]{0:T(128)} %refs_0_.5, s32[32]{0:T(128)} %refs_1_.7, ...), custom_call_target="tpu_custom_call" | custom-call | flops 10000000 | bytes 5000000 | tf_op jit(solution)/shard_map/outer_second/pallas_call | solution.py:780
  50.6 0.2 collective-permute-start.8
  50.8 4.1 %collective-permute-start.9 = (f32[4,1024]{1,0:T(4,128)S(1)}, f32[4,1024]{1,0:T(4,128)S(1)}, u32[]{:S(2)}, u32[]{:S(2)}) collective-permute-start(f32[4,1024]{1,0:T(4,128)S(1)} %get-tuple-element.64), channel_id=1, source_target_pairs={{4,8},{8,4},{12,16},{16,12},{20,24},{24,20},{5,9},{9,5},{13,17},{1... | collective-permute-start | bytes 49160 | tf_op jit(solution)/shard_map/ppermute | solution.py:25
  54.8 1.0 %collective-permute-start.10 = (f32[4,1024]{1,0:T(4,128)S(1)}, f32[4,1024]{1,0:T(4,128)S(1)}, u32[]{:S(2)}, u32[]{:S(2)}) collective-permute-start(f32[4,1024]{1,0:T(4,128)S(1)} %get-tuple-element.65), channel_id=1, source_target_pairs={{0,1},{1,0},{2,3},{3,2},{4,5},{5,4},{6,7},{7,6},{8,9},{9,8},{10,11... | collective-permute-start | bytes 49160 | tf_op jit(solution)/shard_map/ppermute | solution.py:25
  55.8 3.0 %collective-permute-start.11 = (f32[4,1024]{1,0:T(4,128)S(1)}, f32[4,1024]{1,0:T(4,128)S(1)}, u32[]{:S(2)}, u32[]{:S(2)}) collective-permute-start(f32[4,1024]{1,0:T(4,128)S(1)} %get-tuple-element.66), channel_id=1, source_target_pairs={{1,2},{2,1},{5,6},{6,5},{9,10},{10,9},{13,14},{14,13},{17,18},{18,... | collective-permute-start | bytes 49160 | tf_op jit(solution)/shard_map/ppermute | solution.py:25
  58.8 2.8 %inner_duals.1.dual_in_ref = f32[8,24576]{1,0:T(8,128)} custom-call(f32[8,16384]{1,0:T(8,128)S(1)} %get-tuple-element.61.s_ref, s32[2,20480]{1,0:T(2,128)} %index_ref.1, f32[8,20480]{1,0:T(8,128)S(1)} %get-tuple-element.62.y_ref, s32[1,24576]{1,0:T(1,128)} %bitcast.23), custom_call_target="tpu_custom_call" | custom-call | flops 10000000 | bytes 3000000 | tf_op jit(solution)/shard_map/inner_duals/pallas_call | solution.py:804
  61.7 0.0 collective-permute-done.8.xe
  61.7 0.0 collective-permute-done.9.xo
  61.7 0.0 collective-permute-done.10.ye
  61.7 0.0 collective-permute-done.11.yo
  61.7 1.7 %outer_duals.1 = f32[8,24576]{1,0:T(8,128)} custom-call(f32[8,24576]{1,0:T(8,128)} %inner_duals.1.dual_in_ref, f32[4,1024]{1,0:T(4,128)S(1)} %collective-permute-done.8.xe, f32[4,1024]{1,0:T(4,128)S(1)} %collective-permute-done.9.xo, f32[4,1024]{1,0:T(4,128)S(1)} %collective-permute-done.10.ye, ...), custom_call_target="tpu_custom_call", output_to_operand_aliasing={{}: (0, {})} | custom-call | flops 1000000 | bytes 1000000 | tf_op jit(solution)/shard_map/outer_duals/pallas_call | solution.py:813
Async XLA Ops:
  3.6 19.5 %collective-permute-start = (f32[25,1024]{1,0:T(8,128)S(1)}, f32[25,1024]{1,0:T(8,128)S(1)}, u32[]{:S(2)}, u32[]{:S(2)}) collective-permute-start(f32[25,1024]{1,0:T(8,128)S(1)} %get-tuple-element.39), channel_id=1, source_target_pairs={{0,4},{4,0},{8,12},{12,8},{16,20},{20,16},{24,28},{28,24},{1,5},{5... | collective-permute-start | bytes 307208 | tf_op jit(solution)/shard_map/ppermute | solution.py:25
  3.7 19.5 %collective-permute-start.1 = (f32[25,1024]{1,0:T(8,128)S(1)}, f32[25,1024]{1,0:T(8,128)S(1)}, u32[]{:S(2)}, u32[]{:S(2)}) collective-permute-start(f32[25,1024]{1,0:T(8,128)S(1)} %get-tuple-element.40), channel_id=1, source_target_pairs={{4,8},{8,4},{12,16},{16,12},{20,24},{24,20},{5,9},{9,5},{13,17},{1... | collective-permute-start | bytes 307208 | tf_op jit(solution)/shard_map/ppermute | solution.py:25
  8.0 15.1 %collective-permute-start.2 = (f32[25,1024]{1,0:T(8,128)S(1)}, f32[25,1024]{1,0:T(8,128)S(1)}, u32[]{:S(2)}, u32[]{:S(2)}) collective-permute-start(f32[25,1024]{1,0:T(8,128)S(1)} %get-tuple-element.41), channel_id=1, source_target_pairs={{0,1},{1,0},{2,3},{3,2},{4,5},{5,4},{6,7},{7,6},{8,9},{9,8},{10,11... | collective-permute-start | bytes 307208 | tf_op jit(solution)/shard_map/ppermute | solution.py:25
  9.3 13.8 %collective-permute-start.3 = (f32[25,1024]{1,0:T(8,128)S(1)}, f32[25,1024]{1,0:T(8,128)S(1)}, u32[]{:S(2)}, u32[]{:S(2)}) collective-permute-start(f32[25,1024]{1,0:T(8,128)S(1)} %get-tuple-element.42), channel_id=1, source_target_pairs={{1,2},{2,1},{5,6},{6,5},{9,10},{10,9},{13,14},{14,13},{17,18},{18,... | collective-permute-start | bytes 307208 | tf_op jit(solution)/shard_map/ppermute | solution.py:25
  12.4 10.7 %all-to-all-start = ((f32[32,1,128]{2,1,0:T(1,128)}), f32[32,1,128]{2,1,0:T(1,128)S(1)}, u32[]{:S(2)}, u32[]{:S(2)}) async-start(f32[32,1,128]{2,1,0:T(1,128)} %bitcast.4), calls=%async_computation | async-start | bytes 32768 | tf_op jit(solution)/shard_map/all_to_all | solution.py:29
  27.6 19.1 %collective-permute-start.4 = (f32[8,1024]{1,0:T(8,128)}, f32[8,1024]{1,0:T(8,128)}, u32[]{:S(2)}, u32[]{:S(2)}) collective-permute-start(f32[8,1024]{1,0:T(8,128)} %get-tuple-element.49), channel_id=1, source_target_pairs={{0,4},{4,0},{8,12},{12,8},{16,20},{20,16},{24,28},{28,24},{1,5},{5... | collective-permute-start | bytes 98312 | tf_op jit(solution)/shard_map/ppermute | solution.py:25
  28.0 18.8 %collective-permute-start.5 = (f32[8,1024]{1,0:T(8,128)}, f32[8,1024]{1,0:T(8,128)}, u32[]{:S(2)}, u32[]{:S(2)}) collective-permute-start(f32[8,1024]{1,0:T(8,128)} %get-tuple-element.50), channel_id=1, source_target_pairs={{4,8},{8,4},{12,16},{16,12},{20,24},{24,20},{5,9},{9,5},{13,17},{1... | collective-permute-start | bytes 98312 | tf_op jit(solution)/shard_map/ppermute | solution.py:25
  31.9 14.8 %collective-permute-start.6 = (f32[8,1024]{1,0:T(8,128)}, f32[8,1024]{1,0:T(8,128)}, u32[]{:S(2)}, u32[]{:S(2)}) collective-permute-start(f32[8,1024]{1,0:T(8,128)} %get-tuple-element.51), channel_id=1, source_target_pairs={{0,1},{1,0},{2,3},{3,2},{4,5},{5,4},{6,7},{7,6},{8,9},{9,8},{10,11... | collective-permute-start | bytes 98312 | tf_op jit(solution)/shard_map/ppermute | solution.py:25
  32.9 13.8 %collective-permute-start.7 = (f32[8,1024]{1,0:T(8,128)}, f32[8,1024]{1,0:T(8,128)}, u32[]{:S(2)}, u32[]{:S(2)}) collective-permute-start(f32[8,1024]{1,0:T(8,128)} %get-tuple-element.52), channel_id=1, source_target_pairs={{1,2},{2,1},{5,6},{6,5},{9,10},{10,9},{13,14},{14,13},{17,18},{18,... | collective-permute-start | bytes 98312 | tf_op jit(solution)/shard_map/ppermute | solution.py:25
  35.9 10.8 %all-to-all-start.1 = ((f32[32,1,128]{2,1,0:T(1,128)}), f32[32,1,128]{2,1,0:T(1,128)}, u32[]{:S(2)}, u32[]{:S(2)}) async-start(f32[32,1,128]{2,1,0:T(1,128)} %bitcast.7), calls=%async_computation.1 | async-start | bytes 32768 | tf_op jit(solution)/shard_map/all_to_all | solution.py:29
  50.6 11.1 %collective-permute-start.8 = (f32[4,1024]{1,0:T(4,128)S(1)}, f32[4,1024]{1,0:T(4,128)S(1)}, u32[]{:S(2)}, u32[]{:S(2)}) collective-permute-start(f32[4,1024]{1,0:T(4,128)S(1)} %get-tuple-element.63), channel_id=1, source_target_pairs={{0,4},{4,0},{8,12},{12,8},{16,20},{20,16},{24,28},{28,24},{1,5},{5... | collective-permute-start | bytes 49160 | tf_op jit(solution)/shard_map/ppermute | solution.py:25
  50.8 10.9 %collective-permute-start.9 = (f32[4,1024]{1,0:T(4,128)S(1)}, f32[4,1024]{1,0:T(4,128)S(1)}, u32[]{:S(2)}, u32[]{:S(2)}) collective-permute-start(f32[4,1024]{1,0:T(4,128)S(1)} %get-tuple-element.64), channel_id=1, source_target_pairs={{4,8},{8,4},{12,16},{16,12},{20,24},{24,20},{5,9},{9,5},{13,17},{1... | collective-permute-start | bytes 49160 | tf_op jit(solution)/shard_map/ppermute | solution.py:25
  54.8 6.8 %collective-permute-start.10 = (f32[4,1024]{1,0:T(4,128)S(1)}, f32[4,1024]{1,0:T(4,128)S(1)}, u32[]{:S(2)}, u32[]{:S(2)}) collective-permute-start(f32[4,1024]{1,0:T(4,128)S(1)} %get-tuple-element.65), channel_id=1, source_target_pairs={{0,1},{1,0},{2,3},{3,2},{4,5},{5,4},{6,7},{7,6},{8,9},{9,8},{10,11... | collective-permute-start | bytes 49160 | tf_op jit(solution)/shard_map/ppermute | solution.py:25
  55.8 5.8 %collective-permute-start.11 = (f32[4,1024]{1,0:T(4,128)S(1)}, f32[4,1024]{1,0:T(4,128)S(1)}, u32[]{:S(2)}, u32[]{:S(2)}) collective-permute-start(f32[4,1024]{1,0:T(4,128)S(1)} %get-tuple-element.66), channel_id=1, source_target_pairs={{1,2},{2,1},{5,6},{6,5},{9,10},{10,9},{13,14},{14,13},{17,18},{18,... | collective-permute-start | bytes 49160 | tf_op jit(solution)/shard_map/ppermute | solution.py:25

commit v6 on v5

--- a/solution.py
+++ b/solution.py
@@ -366,7 +366,7 @@
     groups = s_ref.shape[1] // (GROUP * BLK)
     buses, cross = (GROUP * BLK, from_ref.shape[1] // groups)
 
-    @pl.loop(0, groups, unroll=4)
+    @pl.loop(0, groups, unroll=8)
     def _(g):
         base = g * buses
         tables = [doubled(s_ref[:, lanes(base + h * LANES)]) for h in range(buses // LANES)]
@@ -598,7 +598,7 @@
     branches = index_ref.shape[1] // groups
     per_pair = branches // (GROUP // 2)
 
-    @pl.loop(0, groups, unroll=4)
+    @pl.loop(0, groups, unroll=8)
     def _(g):
         for p in range(GROUP // 2):
             base = g * GROUP * BLK + p * PAIR

time: 63.9 us -> 63.1 us (0.987)
  Pallas kernels: 28.9 us -> 28 us
    pallas_call x1, Pallas kernels: 3.02 us -> 2.22 us  [on_device(): pl.pallas_call(start_kernel, name='first_messages', in_specs=[scalars(),...]
where the time goes in v6:
time: 63.1 us; the launch traced here: 62.6 us
  starting transfers between devices  33.8 us (54%)
  Pallas kernels  28 us (44%)
  between operations  0.82 us (1%)
    ppermute x12, starting transfers between devices, swapped(): return lax.ppermute(value, axis, moves)  25.3 us
    all_to_all x2, starting transfers between devices, to_all(): lax.all_to_all(rows, ('gx', 'gy'), split_axis=0, concat_axis=0, tiled=True)  8.46 us
    pallas_call x1, Pallas kernels, on_device(): pl.pallas_call(fetching(functools.partial(inner_kernel, False), {0: 0, 1:...  6.55 us
    pallas_call x1, Pallas kernels, on_device(): pl.pallas_call(fetching(functools.partial(inner_kernel, True), {0: 0, 1:...  6.44 us
    pallas_call x1, Pallas kernels, on_device(): pl.pallas_call(functools.partial(outer_kernel, True), name='outer_first',...  4.48 us
    pallas_call x1, Pallas kernels, on_device(): pl.pallas_call(functools.partial(outer_kernel, False), name='outer_second...  3.83 us
    pallas_call x1, Pallas kernels, on_device(): pl.pallas_call(inner_dual_kernel, name='inner_duals', in_specs=[state_spe...  2.75 us
    pallas_call x1, Pallas kernels, on_device(): pl.pallas_call(start_kernel, name='first_messages', in_specs=[scalars(),...  2.22 us
  transfers between devices with their start and end apart: 14, of which 0 were waited for; matrix products, arithmetic and copies ran while one was open for 0% of the time, Pallas kernels for 25%

profile of v6, /device:TPU:5, one launch (start us, length us, event | category | flops | bytes accessed | tf_op | source)
XLA Modules:
  0.0 62.6 jit_solution(16667165611027673118)
XLA Ops:
  0.6 2.2 %first_messages.1 = (f32[25,1024]{1,0:T(8,128)S(1)}, f32[25,1024]{1,0:T(8,128)S(1)}, f32[25,1024]{1,0:T(8,128)S(1)}, f32[25,1024]{1,0:T(8,128)S(1)}, f32[16,1024...) custom-call(s32[32]{0:T(128)} %refs_0_.5, s32[32]{0:T(128)} %level_ref.1, ...), custom_call_target="tpu_custom_call" | custom-call | flops 1000000 | bytes 4000000 | tf_op jit(solution)/shard_map/first_messages/pallas_call | solution.py:694
  2.9 0.1 collective-permute-start
  2.9 4.4 %collective-permute-start.1 = (f32[25,1024]{1,0:T(8,128)S(1)}, f32[25,1024]{1,0:T(8,128)S(1)}, u32[]{:S(2)}, u32[]{:S(2)}) collective-permute-start(f32[25,1024]{1,0:T(8,128)S(1)} %get-tuple-element.40), channel_id=1, source_target_pairs={{4,8},{8,4},{12,16},{16,12},{20,24},{24,20},{5,9},{9,5},{13,17},{1... | collective-permute-start | bytes 307208 | tf_op jit(solution)/shard_map/ppermute | solution.py:25
  7.3 1.3 %collective-permute-start.2 = (f32[25,1024]{1,0:T(8,128)S(1)}, f32[25,1024]{1,0:T(8,128)S(1)}, u32[]{:S(2)}, u32[]{:S(2)}) collective-permute-start(f32[25,1024]{1,0:T(8,128)S(1)} %get-tuple-element.41), channel_id=1, source_target_pairs={{0,1},{1,0},{2,3},{3,2},{4,5},{5,4},{6,7},{7,6},{8,9},{9,8},{10,11... | collective-permute-start | bytes 307208 | tf_op jit(solution)/shard_map/ppermute | solution.py:25
  8.6 3.0 %collective-permute-start.3 = (f32[25,1024]{1,0:T(8,128)S(1)}, f32[25,1024]{1,0:T(8,128)S(1)}, u32[]{:S(2)}, u32[]{:S(2)}) collective-permute-start(f32[25,1024]{1,0:T(8,128)S(1)} %get-tuple-element.42), channel_id=1, source_target_pairs={{1,2},{2,1},{5,6},{6,5},{9,10},{10,9},{13,14},{14,13},{17,18},{18,... | collective-permute-start | bytes 307208 | tf_op jit(solution)/shard_map/ppermute | solution.py:25
  11.6 4.3 %all-to-all-start = ((f32[32,1,128]{2,1,0:T(1,128)}), f32[32,1,128]{2,1,0:T(1,128)S(1)}, u32[]{:S(2)}, u32[]{:S(2)}) async-start(f32[32,1,128]{2,1,0:T(1,128)} %bitcast.4), calls=%async_computation | async-start | bytes 32768 | tf_op jit(solution)/shard_map/all_to_all | solution.py:29
  15.9 6.4 %inner_first.1 = (f32[8,20480]{1,0:T(8,128)S(1)}, f32[8,16384]{1,0:T(8,128)S(1)}, f32[1,16384]{1,0:T(1,128)S(1)}) custom-call(f32[4,16384]{1,0:T(4,128)} %refs_11_.1, s32[2,20480]{1,0:T(2,128)} %index_ref.1, s32[1,24576]{1,0:T(1,128)} %bitcast.19, f32[64,24576]{1,0:T(8,128)} %bitcast.14, s32[8,24576]{1,0:T(8,128)} %refs_20_.3, f32[8,24576]{1,0:T(8,128)} %refs_21_.1), custom_call_target="tpu_custom_call" | custom-call | flops 100000000 | bytes 10000000 | tf_op jit(solution)/shard_map/inner_first/pallas_call | solution.py:729
  22.3 0.0 all-to-all-done
  22.4 0.0 collective-permute-done.refs_5_.refs_6_
  22.4 0.0 collective-permute-done.1.refs_6_.refs_7_
  22.4 0.0 collective-permute-done.2.refs_7_.refs_8_
  22.4 0.0 collective-permute-done.3.refs_8_.refs_9_
  22.4 4.5 %outer_first.1 = (f32[8,16384]{1,0:T(8,128)S(1)}, f32[8,16384]{1,0:T(8,128)S(1)}, f32[8,1024]{1,0:T(8,128)}, f32[8,1024]{1,0:T(8,128)}, f32[8,1024]{1,0:T(8,128)...) custom-call(s32[32]{0:T(128)} %refs_0_.5, ...), custom_call_target="tpu_custom_call" | custom-call | flops 10000000 | bytes 5000000 | tf_op jit(solution)/shard_map/outer_first/pallas_call | solution.py:740
  26.9 0.4 collective-permute-start.4
  27.2 4.0 %collective-permute-start.5 = (f32[8,1024]{1,0:T(8,128)}, f32[8,1024]{1,0:T(8,128)}, u32[]{:S(2)}, u32[]{:S(2)}) collective-permute-start(f32[8,1024]{1,0:T(8,128)} %get-tuple-element.50), channel_id=1, source_target_pairs={{4,8},{8,4},{12,16},{16,12},{20,24},{24,20},{5,9},{9,5},{13,17},{1... | collective-permute-start | bytes 98312 | tf_op jit(solution)/shard_map/ppermute | solution.py:25
  31.2 1.0 %collective-permute-start.6 = (f32[8,1024]{1,0:T(8,128)}, f32[8,1024]{1,0:T(8,128)}, u32[]{:S(2)}, u32[]{:S(2)}) collective-permute-start(f32[8,1024]{1,0:T(8,128)} %get-tuple-element.51), channel_id=1, source_target_pairs={{0,1},{1,0},{2,3},{3,2},{4,5},{5,4},{6,7},{7,6},{8,9},{9,8},{10,11... | collective-permute-start | bytes 98312 | tf_op jit(solution)/shard_map/ppermute | solution.py:25
  32.2 3.0 %collective-permute-start.7 = (f32[8,1024]{1,0:T(8,128)}, f32[8,1024]{1,0:T(8,128)}, u32[]{:S(2)}, u32[]{:S(2)}) collective-permute-start(f32[8,1024]{1,0:T(8,128)} %get-tuple-element.52), channel_id=1, source_target_pairs={{1,2},{2,1},{5,6},{6,5},{9,10},{10,9},{13,14},{14,13},{17,18},{18,... | collective-permute-start | bytes 98312 | tf_op jit(solution)/shard_map/ppermute | solution.py:25
  35.2 4.2 %all-to-all-start.1 = ((f32[32,1,128]{2,1,0:T(1,128)}), f32[32,1,128]{2,1,0:T(1,128)}, u32[]{:S(2)}, u32[]{:S(2)}) async-start(f32[32,1,128]{2,1,0:T(1,128)} %bitcast.7), calls=%async_computation.1 | async-start | bytes 32768 | tf_op jit(solution)/shard_map/all_to_all | solution.py:29
  39.4 6.5 %inner_second.1 = (f32[8,20480]{1,0:T(8,128)S(1)}, f32[8,16384]{1,0:T(8,128)S(1)}) custom-call(f32[8,16384]{1,0:T(8,128)S(1)} %get-tuple-element.53.refs_0_.refs_16_, s32[2,20480]{1,0:T(2,128)} %index_ref.1, s32[1,24576]{1,0:T(1,128)} %bitcast.21, f32[64,24576]{1,0:T(8,128)} %bitcast.16, s32[8,24576]{1,0:T(8,128)} %refs_20_.3, f32[8,24576]{1,0:T(8,128)} %refs_21_.1, ...), custom_call_target="tpu_custom_call" | custom-call | flops 100000000 | bytes 10000000 | tf_op jit(solution)/shard_map/inner_second/pallas_call | solution.py:769
  46.0 0.0 all-to-all-done.1
  46.0 0.0 collective-permute-done.4.refs_10_
  46.0 0.0 collective-permute-done.5.refs_11_
  46.0 0.0 collective-permute-done.6.refs_12_
  46.0 0.0 collective-permute-done.7.refs_13_
  46.0 3.8 %outer_second.1 = (f32[8,16384]{1,0:T(8,128)S(1)}, f32[4,16384]{1,0:T(4,128)}, f32[4,1024]{1,0:T(4,128)S(1)}, f32[4,1024]{1,0:T(4,128)S(1)}, f32[4,1024]{1,0:T(4...) custom-call(s32[32]{0:T(128)} %refs_0_.5, s32[32]{0:T(128)} %refs_1_.7, ...), custom_call_target="tpu_custom_call" | custom-call | flops 10000000 | bytes 5000000 | tf_op jit(solution)/shard_map/outer_second/pallas_call | solution.py:780
  49.8 0.2 collective-permute-start.8
  50.0 4.1 %collective-permute-start.9 = (f32[4,1024]{1,0:T(4,128)S(1)}, f32[4,1024]{1,0:T(4,128)S(1)}, u32[]{:S(2)}, u32[]{:S(2)}) collective-permute-start(f32[4,1024]{1,0:T(4,128)S(1)} %get-tuple-element.64), channel_id=1, source_target_pairs={{4,8},{8,4},{12,16},{16,12},{20,24},{24,20},{5,9},{9,5},{13,17},{1... | collective-permute-start | bytes 49160 | tf_op jit(solution)/shard_map/ppermute | solution.py:25
  54.1 1.0 %collective-permute-start.10 = (f32[4,1024]{1,0:T(4,128)S(1)}, f32[4,1024]{1,0:T(4,128)S(1)}, u32[]{:S(2)}, u32[]{:S(2)}) collective-permute-start(f32[4,1024]{1,0:T(4,128)S(1)} %get-tuple-element.65), channel_id=1, source_target_pairs={{0,1},{1,0},{2,3},{3,2},{4,5},{5,4},{6,7},{7,6},{8,9},{9,8},{10,11... | collective-permute-start | bytes 49160 | tf_op jit(solution)/shard_map/ppermute | solution.py:25
  55.1 3.0 %collective-permute-start.11 = (f32[4,1024]{1,0:T(4,128)S(1)}, f32[4,1024]{1,0:T(4,128)S(1)}, u32[]{:S(2)}, u32[]{:S(2)}) collective-permute-start(f32[4,1024]{1,0:T(4,128)S(1)} %get-tuple-element.66), channel_id=1, source_target_pairs={{1,2},{2,1},{5,6},{6,5},{9,10},{10,9},{13,14},{14,13},{17,18},{18,... | collective-permute-start | bytes 49160 | tf_op jit(solution)/shard_map/ppermute | solution.py:25
  58.1 2.8 %inner_duals.1.dual_in_ref = f32[8,24576]{1,0:T(8,128)} custom-call(f32[8,16384]{1,0:T(8,128)S(1)} %get-tuple-element.61.s_ref, s32[2,20480]{1,0:T(2,128)} %index_ref.1, f32[8,20480]{1,0:T(8,128)S(1)} %get-tuple-element.62.y_ref, s32[1,24576]{1,0:T(1,128)} %bitcast.23), custom_call_target="tpu_custom_call" | custom-call | flops 10000000 | bytes 3000000 | tf_op jit(solution)/shard_map/inner_duals/pallas_call | solution.py:804
  60.9 0.0 collective-permute-done.8.xe
  60.9 0.0 collective-permute-done.9.xo
  60.9 0.0 collective-permute-done.10.ye
  60.9 0.0 collective-permute-done.11.yo
  60.9 1.7 %outer_duals.1 = f32[8,24576]{1,0:T(8,128)} custom-call(f32[8,24576]{1,0:T(8,128)} %inner_duals.1.dual_in_ref, f32[4,1024]{1,0:T(4,128)S(1)} %collective-permute-done.8.xe, f32[4,1024]{1,0:T(4,128)S(1)} %collective-permute-done.9.xo, f32[4,1024]{1,0:T(4,128)S(1)} %collective-permute-done.10.ye, ...), custom_call_target="tpu_custom_call", output_to_operand_aliasing={{}: (0, {})} | custom-call | flops 1000000 | bytes 1000000 | tf_op jit(solution)/shard_map/outer_duals/pallas_call | solution.py:813
Async XLA Ops:
  2.9 19.5 %collective-permute-start = (f32[25,1024]{1,0:T(8,128)S(1)}, f32[25,1024]{1,0:T(8,128)S(1)}, u32[]{:S(2)}, u32[]{:S(2)}) collective-permute-start(f32[25,1024]{1,0:T(8,128)S(1)} %get-tuple-element.39), channel_id=1, source_target_pairs={{0,4},{4,0},{8,12},{12,8},{16,20},{20,16},{24,28},{28,24},{1,5},{5... | collective-permute-start | bytes 307208 | tf_op jit(solution)/shard_map/ppermute | solution.py:25
  2.9 19.4 %collective-permute-start.1 = (f32[25,1024]{1,0:T(8,128)S(1)}, f32[25,1024]{1,0:T(8,128)S(1)}, u32[]{:S(2)}, u32[]{:S(2)}) collective-permute-start(f32[25,1024]{1,0:T(8,128)S(1)} %get-tuple-element.40), channel_id=1, source_target_pairs={{4,8},{8,4},{12,16},{16,12},{20,24},{24,20},{5,9},{9,5},{13,17},{1... | collective-permute-start | bytes 307208 | tf_op jit(solution)/shard_map/ppermute | solution.py:25
  7.3 15.1 %collective-permute-start.2 = (f32[25,1024]{1,0:T(8,128)S(1)}, f32[25,1024]{1,0:T(8,128)S(1)}, u32[]{:S(2)}, u32[]{:S(2)}) collective-permute-start(f32[25,1024]{1,0:T(8,128)S(1)} %get-tuple-element.41), channel_id=1, source_target_pairs={{0,1},{1,0},{2,3},{3,2},{4,5},{5,4},{6,7},{7,6},{8,9},{9,8},{10,11... | collective-permute-start | bytes 307208 | tf_op jit(solution)/shard_map/ppermute | solution.py:25
  8.6 13.8 %collective-permute-start.3 = (f32[25,1024]{1,0:T(8,128)S(1)}, f32[25,1024]{1,0:T(8,128)S(1)}, u32[]{:S(2)}, u32[]{:S(2)}) collective-permute-start(f32[25,1024]{1,0:T(8,128)S(1)} %get-tuple-element.42), channel_id=1, source_target_pairs={{1,2},{2,1},{5,6},{6,5},{9,10},{10,9},{13,14},{14,13},{17,18},{18,... | collective-permute-start | bytes 307208 | tf_op jit(solution)/shard_map/ppermute | solution.py:25
  11.6 10.7 %all-to-all-start = ((f32[32,1,128]{2,1,0:T(1,128)}), f32[32,1,128]{2,1,0:T(1,128)S(1)}, u32[]{:S(2)}, u32[]{:S(2)}) async-start(f32[32,1,128]{2,1,0:T(1,128)} %bitcast.4), calls=%async_computation | async-start | bytes 32768 | tf_op jit(solution)/shard_map/all_to_all | solution.py:29
  26.9 19.1 %collective-permute-start.4 = (f32[8,1024]{1,0:T(8,128)}, f32[8,1024]{1,0:T(8,128)}, u32[]{:S(2)}, u32[]{:S(2)}) collective-permute-start(f32[8,1024]{1,0:T(8,128)} %get-tuple-element.49), channel_id=1, source_target_pairs={{0,4},{4,0},{8,12},{12,8},{16,20},{20,16},{24,28},{28,24},{1,5},{5... | collective-permute-start | bytes 98312 | tf_op jit(solution)/shard_map/ppermute | solution.py:25
  27.2 18.8 %collective-permute-start.5 = (f32[8,1024]{1,0:T(8,128)}, f32[8,1024]{1,0:T(8,128)}, u32[]{:S(2)}, u32[]{:S(2)}) collective-permute-start(f32[8,1024]{1,0:T(8,128)} %get-tuple-element.50), channel_id=1, source_target_pairs={{4,8},{8,4},{12,16},{16,12},{20,24},{24,20},{5,9},{9,5},{13,17},{1... | collective-permute-start | bytes 98312 | tf_op jit(solution)/shard_map/ppermute | solution.py:25
  31.2 14.8 %collective-permute-start.6 = (f32[8,1024]{1,0:T(8,128)}, f32[8,1024]{1,0:T(8,128)}, u32[]{:S(2)}, u32[]{:S(2)}) collective-permute-start(f32[8,1024]{1,0:T(8,128)} %get-tuple-element.51), channel_id=1, source_target_pairs={{0,1},{1,0},{2,3},{3,2},{4,5},{5,4},{6,7},{7,6},{8,9},{9,8},{10,11... | collective-permute-start | bytes 98312 | tf_op jit(solution)/shard_map/ppermute | solution.py:25
  32.2 13.8 %collective-permute-start.7 = (f32[8,1024]{1,0:T(8,128)}, f32[8,1024]{1,0:T(8,128)}, u32[]{:S(2)}, u32[]{:S(2)}) collective-permute-start(f32[8,1024]{1,0:T(8,128)} %get-tuple-element.52), channel_id=1, source_target_pairs={{1,2},{2,1},{5,6},{6,5},{9,10},{10,9},{13,14},{14,13},{17,18},{18,... | collective-permute-start | bytes 98312 | tf_op jit(solution)/shard_map/ppermute | solution.py:25
  35.2 10.8 %all-to-all-start.1 = ((f32[32,1,128]{2,1,0:T(1,128)}), f32[32,1,128]{2,1,0:T(1,128)}, u32[]{:S(2)}, u32[]{:S(2)}) async-start(f32[32,1,128]{2,1,0:T(1,128)} %bitcast.7), calls=%async_computation.1 | async-start | bytes 32768 | tf_op jit(solution)/shard_map/all_to_all | solution.py:29
  49.8 11.0 %collective-permute-start.8 = (f32[4,1024]{1,0:T(4,128)S(1)}, f32[4,1024]{1,0:T(4,128)S(1)}, u32[]{:S(2)}, u32[]{:S(2)}) collective-permute-start(f32[4,1024]{1,0:T(4,128)S(1)} %get-tuple-element.63), channel_id=1, source_target_pairs={{0,4},{4,0},{8,12},{12,8},{16,20},{20,16},{24,28},{28,24},{1,5},{5... | collective-permute-start | bytes 49160 | tf_op jit(solution)/shard_map/ppermute | solution.py:25
  50.0 10.8 %collective-permute-start.9 = (f32[4,1024]{1,0:T(4,128)S(1)}, f32[4,1024]{1,0:T(4,128)S(1)}, u32[]{:S(2)}, u32[]{:S(2)}) collective-permute-start(f32[4,1024]{1,0:T(4,128)S(1)} %get-tuple-element.64), channel_id=1, source_target_pairs={{4,8},{8,4},{12,16},{16,12},{20,24},{24,20},{5,9},{9,5},{13,17},{1... | collective-permute-start | bytes 49160 | tf_op jit(solution)/shard_map/ppermute | solution.py:25
  54.1 6.8 %collective-permute-start.10 = (f32[4,1024]{1,0:T(4,128)S(1)}, f32[4,1024]{1,0:T(4,128)S(1)}, u32[]{:S(2)}, u32[]{:S(2)}) collective-permute-start(f32[4,1024]{1,0:T(4,128)S(1)} %get-tuple-element.65), channel_id=1, source_target_pairs={{0,1},{1,0},{2,3},{3,2},{4,5},{5,4},{6,7},{7,6},{8,9},{9,8},{10,11... | collective-permute-start | bytes 49160 | tf_op jit(solution)/shard_map/ppermute | solution.py:25
  55.1 5.8 %collective-permute-start.11 = (f32[4,1024]{1,0:T(4,128)S(1)}, f32[4,1024]{1,0:T(4,128)S(1)}, u32[]{:S(2)}, u32[]{:S(2)}) collective-permute-start(f32[4,1024]{1,0:T(4,128)S(1)} %get-tuple-element.66), channel_id=1, source_target_pairs={{1,2},{2,1},{5,6},{6,5},{9,10},{10,9},{13,14},{14,13},{17,18},{18,... | collective-permute-start | bytes 49160 | tf_op jit(solution)/shard_map/ppermute | solution.py:25
